TPU v7x, 512 devices: a whole 4x8x8 slice. The times are simulated.
512 devices in a mesh: layer: 32 (over x, z_lo, core), lat: 16 (over z_hi, y).
Axes of the slice: x: 4, y: 8, z: 8 (z_hi: 2, z_lo: 4; z = z_hi * 4 + z_lo), core: 2. Of those that a mesh axis runs over, the one named last changes fastest.
Arguments:
- inputs: bfloat16 [4, 128, 2048], P(None, None, 'lat'), may hold values from -6 to 6
- targets: bfloat16 [512, 2048], P(('layer', 'lat')), may hold values from -6 to 6
- top_index: int32 [4, 128, 64], replicated, may hold values from 0 to 8191, all different within a row
- enc_weight: bfloat16 [2048, 32768], P(None, ('layer', 'lat')), may hold values from -0.125 to 0.125
- dec_weight: bfloat16 [32768, 4, 2048], P(('layer', 'lat')), may hold values from -0.375 to 0.375
Outputs:
- errors: float32 [512, 2048], P(('layer', 'lat'))
- grad_enc: bfloat16 [2048, 32768], P(None, ('layer', 'lat'))
- grad_dec: bfloat16 [32768, 4, 2048], P(('layer', 'lat'))
Inputs may be any that keep to these rules, and one draw needn't show every extreme that they name: `top_index`: each row names 64 different latents.
All inputs are finite; a program needn't handle non-finite values.
Results may differ from a plain program's by a relative error of at most 0.009.
Values may be sent and summed in bfloat16 or wider, within the bound.
No kernel may reach another device: no remote copies, remote signals or barrier semaphores. Data moves between devices by JAX's collectives and lax.ppermute only.
A program may use at most 64 MiB of HBM per device.

v0:
```python
import jax
import jax.numpy as jnp
from jax import lax
from jax.sharding import PartitionSpec as P


def per_device(inputs, targets, top_index, enc_weight, dec_weight):
    n_layer = lax.axis_size("layer")
    n_lat = lax.axis_size("lat")
    layer_count = inputs.shape[0]
    tok_count = inputs.shape[1]
    lat_dev = enc_weight.shape[1]
    per_layer = n_layer // layer_count
    layer_id = lax.axis_index("layer") // per_layer
    lat_first = (lax.axis_index("layer") % per_layer * n_lat + lax.axis_index("lat")) * lat_dev
    own_part = lax.dynamic_index_in_dim(inputs, layer_id, 0, keepdims=False)
    features = lax.all_gather(own_part, "lat", axis=1, tiled=True)
    preact = jnp.dot(features, enc_weight, preferred_element_type=jnp.float32)
    chosen = lax.dynamic_index_in_dim(top_index, layer_id, 0, keepdims=False)
    lat_ids = lat_first + jnp.arange(lat_dev, dtype=jnp.int32)
    active = jnp.any(chosen[:, :, None] == lat_ids[None, None, :], axis=1).astype(jnp.float32)
    code_vals = (preact * active).astype(jnp.bfloat16)
    reach_mask = (jnp.arange(layer_count, dtype=jnp.int32) >= layer_id).astype(jnp.float32)
    width = dec_weight.shape[2]
    row_count = targets.shape[0] * lax.axis_size(("layer", "lat"))
    result = jnp.einsum("nf,ftd->tnd", code_vals, dec_weight, preferred_element_type=jnp.float32)
    result = result * reach_mask[:, None, None]
    decoded = lax.psum_scatter(
        result.reshape(row_count, width), ("layer", "lat"), scatter_dimension=0, tiled=True
    )
    errors = decoded - targets.astype(jnp.float32)
    err_b = errors.astype(jnp.bfloat16)
    all_err = lax.all_gather(err_b, ("layer", "lat"), axis=0, tiled=True)
    err_used = (
        all_err.reshape(layer_count, tok_count, width)
        * reach_mask.astype(jnp.bfloat16)[:, None, None]
    )
    code_grad = jnp.einsum("lnd,fld->nf", err_used, dec_weight, preferred_element_type=jnp.float32)
    pre_grad = (code_grad * active).astype(jnp.bfloat16)
    grad_enc = lax.dot_general(
        features, pre_grad, (((0,), (0,)), ((), ())), preferred_element_type=jnp.float32
    ).astype(jnp.bfloat16)
    grad_dec = jnp.einsum(
        "nf,lnd->fld", code_vals, err_used, preferred_element_type=jnp.float32
    ).astype(jnp.bfloat16)
    return (errors, grad_enc, grad_dec)


def solution(mesh):
    in_specs = (
        P(None, None, "lat"),
        P(("layer", "lat"), None),
        P(),
        P(None, ("layer", "lat")),
        P(("layer", "lat"), None, None),
    )
    out_specs = (
        P(("layer", "lat"), None),
        P(None, ("layer", "lat")),
        P(("layer", "lat"), None, None),
    )
    return jax.shard_map(
        per_device, mesh=mesh, in_specs=in_specs, out_specs=out_specs, check_vma=False
    )
```

profile of v0, /device:TPU:1, one launch (start us, length us, event | category | flops | bytes accessed | tf_op | source)
XLA Modules:
  0.0 1760.5 jit_solution(4051289702254165334)
XLA Ops:
  7.2 0.0 copy-start
  7.2 0.0 all-reduce.3.cloned.1.call-start
  7.3 0.8 constant_dynamic-slice_fusion
  8.1 55.8 %all-gather = bf16[1,128,2048]{2,1,0:T(8,128)(2,1)S(1)} all-gather(bf16[1,128,128]{2,1,0:T(8,128)(2,1)S(1)} %constant_dynamic-slice_fusion), channel_id=2, replica_groups=mesh['layer'=32,'lat'=16] {'lat'}, dimensions={2}, use_global_device_ids=true | all-gather | bytes 557056 | tf_op jit(solution)/shard_map/all_gather | solution.py:17
  63.9 0.0 copy-start.1
  63.9 0.8 dynamic-slice_bitcast_fusion
  64.6 0.3 compare_reduce_fusion
  65.0 1.3 fusion.15
  66.3 0.0 copy-done
  66.3 3.6 convolution_multiply_fusion
  69.9 0.0 copy-done.1
  69.9 0.0 copy-start.2
  69.9 0.0 all-reduce.3.cloned.1.call-update
  69.9 0.0 all-gather.4.cloned.1.call-start
  70.0 286.6 %all-reduce.3.cloned.1.call-done = f32[512,2048]{1,0:T(8,128)} async-done(((f32[512,2048]{1,0:T(8,128)}), f32[512,2048]{1,0:T(8,128)}) %all-reduce.3.cloned.1.call-update) | async-done | bytes 4194320
  356.6 0.0 copy-done.2
  356.6 1.5 convert_bitcast_fusion
  358.0 0.0 all-gather.4.cloned.1.call-update
  358.1 1384.1 %all-gather.4.cloned.1.call-done = bf16[512,1,2048]{2,1,0:T(2,128)(2,1)} async-done(((bf16[1,1,2048]{2,1,0:T(2,128)(2,1)}), bf16[512,1,2048]{2,1,0:T(2,128)(2,1)}) %all-gather.4.cloned.1.call-update) | async-done | bytes 2097168 | tf_op jit(solution)/shard_map/all_gather | solution.py:33
  1742.2 3.5 copy.24
  1745.7 1.6 convolution_convert_fusion
  1747.3 3.4 convolution_convert_fusion.1
  1750.7 3.0 copy.23
  (3 shorter events, 0.0 us)
Async XLA Ops:
  7.2 59.1 %copy-start = (bf16[64,4,2048]{2,1,0:T(4,128)(2,1)S(1)}, bf16[64,4,2048]{2,1,0:T(4,128)(2,1)}, u32[]{:S(2)}) copy-start(bf16[64,4,2048]{2,1,0:T(4,128)(2,1)} %param.9) | copy-start | bytes 3145732
  7.2 349.4 %all-reduce.3.cloned.1.call-start = ((), (), s32[]{:S(2)}) async-start(), calls=%async_computation.1 | async-start | bytes 8388608
  63.9 6.0 copy-start.1
  69.9 286.7 %copy-start.2 = (bf16[1,2048]{1,0:T(2,128)(2,1)S(1)}, bf16[1,2048]{1,0:T(2,128)(2,1)}, u32[]{:S(2)}) copy-start(bf16[1,2048]{1,0:T(2,128)(2,1)} %param.6) | copy-start | bytes 12292
  69.9 1672.3 %all-gather.4.cloned.1.call-start = ((), (), s32[]{:S(2)}) async-start(), calls=%async_computation | async-start | bytes 4202496 | tf_op jit(solution)/shard_map/all_gather | solution.py:33
Sparse Core Ops, SparseCore 0:
  70.0 286.4 all-reduce.2
  359.4 1382.7 all-gather.3
where the time goes:
time: 1760 us
  waiting for transfers between devices  1670 us (95%)
  blocking collectives  55.8 us (3%)
    all_gather x1, waiting for transfers between devices, per_device(): all_err = lax.all_gather(err_b, ('layer', 'lat'), axis=0, tiled=True)  1380 us
    unnamed x3, waiting for transfers between devices  287 us
    all_gather x1, blocking collectives, per_device(): features = lax.all_gather(own_part, 'lat', axis=1, tiled=True)  55.8 us
  transfers between devices with their start and end apart: 2, of which 2 were waited for; matrix products, arithmetic and copies ran while one was open for 0% of the time, Pallas kernels for 0%

commit v1 on v0

v1 whole, which is shorter than its diff:
```python
import jax
import jax.numpy as jnp
from jax import lax
from jax.sharding import Mesh
from jax.sharding import PartitionSpec as P

AXES = ("x", "zl", "core", "zh", "y")
GROUP = ("x", "core")
CHIPS = ("zl", "zh", "y")
LAT = ("zh", "y")
F32 = jnp.float32
BF16 = jnp.bfloat16


def exchange(value, axes):
    return lax.all_to_all(value, axes, 0, 0, tiled=True)


def spread(value, axes):
    count = lax.axis_size(axes)
    return exchange(jnp.broadcast_to(value[None], (count,) + value.shape), axes)


def per_device(inputs, targets, top_index, enc_weight, dec_weight):
    layers, tokens, _ = inputs.shape
    lat_dev = enc_weight.shape[1]
    width = dec_weight.shape[2]
    n_x, n_zl, n_core = lax.axis_size("x"), lax.axis_size("zl"), lax.axis_size("core")
    n_lat = lax.axis_size(LAT)
    n_group, n_chips = lax.axis_size(GROUP), lax.axis_size(CHIPS)
    cols = width // n_group
    layer_id = lax.axis_index("x")

    weights = dec_weight.reshape(lat_dev, layers, n_group, cols).transpose(2, 0, 1, 3)
    weights = exchange(weights, GROUP).reshape(n_x, n_core * lat_dev, layers, cols)
    target = exchange(targets.reshape(n_group, 1, cols), GROUP).reshape(layers * n_core, cols)

    own = lax.dynamic_index_in_dim(inputs, layer_id, 0, keepdims=False).T
    features = spread(own, LAT).reshape(width, tokens)
    preact = lax.dot_general(
        enc_weight, features, (((0,), (0,)), ((), ())), preferred_element_type=F32
    )
    chosen = lax.dynamic_index_in_dim(top_index, layer_id, 0, keepdims=False).T
    lat_first = lax.axis_index(("zl", "core", "zh", "y")) * lat_dev
    lat_ids = lat_first + jnp.arange(lat_dev, dtype=jnp.int32)
    active = jnp.any(chosen[None] == lat_ids[:, None, None], axis=1).astype(F32)
    own_codes = (preact * active).astype(BF16)
    codes = spread(own_codes, GROUP).reshape(n_x, n_core * lat_dev, tokens)

    partial = []
    for t in range(layers):
        partial.append(
            lax.dot_general(
                codes[: t + 1].reshape(-1, tokens),
                weights[: t + 1, :, t].reshape(-1, cols),
                (((0,), (0,)), ((), ())),
                preferred_element_type=F32,
            ).astype(BF16)
        )
    partial = jnp.stack(partial).reshape(layers, n_zl, n_core, n_lat, cols)
    partial = partial.transpose(1, 3, 0, 2, 4).reshape(n_chips, layers * n_core, cols)
    partial = exchange(partial, CHIPS)
    errors = jnp.sum(partial.astype(F32), axis=0) - target.astype(F32)
    err_b = spread(errors.astype(BF16), CHIPS)
    err_b = err_b.reshape(n_zl, n_lat, layers, n_core, cols).transpose(2, 0, 3, 1, 4)
    err_b = err_b.reshape(layers, tokens, cols)

    grads, dec_rows = [], []
    for s in range(layers):
        total = jnp.zeros((n_core * lat_dev, tokens), F32)
        rows = []
        for t in range(layers):
            if t < s:
                rows.append(jnp.zeros((n_core * lat_dev, cols), BF16))
                continue
            total = total + lax.dot_general(
                weights[s, :, t], err_b[t], (((1,), (1,)), ((), ())), preferred_element_type=F32
            )
            rows.append(jnp.dot(codes[s], err_b[t], preferred_element_type=F32).astype(BF16))
        grads.append(total)
        dec_rows.append(jnp.stack(rows, axis=1))
    code_grad = jnp.stack(grads).reshape(n_group, lat_dev, tokens)
    code_grad = jnp.sum(exchange(code_grad, GROUP), axis=0)
    dec_rows = jnp.stack(dec_rows).reshape(n_group, lat_dev, layers, cols)
    grad_dec = exchange(dec_rows, GROUP).transpose(1, 2, 0, 3).reshape(lat_dev, layers, width)
    errors = exchange(errors.reshape(n_group, 1, cols), GROUP).reshape(1, width)
    pre_grad = (code_grad * active).astype(BF16)
    grad_enc = lax.dot_general(
        features, pre_grad, (((1,), (1,)), ((), ())), preferred_element_type=F32
    ).astype(BF16)
    return errors, grad_enc, grad_dec


def solution(mesh):
    fine = Mesh(mesh.devices.reshape(4, 4, 2, 2, 8), AXES)
    in_specs = (
        P(None, None, LAT),
        P(AXES, None),
        P(),
        P(None, AXES),
        P(AXES, None, None),
    )
    out_specs = (P(AXES, None), P(None, AXES), P(AXES, None, None))
    return jax.shard_map(
        per_device, mesh=fine, in_specs=in_specs, out_specs=out_specs, check_vma=False
    )
```

time: 1760 us -> 162 us (0.09)
  waiting for transfers between devices: 1670 us -> 78.8 us
  starting transfers between devices: 0.08 us -> 60.5 us
  blocking collectives: 55.8 us -> 0 us
    all_gather x1 -> x0, waiting for transfers between devices: 1380 us -> none  [per_device(): all_err = lax.all_gather(err_b, ('layer', 'lat'), axis=0, tiled=True)]
    unnamed x3 -> x0, waiting for transfers between devices: 287 us -> none
    all_to_all x0 -> x9, waiting for transfers between devices: none -> 78.8 us  [exchange(): return lax.all_to_all(value, axes, 0, 0, tiled=True)]
    all_to_all x0 -> x9, starting transfers between devices: none -> 60.5 us  [exchange(): return lax.all_to_all(value, axes, 0, 0, tiled=True)]
    all_gather x1 -> x0, blocking collectives: 55.8 us -> none  [per_device(): features = lax.all_gather(own_part, 'lat', axis=1, tiled=True)]
  transfers between devices with their start and end apart: 2 -> 9, of which waited for: 2 -> 9; matrix products, arithmetic and copies ran while one was open for 0% -> 9% of each run, Pallas kernels for 0% -> 0%
where the time goes in v1:
time: 162 us; the launch traced here: 161 us
  waiting for transfers between devices  78.8 us (49%)
  starting transfers between devices  60.5 us (37%)
  local copies, waits for them, and re-layouts  13.2 us (8%)
  matrix products  5.09 us (3%)
  other arithmetic  2.17 us (1%)
    all_to_all x9, waiting for transfers between devices, exchange(): return lax.all_to_all(value, axes, 0, 0, tiled=True)  78.8 us
    all_to_all x9, starting transfers between devices, exchange(): return lax.all_to_all(value, axes, 0, 0, tiled=True)  60.5 us
    unnamed x11, local copies, waits for them, and re-layouts  3.4 us
  transfers between devices with their start and end apart: 9, of which 9 were waited for; matrix products, arithmetic and copies ran while one was open for 9% of the time, Pallas kernels for 0%

profile of v1, /device:TPU:1, one launch (start us, length us, event | category | flops | bytes accessed | tf_op | source)
XLA Modules:
  0.0 160.8 jit_solution(11581457735354265549)
XLA Ops:
  0.7 0.9 dynamic-slice_bitcast_fusion
  1.6 0.9 broadcast_in_dim.6
  2.6 16.2 %all-to-all-start = ((bf16[16,128,128]{2,1,0:T(8,128)(2,1)}), bf16[16,128,128]{2,1,0:T(8,128)(2,1)S(1)}, u32[]{:S(2)}, u32[]{:S(2)}) async-start(bf16[16,128,128]{2,1,0:T(8,128)(2,1)} %broadcast_in_dim.6), calls=%async_computation | async-start | bytes 1048576 | tf_op jit(solution)/shard_map/all_to_all | solution.py:16
  18.8 0.8 reshape.111
  19.5 1.6 copy.50
  21.1 15.7 %all-to-all-done = bf16[16,128,128]{2,1,0:T(8,128)(2,1)S(1)} async-done(((bf16[16,128,128]{2,1,0:T(8,128)(2,1)}), bf16[16,128,128]{2,1,0:T(8,128)(2,1)S(1)}, u32[]{:S(2)}, u32[]{:S(2)}) %all-to-all-start) | async-done | bytes 524320 | tf_op jit(solution)/shard_map/all_to_all | solution.py:16
  36.9 6.8 %all-to-all-start.2 = ((bf16[8,64,4,256]{3,1,2,0:T(8,128)(2,1)}), bf16[8,64,4,256]{3,1,2,0:T(8,128)(2,1)S(1)}, u32[]{:S(2)}, u32[]{:S(2)}) async-start(bf16[8,64,4,256]{3,1,2,0:T(8,128)(2,1)} %copy.50), calls=%async_computation.2 | async-start | bytes 2097152 | tf_op jit(solution)/shard_map/all_to_all | solution.py:16
  43.6 0.8 dynamic-slice_bitcast_fusion.1
  44.4 0.3 compare_reduce_fusion
  44.7 0.2 fusion.14
  45.0 13.8 %all-to-all-done.2 = bf16[8,64,4,256]{3,1,2,0:T(8,128)(2,1)S(1)} async-done(((bf16[8,64,4,256]{3,1,2,0:T(8,128)(2,1)}), bf16[8,64,4,256]{3,1,2,0:T(8,128)(2,1)S(1)}, u32[]{:S(2)}, u32[]{:S(2)}) %all-to-all-start.2) | async-done | bytes 1048608 | tf_op jit(solution)/shard_map/all_to_all | solution.py:16
  58.7 0.7 broadcast_in_dim.7
  59.4 4.1 %all-to-all-start.1 = ((bf16[8,64,128]{2,1,0:T(8,128)(2,1)}), bf16[8,64,128]{2,1,0:T(8,128)(2,1)S(1)}, u32[]{:S(2)}, u32[]{:S(2)}) async-start(bf16[8,64,128]{2,1,0:T(8,128)(2,1)} %broadcast_in_dim.7), calls=%async_computation.1 | async-start | bytes 262144 | tf_op jit(solution)/shard_map/all_to_all | solution.py:16
  63.5 0.5 broadcast.28
  64.1 0.7 reduce
  64.7 0.6 reshape.114
  65.5 3.3 %all-to-all-done.1 = bf16[8,64,128]{2,1,0:T(8,128)(2,1)S(1)} async-done(((bf16[8,64,128]{2,1,0:T(8,128)(2,1)}), bf16[8,64,128]{2,1,0:T(8,128)(2,1)S(1)}, u32[]{:S(2)}, u32[]{:S(2)}) %all-to-all-start.1) | async-done | bytes 131104 | tf_op jit(solution)/shard_map/all_to_all | solution.py:16
  68.8 4.1 %all-to-all-start.4 = ((bf16[8,2,128]{2,1,0:T(2,128)(2,1)}), bf16[8,2,128]{2,1,0:T(2,128)(2,1)S(1)}, u32[]{:S(2)}, u32[]{:S(2)}) async-start(bf16[8,2,128]{2,1,0:T(2,128)(2,1)} %reshape.114), calls=%async_computation.4 | async-start | bytes 8192 | tf_op jit(solution)/shard_map/all_to_all | solution.py:16
  72.9 0.2 convolution_convert_fusion.12
  73.1 0.2 convolution_convert_fusion.11
  73.4 0.2 convolution_convert_fusion.13
  73.6 0.2 convolution_convert_fusion.14
  73.9 0.9 copy.56
  74.7 2.7 %all-to-all-done.4 = bf16[8,2,128]{2,1,0:T(2,128)(2,1)S(1)} async-done(((bf16[8,2,128]{2,1,0:T(2,128)(2,1)}), bf16[8,2,128]{2,1,0:T(2,128)(2,1)S(1)}, u32[]{:S(2)}, u32[]{:S(2)}) %all-to-all-start.4) | async-done | bytes 4128 | tf_op jit(solution)/shard_map/all_to_all | solution.py:16
  77.4 7.5 %all-to-all-start.3 = ((bf16[64,8,256]{2,1,0:T(8,128)(2,1)}), bf16[64,8,256]{2,1,0:T(8,128)(2,1)S(1)}, u32[]{:S(2)}, u32[]{:S(2)}) async-start(bf16[64,8,256]{2,1,0:T(8,128)(2,1)} %copy.56), calls=%async_computation.3 | async-start | bytes 524288 | tf_op jit(solution)/shard_map/all_to_all | solution.py:16
  85.0 12.0 %all-to-all-done.3 = bf16[64,8,256]{2,1,0:T(8,128)(2,1)S(1)} async-done(((bf16[64,8,256]{2,1,0:T(8,128)(2,1)}), bf16[64,8,256]{2,1,0:T(8,128)(2,1)S(1)}, u32[]{:S(2)}, u32[]{:S(2)}) %all-to-all-start.3) | async-done | bytes 262176 | tf_op jit(solution)/shard_map/all_to_all | solution.py:16
  97.1 0.7 broadcast_in_dim.8
  97.9 6.4 %all-to-all-start.6 = ((bf16[64,8,256]{2,1,0:T(8,128)(2,1)}), bf16[64,8,256]{2,1,0:T(8,128)(2,1)S(1)}, u32[]{:S(2)}, u32[]{:S(2)}) async-start(bf16[64,8,256]{2,1,0:T(8,128)(2,1)} %broadcast_in_dim.8), calls=%async_computation.6 | async-start | bytes 524288 | tf_op jit(solution)/shard_map/all_to_all | solution.py:16
  104.3 0.6 copy.58
  104.9 11.5 %all-to-all-done.6 = bf16[64,8,256]{2,1,0:T(8,128)(2,1)S(1)} async-done(((bf16[64,8,256]{2,1,0:T(8,128)(2,1)}), bf16[64,8,256]{2,1,0:T(8,128)(2,1)S(1)}, u32[]{:S(2)}, u32[]{:S(2)}) %all-to-all-start.6) | async-done | bytes 262176 | tf_op jit(solution)/shard_map/all_to_all | solution.py:16
  116.5 6.5 %all-to-all-start.5 = ((f32[8,1,256]{2,1,0:T(1,128)}), f32[8,1,256]{2,1,0:T(1,128)S(1)}, u32[]{:S(2)}, u32[]{:S(2)}) async-start(f32[8,1,256]{2,1,0:T(1,128)} %copy.58), calls=%async_computation.5 | async-start | bytes 16384 | tf_op jit(solution)/shard_map/all_to_all | solution.py:16
  123.1 0.1 convolution_bitcast_fusion
  123.3 0.1 fusion.15
  123.4 0.2 fusion.8
  123.6 0.1 fusion.7
  123.7 0.1 fusion.6
  123.9 0.1 fusion.5
  124.0 0.1 fusion.16
  124.2 0.2 fusion.4
  124.4 0.1 fusion.3
  124.5 0.1 fusion.2
  124.7 0.1 fusion.1
  124.8 0.1 fusion.17
  125.0 0.2 fusion
  125.2 0.2 fusion.10
  125.3 0.2 convolution_add_fusion.2
  125.5 0.2 fusion.11
  125.7 0.2 convolution_add_fusion.5
  125.8 0.2 convolution_add_fusion.4
  126.0 0.2 fusion.12
  126.2 0.7 pad_maximum_fusion.2
  126.9 0.1 fusion.9
  127.0 0.6 all-to-all-done.5
  127.6 4.3 %all-to-all-start.7 = ((f32[8,64,128]{2,1,0:T(8,128)}), f32[8,64,128]{2,1,0:T(8,128)S(1)}, u32[]{:S(2)}, u32[]{:S(2)}) async-start(f32[8,64,128]{2,1,0:T(8,128)} %bitcast.50), calls=%async_computation.7 | async-start | bytes 524288 | tf_op jit(solution)/shard_map/all_to_all | solution.py:16
  131.9 0.2 maximum_bitcast_fusion.2
  132.1 0.1 pad_maximum_fusion
  132.3 1.0 copy.65
  133.3 5.1 %all-to-all-done.7 = f32[8,64,128]{2,1,0:T(8,128)S(1)} async-done(((f32[8,64,128]{2,1,0:T(8,128)}), f32[8,64,128]{2,1,0:T(8,128)S(1)}, u32[]{:S(2)}, u32[]{:S(2)}) %all-to-all-start.7) | async-done | bytes 262176 | tf_op jit(solution)/shard_map/all_to_all | solution.py:16
  138.4 4.5 %all-to-all-start.8 = ((bf16[8,64,4,256]{3,1,2,0:T(8,128)(2,1)}), bf16[8,64,4,256]{3,1,2,0:T(8,128)(2,1)S(1)}, u32[]{:S(2)}, u32[]{:S(2)}) async-start(bf16[8,64,4,256]{3,1,2,0:T(8,128)(2,1)} %copy.65), calls=%async_computation.8 | async-start | bytes 2097152 | tf_op jit(solution)/shard_map/all_to_all | solution.py:16
  142.9 1.0 convolution_convert_fusion
  143.9 14.1 %all-to-all-done.8 = bf16[8,64,4,256]{3,1,2,0:T(8,128)(2,1)S(1)} async-done(((bf16[8,64,4,256]{3,1,2,0:T(8,128)(2,1)}), bf16[8,64,4,256]{3,1,2,0:T(8,128)(2,1)S(1)}, u32[]{:S(2)}, u32[]{:S(2)}) %all-to-all-start.8) | async-done | bytes 1048608 | tf_op jit(solution)/shard_map/all_to_all | solution.py:16
  158.0 0.6 copy.71
  158.6 1.6 reshape.112
  160.2 0.6 copy.77
  (32 shorter events, 0.7 us)
Async XLA Ops:
  0.6 44.1 %copy-start = (bf16[2048,64]{0,1:T(8,128)(2,1)S(1)}, bf16[2048,64]{0,1:T(8,128)(2,1)}, u32[]{:S(2)}) copy-start(bf16[2048,64]{0,1:T(8,128)(2,1)} %param.8) | copy-start | bytes 786436
  0.6 18.1 %copy-start.1 = (bf16[64,4,2048]{2,1,0:T(4,128)(2,1)S(1)}, bf16[64,4,2048]{2,1,0:T(4,128)(2,1)}, u32[]{:S(2)}) copy-start(bf16[64,4,2048]{2,1,0:T(4,128)(2,1)} %param.9) | copy-start | bytes 3145732
  2.6 34.3 %all-to-all-start = ((bf16[16,128,128]{2,1,0:T(8,128)(2,1)}), bf16[16,128,128]{2,1,0:T(8,128)(2,1)S(1)}, u32[]{:S(2)}, u32[]{:S(2)}) async-start(bf16[16,128,128]{2,1,0:T(8,128)(2,1)} %broadcast_in_dim.6), calls=%async_computation | async-start | bytes 1048576 | tf_op jit(solution)/shard_map/all_to_all | solution.py:16
  36.9 21.9 %all-to-all-start.2 = ((bf16[8,64,4,256]{3,1,2,0:T(8,128)(2,1)}), bf16[8,64,4,256]{3,1,2,0:T(8,128)(2,1)S(1)}, u32[]{:S(2)}, u32[]{:S(2)}) async-start(bf16[8,64,4,256]{3,1,2,0:T(8,128)(2,1)} %copy.50), calls=%async_computation.2 | async-start | bytes 2097152 | tf_op jit(solution)/shard_map/all_to_all | solution.py:16
  43.6 20.4 %copy-start.2 = (bf16[1,2048]{1,0:T(2,128)(2,1)S(1)}, bf16[1,2048]{1,0:T(2,128)(2,1)}, u32[]{:S(2)}) copy-start(bf16[1,2048]{1,0:T(2,128)(2,1)} %param.6) | copy-start | bytes 12292
  59.4 9.4 %all-to-all-start.1 = ((bf16[8,64,128]{2,1,0:T(8,128)(2,1)}), bf16[8,64,128]{2,1,0:T(8,128)(2,1)S(1)}, u32[]{:S(2)}, u32[]{:S(2)}) async-start(bf16[8,64,128]{2,1,0:T(8,128)(2,1)} %broadcast_in_dim.7), calls=%async_computation.1 | async-start | bytes 262144 | tf_op jit(solution)/shard_map/all_to_all | solution.py:16
  68.8 8.6 %all-to-all-start.4 = ((bf16[8,2,128]{2,1,0:T(2,128)(2,1)}), bf16[8,2,128]{2,1,0:T(2,128)(2,1)S(1)}, u32[]{:S(2)}, u32[]{:S(2)}) async-start(bf16[8,2,128]{2,1,0:T(2,128)(2,1)} %reshape.114), calls=%async_computation.4 | async-start | bytes 8192 | tf_op jit(solution)/shard_map/all_to_all | solution.py:16
  77.4 19.6 %all-to-all-start.3 = ((bf16[64,8,256]{2,1,0:T(8,128)(2,1)}), bf16[64,8,256]{2,1,0:T(8,128)(2,1)S(1)}, u32[]{:S(2)}, u32[]{:S(2)}) async-start(bf16[64,8,256]{2,1,0:T(8,128)(2,1)} %copy.56), calls=%async_computation.3 | async-start | bytes 524288 | tf_op jit(solution)/shard_map/all_to_all | solution.py:16
  97.9 18.6 %all-to-all-start.6 = ((bf16[64,8,256]{2,1,0:T(8,128)(2,1)}), bf16[64,8,256]{2,1,0:T(8,128)(2,1)S(1)}, u32[]{:S(2)}, u32[]{:S(2)}) async-start(bf16[64,8,256]{2,1,0:T(8,128)(2,1)} %broadcast_in_dim.8), calls=%async_computation.6 | async-start | bytes 524288 | tf_op jit(solution)/shard_map/all_to_all | solution.py:16
  116.5 11.2 %all-to-all-start.5 = ((f32[8,1,256]{2,1,0:T(1,128)}), f32[8,1,256]{2,1,0:T(1,128)S(1)}, u32[]{:S(2)}, u32[]{:S(2)}) async-start(f32[8,1,256]{2,1,0:T(1,128)} %copy.58), calls=%async_computation.5 | async-start | bytes 16384 | tf_op jit(solution)/shard_map/all_to_all | solution.py:16
  127.6 10.8 %all-to-all-start.7 = ((f32[8,64,128]{2,1,0:T(8,128)}), f32[8,64,128]{2,1,0:T(8,128)S(1)}, u32[]{:S(2)}, u32[]{:S(2)}) async-start(f32[8,64,128]{2,1,0:T(8,128)} %bitcast.50), calls=%async_computation.7 | async-start | bytes 524288 | tf_op jit(solution)/shard_map/all_to_all | solution.py:16
  138.4 19.6 %all-to-all-start.8 = ((bf16[8,64,4,256]{3,1,2,0:T(8,128)(2,1)}), bf16[8,64,4,256]{3,1,2,0:T(8,128)(2,1)S(1)}, u32[]{:S(2)}, u32[]{:S(2)}) async-start(bf16[8,64,4,256]{3,1,2,0:T(8,128)(2,1)} %copy.65), calls=%async_computation.8 | async-start | bytes 2097152 | tf_op jit(solution)/shard_map/all_to_all | solution.py:16

commit v2 on v0

v2 whole, which is shorter than its diff:
```python
import functools

import jax
import jax.numpy as jnp
from jax import lax
from jax.experimental import pallas as pl
from jax.experimental.pallas import tpu as pltpu
from jax.sharding import Mesh
from jax.sharding import PartitionSpec as P

AXES = ("x", "zp", "zn", "core", "zh", "y")
GROUP = ("x", "zn", "core")
CHIPS = ("zp", "zh", "y")
LAT = ("zh", "y")
F32 = jnp.float32
BF16 = jnp.bfloat16


def exchange(value, axes):
    return lax.all_to_all(value, axes, 0, 0, tiled=True)


def dot(a, b, dim_a, dim_b):
    return lax.dot_general(a, b, (((dim_a,), (dim_b,)), ((), ())), preferred_element_type=F32)


def call(body, out_shape, *args, scalars=0, scratch=()):
    specs = [pl.BlockSpec(memory_space=pltpu.SMEM)] * scalars
    specs += [pl.BlockSpec(memory_space=pltpu.VMEM)] * (len(args) - scalars)
    return pl.pallas_call(
        body,
        out_shape=out_shape,
        in_specs=specs,
        out_specs=jax.tree.map(lambda _: pl.BlockSpec(memory_space=pltpu.VMEM), out_shape),
        scratch_shapes=list(scratch),
        compiler_params=pltpu.CompilerParams(vmem_limit_bytes=40 * 1024 * 1024),
    )(*args)


def shape(dims, dtype=BF16):
    return jax.ShapeDtypeStruct(dims, dtype)


def own_slice(place, inputs_ref, out_ref):
    own = inputs_ref[place[0]]
    for j in range(out_ref.shape[0]):
        out_ref[j] = own


def encode(place, features_ref, enc_ref, chosen_ref, codes_ref, active_ref):
    parts, tokens, depth = features_ref.shape
    lat_dev = enc_ref.shape[0]
    total = jnp.zeros((lat_dev, tokens), F32)
    for j in range(parts):
        total = total + dot(enc_ref[:, j * depth : (j + 1) * depth], features_ref[j], 1, 1)
    ids = place[1] + lax.broadcasted_iota(jnp.int32, (lat_dev, tokens), 0)
    chosen = chosen_ref[place[0]]
    active = jnp.zeros((lat_dev, tokens), F32)
    for k in range(chosen.shape[0]):
        active = jnp.where(chosen[k : k + 1] == ids, 1.0, active)
    codes = (total * active).astype(BF16)
    active_ref[...] = active
    for g in range(codes_ref.shape[0]):
        codes_ref[g] = codes


def row_blocks(tokens, n_chips, n_near, n_lat):
    for p in range(n_chips // n_lat):
        for n in range(n_near):
            yield (p * n_near + n) * n_lat, p * n_lat, n


def decode(n_lat, layers, codes_ref, weights_ref, out_ref, rows):
    n_group, lat_dev, tokens = codes_ref.shape
    n_chips, n_rows, cols = out_ref.shape
    n_near = n_group // layers
    flipped = []
    for s in range(layers):
        mine = codes_ref[s * n_near : (s + 1) * n_near].reshape(n_near * lat_dev, tokens)
        flipped.append(mine.T)
    for t in range(layers):
        total = jnp.zeros((tokens, cols), F32)
        for s in range(t + 1):
            near = weights_ref[
                s * n_near : (s + 1) * n_near, t * lat_dev : (t + 1) * lat_dev
            ].reshape(n_near * lat_dev, cols)
            total = total + dot(flipped[s], near, 1, 0)
        for first, chip, n in row_blocks(tokens, n_chips, n_near, n_lat):
            start = chip * n_rows + t * n_near + n
            rows[pl.ds(start, n_lat, stride=n_rows), :] = total[first : first + n_lat]
    out_ref[...] = rows[...].reshape(out_ref.shape).astype(BF16)


def sum_rows(partial_ref, weights_ref, err_ref, pair_ref):
    n_chips, n_rows, cols = partial_ref.shape
    first = weights_ref.shape[1] - 8
    total = partial_ref[0].astype(F32)
    for c in range(1, n_chips):
        total = total + partial_ref[c].astype(F32)
    target = jnp.concatenate(
        [weights_ref[g, first : first + 8][:1].astype(F32) for g in range(n_rows)], axis=0
    )
    errors = total - target
    err_b = errors.astype(BF16)
    high = err_b.astype(F32)
    pair_ref[0] = high
    pair_ref[1] = errors - high
    for c in range(n_chips):
        err_ref[c] = err_b


def backward(n_lat, layers, err_ref, codes_ref, weights_ref, pair_ref, out_ref, rows, mixed):
    n_group, lat_dev, tokens = codes_ref.shape
    n_chips, n_rows, cols = err_ref.shape
    n_near = n_group // layers
    near_lat = n_near * lat_dev
    rows[...] = err_ref[...].astype(F32).reshape(n_chips * n_rows, cols)
    err = []
    for t in range(layers):
        pieces = []
        for first, chip, n in row_blocks(tokens, n_chips, n_near, n_lat):
            start = chip * n_rows + t * n_near + n
            pieces.append(rows[pl.ds(start, n_lat, stride=n_rows), :])
        err.append(jnp.concatenate(pieces, axis=0).astype(BF16))
    dec_rows = layers * lat_dev
    for s in range(layers):
        mine = slice(s * n_near, (s + 1) * n_near)
        codes = codes_ref[mine].reshape(near_lat, tokens)
        total = jnp.zeros((near_lat, tokens), F32)
        for t in range(layers):
            if t < s:
                row = jnp.zeros((near_lat, cols), F32)
            else:
                row = dot(codes, err[t], 1, 0)
                near = weights_ref[mine, t * lat_dev : (t + 1) * lat_dev]
                total = total + dot(near.reshape(near_lat, cols), err[t], 1, 1)
            mixed[pl.ds(t, near_lat, stride=layers), :] = row
        out_ref[mine, 0:dec_rows] = mixed[...].reshape(n_near, dec_rows, cols).astype(BF16)
        total = total.reshape(n_near, lat_dev, tokens).astype(BF16)
        out_ref[mine, dec_rows : dec_rows + lat_dev] = total
    for g in range(n_group):
        high = jnp.broadcast_to(pair_ref[0, g : g + 1], (8, cols))
        low = jnp.broadcast_to(pair_ref[1, g : g + 1], (8, cols))
        first = lax.broadcasted_iota(jnp.int32, (8, cols), 0) == 0
        out_ref[g, dec_rows + lat_dev :] = jnp.where(first, high, low).astype(BF16)


def finish(dec_rows, arrived_ref, features_ref, active_ref, enc_ref, errors_ref):
    n_group, n_rows, cols = arrived_ref.shape
    lat_dev = active_ref.shape[0]
    total = arrived_ref[0, dec_rows : dec_rows + lat_dev].astype(F32)
    for g in range(1, n_group):
        total = total + arrived_ref[g, dec_rows : dec_rows + lat_dev].astype(F32)
    pre_grad = (total * active_ref[...]).astype(BF16)
    parts, _, depth = features_ref.shape
    for j in range(parts):
        enc_ref[:, j * depth : (j + 1) * depth] = dot(pre_grad, features_ref[j], 1, 0).astype(BF16)
    for g in range(n_group):
        pair = arrived_ref[g, dec_rows + lat_dev :].astype(F32)
        errors_ref[:, g * cols : (g + 1) * cols] = pair[0:1] + pair[1:2]


def per_device(inputs, targets, top_index, enc_weight, dec_weight):
    layers, tokens, depth = inputs.shape
    lat_dev = enc_weight.shape[1]
    width = dec_weight.shape[2]
    n_group, n_chips, n_lat = lax.axis_size(GROUP), lax.axis_size(CHIPS), lax.axis_size(LAT)
    cols = width // n_group
    dec_rows = layers * lat_dev
    lat_first = lax.axis_index(("zp", "zn", "core", "zh", "y")) * lat_dev
    place = jnp.stack([lax.axis_index("x"), lat_first]).astype(jnp.int32)

    own = call(own_slice, shape((n_lat, tokens, depth)), place, inputs, scalars=1)
    features = exchange(own, LAT)

    weights = dec_weight.reshape(lat_dev, layers, n_group, cols).transpose(2, 1, 0, 3)
    weights = weights.reshape(n_group, dec_rows, cols)
    target = jnp.broadcast_to(targets.reshape(n_group, 1, cols), (n_group, 8, cols))
    weights = jnp.concatenate([weights, target], axis=1)
    features, weights = lax.optimization_barrier((features, weights))
    weights = exchange(weights, GROUP)

    codes, active = call(
        encode,
        (shape((n_group, lat_dev, tokens)), shape((lat_dev, tokens), F32)),
        place,
        features,
        enc_weight.T,
        top_index.transpose(0, 2, 1),
        scalars=1,
    )
    codes, weights = lax.optimization_barrier((codes, weights))
    codes = exchange(codes, GROUP)

    partial = call(
        functools.partial(decode, n_lat, layers),
        shape((n_chips, n_group, cols)),
        codes,
        weights,
        scratch=[pltpu.VMEM((n_chips * n_group, cols), F32)],
    )
    partial = exchange(partial, CHIPS)
    err_b, pair = call(
        sum_rows,
        (shape((n_chips, n_group, cols)), shape((2, n_group, cols), F32)),
        partial,
        weights,
    )
    err_b = exchange(err_b, CHIPS)
    outgoing = call(
        functools.partial(backward, n_lat, layers),
        shape((n_group, dec_rows + lat_dev + 8, cols)),
        err_b,
        codes,
        weights,
        pair,
        scratch=[
            pltpu.VMEM((n_chips * n_group, cols), F32),
            pltpu.VMEM((n_group * lat_dev, cols), F32),
        ],
    )
    arrived = exchange(outgoing, GROUP)
    grad_enc, errors = call(
        functools.partial(finish, dec_rows),
        (shape((lat_dev, width)), shape((1, width), F32)),
        arrived,
        features,
        active,
    )
    grad_dec = arrived[:, :dec_rows].reshape(n_group, lat_dev, layers, cols)
    grad_dec = grad_dec.transpose(1, 2, 0, 3).reshape(lat_dev, layers, width)
    return errors, grad_enc.T, grad_dec


def solution(mesh):
    fine = Mesh(mesh.devices.reshape(4, 2, 2, 2, 2, 8), AXES)
    in_specs = (
        P(None, None, LAT),
        P(AXES, None),
        P(),
        P(None, AXES),
        P(AXES, None, None),
    )
    out_specs = (P(AXES, None), P(None, AXES), P(AXES, None, None))
    return jax.shard_map(
        per_device, mesh=fine, in_specs=in_specs, out_specs=out_specs, check_vma=False
    )
```

time: 1760 us -> 133 us (0.08)
  waiting for transfers between devices: 1670 us -> 30.7 us
  starting transfers between devices: 0.08 us -> 23.9 us
    all_gather x1 -> x0, waiting for transfers between devices: 1380 us -> none  [per_device(): all_err = lax.all_gather(err_b, ('layer', 'lat'), axis=0, tiled=True)]
    unnamed x3 -> x0, waiting for transfers between devices: 287 us -> none
    all_to_all x0 -> x4, blocking collectives: none -> 67.6 us  [exchange(): return lax.all_to_all(value, axes, 0, 0, tiled=True)]
    all_gather x1 -> x0, blocking collectives: 55.8 us -> none  [per_device(): features = lax.all_gather(own_part, 'lat', axis=1, tiled=True)]
    all_to_all x0 -> x2, waiting for transfers between devices: none -> 30.7 us  [exchange(): return lax.all_to_all(value, axes, 0, 0, tiled=True)]
    all_to_all x0 -> x2, starting transfers between devices: none -> 23.9 us  [exchange(): return lax.all_to_all(value, axes, 0, 0, tiled=True)]
  transfers between devices with their start and end apart: 2 -> 2, of which waited for: 2 -> 2; matrix products, arithmetic and copies ran while one was open for 0% -> 2% of each run, Pallas kernels for 0% -> 1%
where the time goes in v2:
time: 133 us
  blocking collectives  67.6 us (51%)
  waiting for transfers between devices  30.7 us (23%)
  starting transfers between devices  23.9 us (18%)
  Pallas kernels  4.52 us (3%)
  local copies, waits for them, and re-layouts  3.97 us (3%)
    all_to_all x4, blocking collectives, exchange(): return lax.all_to_all(value, axes, 0, 0, tiled=True)  67.6 us
    all_to_all x2, waiting for transfers between devices, exchange(): return lax.all_to_all(value, axes, 0, 0, tiled=True)  30.7 us
    all_to_all x2, starting transfers between devices, exchange(): return lax.all_to_all(value, axes, 0, 0, tiled=True)  23.9 us
    pallas_call x6, Pallas kernels, call(): pl.pallas_call(body, out_shape=out_shape, in_specs=specs, out_specs=jax.t...  4.52 us
  transfers between devices with their start and end apart: 2, of which 2 were waited for; matrix products, arithmetic and copies ran while one was open for 2% of the time, Pallas kernels for 1%

profile of v2, /device:TPU:1, one launch (start us, length us, event | category | flops | bytes accessed | tf_op | source)
XLA Modules:
  0.0 132.6 jit_solution(11168020064563142812)
XLA Ops:
  0.6 0.1 pad_add_fusion.place
  0.7 0.0 copy-start.2
  0.7 0.9 copy-done.2
  1.6 0.0 copy-start.3
  1.6 1.4 %shard_map.76 = bf16[16,128,128]{2,1,0:T(8,128)(2,1)} custom-call(s32[2]{0:T(128)S(1)} %pad_add_fusion.place, bf16[4,128,128]{2,1,0:T(8,128)(2,1)S(1)} %copy-done.2), custom_call_target="tpu_custom_call" | custom-call | tf_op jit(solution)/shard_map/pallas_call | solution.py:30
  3.1 16.2 %all-to-all-start = ((bf16[16,128,128]{2,1,0:T(8,128)(2,1)}), bf16[16,128,128]{2,1,0:T(8,128)(2,1)S(1)}, u32[]{:S(2)}, u32[]{:S(2)}) async-start(bf16[16,128,128]{2,1,0:T(8,128)(2,1)} %shard_map.76), calls=%async_computation | async-start | bytes 1048576 | tf_op jit(solution)/shard_map/all_to_all | solution.py:20
  19.3 0.0 copy-done.3
  19.3 0.7 reshape.20
  20.0 0.0 copy-start.4
  20.0 0.7 copy.8
  20.7 0.0 copy-done.4
  20.8 1.1 pad_maximum_fusion
  21.8 0.0 copy-start
  21.8 0.0 copy-start.1
  21.8 15.5 %all-to-all-done.features_ref = bf16[16,128,128]{2,1,0:T(8,128)(2,1)S(1)} async-done(((bf16[16,128,128]{2,1,0:T(8,128)(2,1)}), bf16[16,128,128]{2,1,0:T(8,128)(2,1)S(1)}, u32[]{:S(2)}, u32[]{:S(2)}) %all-to-all-start) | async-done | bytes 524320 | tf_op jit(solution)/shard_map/all_to_all | solution.py:20
  37.4 7.7 %all-to-all-start.1 = ((bf16[16,264,128]{2,1,0:T(8,128)(2,1)}), bf16[16,264,128]{2,1,0:T(8,128)(2,1)S(1)}, u32[]{:S(2)}, u32[]{:S(2)}) async-start(bf16[16,264,128]{2,1,0:T(8,128)(2,1)} %pad_maximum_fusion), calls=%async_computation.1 | async-start | bytes 2162688 | tf_op jit(solution)/shard_map/all_to_all | solution.py:20
  45.1 0.0 copy-done
  45.1 0.0 copy-done.1
  45.1 1.1 shard_map.77
  46.1 15.2 %all-to-all-done.1.weights_ref = bf16[16,264,128]{2,1,0:T(8,128)(2,1)S(1)} async-done(((bf16[16,264,128]{2,1,0:T(8,128)(2,1)}), bf16[16,264,128]{2,1,0:T(8,128)(2,1)S(1)}, u32[]{:S(2)}, u32[]{:S(2)}) %all-to-all-start.1) | async-done | bytes 1081376 | tf_op jit(solution)/shard_map/all_to_all | solution.py:20
  61.3 10.5 %all_to_all.30.codes_ref = bf16[16,64,128]{2,1,0:T(8,128)(2,1)S(1)} all-to-all(bf16[16,64,128]{2,1,0:T(8,128)(2,1)S(1)} %get-tuple-element.16), channel_id=1, replica_groups=mesh['x'=4,'zp'=2,'zn'=2,'core'=2,'zh'=2,'y'=8] {'x','zn','core'}, dimensions={0} | all-to-all | bytes 524288 | tf_op jit(solution)/shard_map/all_to_all | solution.py:20
  71.8 0.4 shard_map.78
  72.2 17.6 %all_to_all.31.partial_ref = bf16[32,16,128]{2,1,0:T(8,128)(2,1)S(1)} all-to-all(bf16[32,16,128]{2,1,0:T(8,128)(2,1)S(1)} %shard_map.78), channel_id=1, replica_groups=mesh['x'=4,'zp'=2,'zn'=2,'core'=2,'zh'=2,'y'=8] {'zp','zh','y'}, dimensions={0} | all-to-all | bytes 262144 | tf_op jit(solution)/shard_map/all_to_all | solution.py:20
  89.8 14.7 %all_to_all.32.err_ref = bf16[32,16,128]{2,1,0:T(8,128)(2,1)S(1)} all-to-all(bf16[32,16,128]{2,1,0:T(8,128)(2,1)S(1)} %get-tuple-element.18), channel_id=1, replica_groups=mesh['x'=4,'zp'=2,'zn'=2,'core'=2,'zh'=2,'y'=8] {'zp','zh','y'}, dimensions={0} | all-to-all | bytes 262144 | tf_op jit(solution)/shard_map/all_to_all | solution.py:20
  104.5 0.6 shard_map.80
  105.1 24.8 %all_to_all.33.arrived_ref = bf16[16,328,128]{2,1,0:T(8,128)(2,1)S(1)} all-to-all(bf16[16,328,128]{2,1,0:T(8,128)(2,1)S(1)} %shard_map.80), channel_id=1, replica_groups=mesh['x'=4,'zp'=2,'zn'=2,'core'=2,'zh'=2,'y'=8] {'x','zn','core'}, dimensions={0} | all-to-all | bytes 2686976 | tf_op jit(solution)/shard_map/all_to_all | solution.py:20
  129.9 0.1 slice.4
  130.0 1.6 %copy.12 = bf16[16,64,1,4,128]{4,3,0,2,1:T(4,128)(2,1)} copy(bf16[16,64,1,4,128]{4,3,2,1,0:T(4,128)(2,1)S(1)} %bitcast.19) | data formatting | bytes 2097152 | tf_op jit(solution)/shard_map/reshape | solution.py:231
  131.6 1.0 shard_map.81
  (3 shorter events, 0.1 us)
Async XLA Ops:
  0.7 0.9 copy-start.2
  1.6 17.6 %copy-start.3 = (bf16[64,4,2048]{2,1,0:T(4,128)(2,1)S(1)}, bf16[64,4,2048]{2,1,0:T(4,128)(2,1)}, u32[]{:S(2)}) copy-start(bf16[64,4,2048]{2,1,0:T(4,128)(2,1)} %param.9) | copy-start | bytes 3145732
  3.1 34.3 %all-to-all-start = ((bf16[16,128,128]{2,1,0:T(8,128)(2,1)}), bf16[16,128,128]{2,1,0:T(8,128)(2,1)S(1)}, u32[]{:S(2)}, u32[]{:S(2)}) async-start(bf16[16,128,128]{2,1,0:T(8,128)(2,1)} %shard_map.76), calls=%async_computation | async-start | bytes 1048576 | tf_op jit(solution)/shard_map/all_to_all | solution.py:20
  20.0 0.7 copy-start.4
  21.8 23.2 %copy-start = (bf16[2048,64]{0,1:T(8,128)(2,1)S(1)}, bf16[2048,64]{0,1:T(8,128)(2,1)}, u32[]{:S(2)}) copy-start(bf16[2048,64]{0,1:T(8,128)(2,1)} %param.8) | copy-start | bytes 786436
  21.8 23.2 %copy-start.1 = (s32[4,128,64]{1,2,0:T(8,128)S(1)}, s32[4,128,64]{1,2,0:T(8,128)}, u32[]{:S(2)}) copy-start(s32[4,128,64]{1,2,0:T(8,128)} %param.7) | copy-start | bytes 393220
  37.4 23.9 %all-to-all-start.1 = ((bf16[16,264,128]{2,1,0:T(8,128)(2,1)}), bf16[16,264,128]{2,1,0:T(8,128)(2,1)S(1)}, u32[]{:S(2)}, u32[]{:S(2)}) async-start(bf16[16,264,128]{2,1,0:T(8,128)(2,1)} %pad_maximum_fusion), calls=%async_computation.1 | async-start | bytes 2162688 | tf_op jit(solution)/shard_map/all_to_all | solution.py:20

commit v3 on v2

v3 whole, which is shorter than its diff:
```python
import functools

import jax
import jax.numpy as jnp
from jax import lax
from jax.experimental import pallas as pl
from jax.experimental.pallas import tpu as pltpu
from jax.sharding import Mesh
from jax.sharding import PartitionSpec as P

AXES = ("x", "zp", "zn", "core", "zh", "y")
GROUP = ("x", "core")
CHIPS = ("zp", "zn", "zh", "y")
LAT = ("zh", "y")
NEAR_HALVES = ("zp", "zh", "y")
F32 = jnp.float32
BF16 = jnp.bfloat16
LANES = 128


def exchange(value, axes):
    return lax.all_to_all(value, axes, 0, 0, tiled=True)


def dot(a, b, dim_a, dim_b):
    return lax.dot_general(a, b, (((dim_a,), (dim_b,)), ((), ())), preferred_element_type=F32)


def call(body, out_shape, *args, scalars=0, scratch=()):
    specs = [pl.BlockSpec(memory_space=pltpu.SMEM)] * scalars
    specs += [pl.BlockSpec(memory_space=pltpu.VMEM)] * (len(args) - scalars)
    return pl.pallas_call(
        body,
        out_shape=out_shape,
        in_specs=specs,
        out_specs=jax.tree.map(lambda _: pl.BlockSpec(memory_space=pltpu.VMEM), out_shape),
        scratch_shapes=list(scratch),
        compiler_params=pltpu.CompilerParams(vmem_limit_bytes=40 * 1024 * 1024),
    )(*args)


def shape(dims, dtype=BF16):
    return jax.ShapeDtypeStruct(dims, dtype)


def own_slice(place, inputs_ref, out_ref):
    own = inputs_ref[place[0]]
    for j in range(out_ref.shape[0]):
        out_ref[j] = own


def encode(place, features_ref, enc_ref, chosen_ref, codes_ref, active_ref):
    parts, tokens, depth = features_ref.shape
    lat_dev = enc_ref.shape[0]
    total = jnp.zeros((lat_dev, tokens), F32)
    for j in range(parts):
        total = total + dot(enc_ref[:, j * depth : (j + 1) * depth], features_ref[j], 1, 1)
    ids = place[1] + lax.broadcasted_iota(jnp.int32, (lat_dev, tokens), 0)
    chosen = chosen_ref[place[0]]
    active = jnp.zeros((lat_dev, tokens), F32)
    for k in range(chosen.shape[0]):
        active = jnp.where(chosen[k : k + 1] == ids, 1.0, active)
    codes = (total * active).astype(BF16)
    active_ref[...] = active
    for g in range(codes_ref.shape[0]):
        codes_ref[g] = codes


def row_blocks(tokens, n_chips, n_near, n_lat):
    for p in range(n_chips // n_lat):
        for n in range(n_near):
            yield (p * n_near + n) * n_lat, p * n_lat, n


def decode(n_lat, place, codes_ref, p0, p1, p2, p3, out_ref, weights_ref, *rows):
    n_group, lat_dev, tokens = codes_ref.shape
    n_chips, n_rows, cols = out_ref.shape
    layers = weights_ref.shape[0]
    n_near = n_group // layers
    for d, piece in enumerate((p0, p1, p2, p3)):
        weights_ref[lax.rem(place[0] + layers - d, layers)] = piece[...]
    flipped = []
    for s in range(layers):
        mine = codes_ref[s * n_near : (s + 1) * n_near].reshape(n_near * lat_dev, tokens)
        flipped.append(mine.T)
    for t in range(layers):
        total = jnp.zeros((tokens, cols), F32)
        for s in range(t + 1):
            near = weights_ref[s, t, :, :lat_dev].reshape(n_near * lat_dev, cols)
            total = total + dot(flipped[s], near, 1, 0)
        for first, chip, n in row_blocks(tokens, n_chips, n_near, n_lat):
            start = chip * n_rows + t * n_near + n
            for i, row in enumerate(rows):
                piece = total[first : first + n_lat, i * LANES : (i + 1) * LANES]
                row[pl.ds(start, n_lat, stride=n_rows), :] = piece
    for i, row in enumerate(rows):
        piece = row[...].reshape(n_chips, n_rows, LANES).astype(BF16)
        out_ref[:, :, i * LANES : (i + 1) * LANES] = piece


def sum_rows(partial_ref, weights_ref, err_ref, pair_ref):
    n_chips, n_rows, cols = partial_ref.shape
    layers, _, n_near, padded, _ = weights_ref.shape
    total = partial_ref[0].astype(F32)
    for c in range(1, n_chips):
        total = total + partial_ref[c].astype(F32)
    target = jnp.concatenate(
        [
            weights_ref[t, 0, n, padded - 8 :].astype(F32)[:1]
            for t in range(layers)
            for n in range(n_near)
        ],
        axis=0,
    )
    errors = total - target
    err_b = errors.astype(BF16)
    high = err_b.astype(F32)
    pair_ref[0] = high
    pair_ref[1] = errors - high
    for c in range(n_chips):
        err_ref[c] = err_b


def backward(n_lat, layers, err_ref, codes_ref, weights_ref, pair_ref, out_ref, *scratch):
    n_group, lat_dev, tokens = codes_ref.shape
    n_chips, n_rows, cols = err_ref.shape
    n_near = n_group // layers
    near_lat = n_near * lat_dev
    parts = cols // LANES
    rows, mixed = scratch[:parts], scratch[parts:]
    for i, row in enumerate(rows):
        piece = err_ref[:, :, i * LANES : (i + 1) * LANES].astype(F32)
        row[...] = piece.reshape(n_chips * n_rows, LANES)
    err = []
    for t in range(layers):
        pieces = []
        for first, chip, n in row_blocks(tokens, n_chips, n_near, n_lat):
            start = chip * n_rows + t * n_near + n
            piece = [row[pl.ds(start, n_lat, stride=n_rows), :] for row in rows]
            pieces.append(jnp.concatenate(piece, axis=1))
        err.append(jnp.concatenate(pieces, axis=0).astype(BF16))
    dec_rows = layers * lat_dev
    grad_rows = lat_dev * tokens // cols
    for s in range(layers):
        mine = slice(s * n_near, (s + 1) * n_near)
        codes = codes_ref[mine].reshape(near_lat, tokens)
        total = jnp.zeros((near_lat, tokens), F32)
        for t in range(layers):
            if t < s:
                row = jnp.zeros((near_lat, cols), F32)
            else:
                row = dot(codes, err[t], 1, 0)
                near = weights_ref[s, t, :, :lat_dev]
                total = total + dot(near.reshape(near_lat, cols), err[t], 1, 1)
            for i, part in enumerate(mixed):
                piece = row[:, i * LANES : (i + 1) * LANES]
                part[pl.ds(t, near_lat, stride=layers), :] = piece
        for i, part in enumerate(mixed):
            piece = part[...].reshape(n_near, dec_rows, LANES).astype(BF16)
            out_ref[mine, 0:dec_rows, i * LANES : (i + 1) * LANES] = piece
        total = total.reshape(n_near, cols // tokens, grad_rows, tokens).astype(BF16)
        for i in range(cols // tokens):
            lanes = slice(i * tokens, (i + 1) * tokens)
            out_ref[mine, dec_rows : dec_rows + grad_rows, lanes] = total[:, i]
    for g in range(n_group):
        high = jnp.broadcast_to(pair_ref[0, g : g + 1], (8, cols))
        low = jnp.broadcast_to(pair_ref[1, g : g + 1], (8, cols))
        first = lax.broadcasted_iota(jnp.int32, (8, cols), 0) == 0
        out_ref[g, dec_rows + grad_rows :] = jnp.where(first, high, low).astype(BF16)


def finish(dec_rows, layers, arrived_ref, features_ref, active_ref, enc_ref, errors_ref):
    n_group, _, cols = arrived_ref.shape
    lat_dev, tokens = active_ref.shape
    grad_rows = lat_dev * tokens // cols
    n_near = n_group // layers
    total = arrived_ref[0, dec_rows : dec_rows + grad_rows].astype(F32)
    for g in range(1, n_group):
        total = total + arrived_ref[g, dec_rows : dec_rows + grad_rows].astype(F32)
    halves = [total[:, i * tokens : (i + 1) * tokens] for i in range(cols // tokens)]
    pre_grad = (jnp.concatenate(halves, axis=0) * active_ref[...]).astype(BF16)
    parts, _, depth = features_ref.shape
    for j in range(parts):
        enc_ref[:, j * depth : (j + 1) * depth] = dot(pre_grad, features_ref[j], 1, 0).astype(BF16)
    for g in range(n_group):
        pair = arrived_ref[g, dec_rows + grad_rows :].astype(F32)
        first = (g % n_near * layers + g // n_near) * cols
        errors_ref[:, first : first + cols] = pair[0:1] + pair[1:2]


def shift(value, axis, by):
    count = lax.axis_size(axis)
    return lax.ppermute(value, axis, [(i, (i + by) % count) for i in range(count)])


def per_device(inputs, targets, top_index, enc_weight, dec_weight):
    layers, tokens, depth = inputs.shape
    lat_dev = enc_weight.shape[1]
    width = dec_weight.shape[2]
    n_group, n_chips, n_lat = lax.axis_size(GROUP), lax.axis_size(CHIPS), lax.axis_size(LAT)
    n_near = n_group // layers
    cols = width // n_group
    half = width // n_near
    dec_rows = layers * lat_dev
    grad_rows = lat_dev * tokens // cols
    x, core = lax.axis_index("x"), lax.axis_index("core")
    lat_first = lax.axis_index(("zp", "zn", "core", "zh", "y")) * lat_dev
    place = jnp.stack([x, lat_first]).astype(jnp.int32)

    padded = lat_dev + 8
    target = jnp.broadcast_to(targets[None], (8, layers, width))
    both = jnp.concatenate([dec_weight, target], axis=0)
    kept = lax.dynamic_slice_in_dim(both, core * half, half, 2)
    sent = lax.dynamic_slice_in_dim(both, (1 - core) * half, half, 2)
    came = shift(sent, "core", 1)

    n_y = lax.axis_size("y")
    pairs = [[zp * 2 + 0, (1 - zp) * 2 + 1] for zp in range(2)]
    groups = [[i * n_y + y for i in pair for y in range(n_y)] for pair in pairs]
    own = call(own_slice, shape((n_lat, tokens, depth)), place, inputs, scalars=1)
    features = lax.all_to_all(own, NEAR_HALVES, 0, 0, tiled=True, axis_index_groups=groups)

    mine = jnp.where(core == 0, jnp.stack([kept, came]), jnp.stack([came, kept]))
    mine = mine.reshape(n_near, padded, layers, layers, cols).transpose(3, 2, 0, 1, 4)
    pieces = [lax.dynamic_index_in_dim(mine, x, 0, keepdims=False)]
    for d in range(1, layers):
        piece = lax.dynamic_index_in_dim(mine, (x + d) % layers, 0, keepdims=False)
        pieces.append(shift(piece, "x", d))

    codes, active = call(
        encode,
        (shape((n_group, lat_dev, tokens)), shape((lat_dev, tokens), F32)),
        place,
        features,
        enc_weight.T,
        top_index.transpose(0, 2, 1),
        scalars=1,
    )
    codes = exchange(codes, GROUP)

    partial, weights = call(
        functools.partial(decode, n_lat),
        (shape((n_chips, n_group, cols)), shape((layers, layers, n_near, padded, cols))),
        place,
        codes,
        *pieces,
        scalars=1,
        scratch=[pltpu.VMEM((n_chips * n_group, LANES), F32)] * (cols // LANES),
    )
    partial = exchange(partial, CHIPS)
    err_b, pair = call(
        sum_rows,
        (shape((n_chips, n_group, cols)), shape((2, n_group, cols), F32)),
        partial,
        weights,
    )
    err_b = exchange(err_b, CHIPS)
    outgoing = call(
        functools.partial(backward, n_lat, layers),
        shape((n_group, dec_rows + grad_rows + 8, cols)),
        err_b,
        codes,
        weights,
        pair,
        scratch=[pltpu.VMEM((n_chips * n_group, LANES), F32)] * (cols // LANES)
        + [pltpu.VMEM((n_near * dec_rows, LANES), F32)] * (cols // LANES),
    )
    arrived = exchange(outgoing, GROUP)
    grad_enc, errors = call(
        functools.partial(finish, dec_rows, layers),
        (shape((lat_dev, width)), shape((1, width), F32)),
        arrived,
        features,
        active,
    )
    grad_dec = arrived[:, :dec_rows].reshape(layers, n_near, lat_dev, layers, cols)
    grad_dec = grad_dec.transpose(2, 3, 1, 0, 4).reshape(lat_dev, layers, width)
    return errors, grad_enc.T, grad_dec


def solution(mesh):
    fine = Mesh(mesh.devices.reshape(4, 2, 2, 2, 2, 8), AXES)
    in_specs = (
        P(None, None, LAT),
        P(AXES, None),
        P(),
        P(None, AXES),
        P(AXES, None, None),
    )
    out_specs = (P(AXES, None), P(None, AXES), P(AXES, None, None))
    return jax.shard_map(
        per_device, mesh=fine, in_specs=in_specs, out_specs=out_specs, check_vma=False
    )
```

time: 133 us -> 123 us (0.925)
  waiting for transfers between devices: 30.7 us -> 11.3 us
  starting transfers between devices: 23.9 us -> 34.6 us
  blocking collectives: 67.6 us -> 59.1 us
  local copies, waits for them, and re-layouts: 3.97 us -> 7.92 us
  other arithmetic: 1.17 us -> 2.69 us
  Pallas kernels: 4.52 us -> 5.9 us
    all_to_all x2 -> x1, waiting for transfers between devices: 30.7 us -> 5.26 us  [exchange(): return lax.all_to_all(value, axes, 0, 0, tiled=True)]
    ppermute x0 -> x4, starting transfers between devices: none -> 18.2 us  [shift(): lax.ppermute(value, axis, [(i, (i + by) % count) for i in range(count)])]
    all_to_all x2 -> x1, starting transfers between devices: 23.9 us -> 6.31 us  [exchange(): return lax.all_to_all(value, axes, 0, 0, tiled=True)]
    all_to_all x0 -> x1, starting transfers between devices: none -> 10 us  [per_device(): lax.all_to_all(own, NEAR_HALVES, 0, 0, tiled=True, axis_index_groups=groups)]
    all_to_all x4 -> x3, blocking collectives: 67.6 us -> 59.1 us  [exchange(): return lax.all_to_all(value, axes, 0, 0, tiled=True)]
    all_to_all x0 -> x1, waiting for transfers between devices: none -> 6.05 us  [per_device(): lax.all_to_all(own, NEAR_HALVES, 0, 0, tiled=True, axis_index_groups=groups)]
    transpose x0 -> x1, local copies, waits for them, and re-layouts: none -> 2.33 us  [per_device(): grad_dec = grad_dec.transpose(2, 3, 1, 0, 4).reshape(lat_dev, layers, width)]
    pallas_call x6, Pallas kernels: 4.52 us -> 5.9 us  [call(): pl.pallas_call(body, out_shape=out_shape, in_specs=specs, out_specs=jax.t...]
  transfers between devices with their start and end apart: 2 -> 6, of which waited for: 2 -> 2; matrix products, arithmetic and copies ran while one was open for 2% -> 1% of each run, Pallas kernels for 1% -> 3%
where the time goes in v3:
time: 123 us; the launch traced here: 122 us
  blocking collectives  59.1 us (48%)
  starting transfers between devices  34.6 us (28%)
  waiting for transfers between devices  11.3 us (9%)
  local copies, waits for them, and re-layouts  7.92 us (6%)
  Pallas kernels  5.9 us (5%)
  other arithmetic  2.69 us (2%)
    all_to_all x3, blocking collectives, exchange(): return lax.all_to_all(value, axes, 0, 0, tiled=True)  59.1 us
    ppermute x4, starting transfers between devices, shift(): lax.ppermute(value, axis, [(i, (i + by) % count) for i in range(count)])  18.2 us
    all_to_all x1, starting transfers between devices, per_device(): lax.all_to_all(own, NEAR_HALVES, 0, 0, tiled=True, axis_index_groups=groups)  10 us
    all_to_all x1, starting transfers between devices, exchange(): return lax.all_to_all(value, axes, 0, 0, tiled=True)  6.31 us
    all_to_all x1, waiting for transfers between devices, per_device(): lax.all_to_all(own, NEAR_HALVES, 0, 0, tiled=True, axis_index_groups=groups)  6.05 us
    pallas_call x6, Pallas kernels, call(): pl.pallas_call(body, out_shape=out_shape, in_specs=specs, out_specs=jax.t...  5.9 us
    all_to_all x1, waiting for transfers between devices, exchange(): return lax.all_to_all(value, axes, 0, 0, tiled=True)  5.26 us
  transfers between devices with their start and end apart: 6, of which 2 were waited for; matrix products, arithmetic and copies ran while one was open for 1% of the time, Pallas kernels for 3%

profile of v3, /device:TPU:1, one launch (start us, length us, event | category | flops | bytes accessed | tf_op | source)
XLA Modules:
  0.0 122.4 jit_solution(16768529637301739155)
XLA Ops:
  0.6 0.7 reduce
  1.4 0.0 copy-start.2
  1.4 1.8 %fusion.1 = (bf16[72,4,1024]{2,1,0:T(4,128)(2,1)S(1)}, bf16[72,4,1024]{2,1,0:T(4,128)(2,1)S(1)}) fusion(s32[]{:T(128)S(6)} %select_n.44, bf16[8,4,2048]{2,1,0:T(4,128)(2,1)S(1)} %broadcast_in_dim.9, bf16[64,4,2048]{2,1,0:T(4,128)(2,1)} %param.9, s32[]{:T(128)S(6)} %select_n.45), kind=kLoop, calls=%fused_computation.6 | loop fusion | flops 2359296 | bytes 2359304 | tf_op jit(solution)/shard_map/concatenate | solution.py:212
  3.2 8.8 %collective-permute-start = (bf16[72,4,1024]{2,1,0:T(4,128)(2,1)S(1)}, bf16[72,4,1024]{2,1,0:T(4,128)(2,1)S(1)}, u32[]{:S(2)}, u32[]{:S(2)}) collective-permute-start(bf16[72,4,1024]{2,1,0:T(4,128)(2,1)S(1)} %get-tuple-element.24), channel_id=1, source_target_pairs={{0,16},{16,0},{1,17},{17,1},{2,18},{18,2},{3,19},{19,3},{4,20},{20... | collective-permute-start | bytes 1769480 | tf_op jit(solution)/shard_map/ppermute | solution.py:193
  12.0 0.1 pad_add_fusion.place
  12.1 0.0 copy-done.2
  12.1 1.4 %shard_map.76 = bf16[16,128,128]{2,1,0:T(8,128)(2,1)} custom-call(s32[2]{0:T(128)S(1)} %pad_add_fusion.place, bf16[4,128,128]{2,1,0:T(8,128)(2,1)S(1)} %copy-done.2), custom_call_target="tpu_custom_call" | custom-call | tf_op jit(solution)/shard_map/pallas_call | solution.py:32
  13.5 10.0 %all-to-all-start = ((bf16[16,128,128]{2,1,0:T(8,128)(2,1)}), bf16[16,128,128]{2,1,0:T(8,128)(2,1)S(1)}, u32[]{:S(2)}, u32[]{:S(2)}) async-start(bf16[16,128,128]{2,1,0:T(8,128)(2,1)} %shard_map.76), calls=%async_computation | async-start | bytes 1048576 | tf_op jit(solution)/shard_map/all_to_all | solution.py:221
  23.6 0.2 reshape.24
  23.8 0.2 copy.11
  24.0 0.0 collective-permute-done
  24.0 0.2 reshape.25
  24.3 0.2 copy.12
  24.5 0.1 maximum_select_fusion
  24.6 0.0 copy-start
  24.6 0.0 copy-start.1
  24.6 0.1 dynamic-slice_bitcast_fusion
  24.7 4.5 %collective-permute-start.3 = (bf16[4,2,72,256]{3,2,1,0:T(8,128)(2,1)S(1)}, bf16[4,2,72,256]{3,2,1,0:T(8,128)(2,1)S(1)}, u32[]{:S(2)}, u32[]{:S(2)}) collective-permute-start(bf16[4,2,72,256]{3,2,1,0:T(8,128)(2,1)S(1)} %get-tuple-element.19), channel_id=1, source_target_pairs={{0,384},{128,0},{256,128},{384,256},{1,385},{129,1},{257,129},{385... | collective-permute-start | bytes 884744 | tf_op jit(solution)/shard_map/ppermute | solution.py:193
  29.2 2.4 %collective-permute-start.2 = (bf16[4,2,72,256]{3,2,1,0:T(8,128)(2,1)S(1)}, bf16[4,2,72,256]{3,2,1,0:T(8,128)(2,1)S(1)}, u32[]{:S(2)}, u32[]{:S(2)}) collective-permute-start(bf16[4,2,72,256]{3,2,1,0:T(8,128)(2,1)S(1)} %get-tuple-element.20), channel_id=1, source_target_pairs={{0,256},{128,384},{256,0},{384,128},{1,257},{129,385},{257,1},{385... | collective-permute-start | bytes 884744 | tf_op jit(solution)/shard_map/ppermute | solution.py:193
  31.7 2.5 %collective-permute-start.1 = (bf16[4,2,72,256]{3,2,1,0:T(8,128)(2,1)S(1)}, bf16[4,2,72,256]{3,2,1,0:T(8,128)(2,1)S(1)}, u32[]{:S(2)}, u32[]{:S(2)}) collective-permute-start(bf16[4,2,72,256]{3,2,1,0:T(8,128)(2,1)S(1)} %get-tuple-element.21), channel_id=1, source_target_pairs={{0,128},{128,256},{256,384},{384,0},{1,129},{129,257},{257,385},{3... | collective-permute-start | bytes 884744 | tf_op jit(solution)/shard_map/ppermute | solution.py:193
  34.2 6.1 %all-to-all-done.features_ref = bf16[16,128,128]{2,1,0:T(8,128)(2,1)S(1)} async-done(((bf16[16,128,128]{2,1,0:T(8,128)(2,1)}), bf16[16,128,128]{2,1,0:T(8,128)(2,1)S(1)}, u32[]{:S(2)}, u32[]{:S(2)}) %all-to-all-start) | async-done | bytes 524320 | tf_op jit(solution)/shard_map/all_to_all | solution.py:221
  40.2 0.0 copy-done
  40.2 0.0 copy-done.1
  40.2 1.7 %shard_map.77 = (bf16[8,64,128]{2,1,0:T(8,128)(2,1)}, f32[64,128]{1,0:T(8,128)S(1)}) custom-call(s32[2]{0:T(128)S(1)} %pad_add_fusion.place, bf16[16,128,128]{2,1,0:T(8,128)(2,1)S(1)} %all-to-all-done.features_ref, bf16[64,2048]{1,0:T(8,128)(2,1)S(1)} %bitcast.22, s32[4,64,128]{2,1,0:T(8,128)S(1)} %bitcast.23), custom_call_target="tpu_custom_call" | custom-call | tf_op jit(solution)/shard_map/pallas_call | solution.py:32
  41.9 6.3 %all-to-all-start.1 = ((bf16[8,64,128]{2,1,0:T(8,128)(2,1)}), bf16[8,64,128]{2,1,0:T(8,128)(2,1)S(1)}, u32[]{:S(2)}, u32[]{:S(2)}) async-start(bf16[8,64,128]{2,1,0:T(8,128)(2,1)} %get-tuple-element.11), calls=%async_computation.1 | async-start | bytes 262144 | tf_op jit(solution)/shard_map/all_to_all | solution.py:22
  48.3 0.0 collective-permute-done.3.p3
  48.3 0.0 collective-permute-done.2.p2
  48.3 0.0 collective-permute-done.1.p1
  48.3 5.3 %all-to-all-done.1.codes_ref = bf16[8,64,128]{2,1,0:T(8,128)(2,1)S(1)} async-done(((bf16[8,64,128]{2,1,0:T(8,128)(2,1)}), bf16[8,64,128]{2,1,0:T(8,128)(2,1)S(1)}, u32[]{:S(2)}, u32[]{:S(2)}) %all-to-all-start.1) | async-done | bytes 131104 | tf_op jit(solution)/shard_map/all_to_all | solution.py:22
  53.5 1.0 shard_map.78
  54.5 18.2 %all_to_all.25.partial_ref = bf16[64,8,256]{2,1,0:T(8,128)(2,1)S(1)} all-to-all(bf16[64,8,256]{2,1,0:T(8,128)(2,1)S(1)} %get-tuple-element.12), channel_id=1, replica_groups=mesh['x'=4,'zp'=2,'zn'=2,'core'=2,'zh'=2,'y'=8] {'zp','zn','zh','y'}, dimensions={0} | all-to-all | bytes 524288 | tf_op jit(solution)/shard_map/all_to_all | solution.py:22
  72.7 0.1 shard_map.79
  72.8 18.3 %all_to_all.26.err_ref = bf16[64,8,256]{2,1,0:T(8,128)(2,1)S(1)} all-to-all(bf16[64,8,256]{2,1,0:T(8,128)(2,1)S(1)} %get-tuple-element.14), channel_id=1, replica_groups=mesh['x'=4,'zp'=2,'zn'=2,'core'=2,'zh'=2,'y'=8] {'zp','zn','zh','y'}, dimensions={0} | all-to-all | bytes 524288 | tf_op jit(solution)/shard_map/all_to_all | solution.py:22
  91.1 0.7 shard_map.80
  91.8 22.7 %all_to_all.27.arrived_ref = bf16[8,296,256]{2,1,0:T(8,128)(2,1)S(1)} all-to-all(bf16[8,296,256]{2,1,0:T(8,128)(2,1)S(1)} %shard_map.80), channel_id=1, replica_groups=mesh['x'=4,'zp'=2,'zn'=2,'core'=2,'zh'=2,'y'=8] {'x','core'}, dimensions={0} | all-to-all | bytes 2424832 | tf_op jit(solution)/shard_map/all_to_all | solution.py:22
  114.5 1.0 slice.4
  115.5 1.3 %reshape.22 = bf16[4,2,64,4,256]{4,3,2,1,0:T(4,128)(2,1)S(1)} reshape(bf16[8,256,256]{2,1,0:T(8,128)(2,1)} %slice.4) | data formatting | bytes 2097152 | tf_op jit(solution)/shard_map/reshape | solution.py:276
  116.9 2.3 %copy.15 = bf16[64,4,2,4,256]{4,3,2,1,0:T(4,128)(2,1)} copy(bf16[64,4,2,4,256]{4,1,0,2,3:T(4,128)(2,1)S(1)} %bitcast.24) | data formatting | bytes 2097152 | tf_op jit(solution)/shard_map/transpose | solution.py:277
  119.2 2.2 %reshape.23 = bf16[64,4,2048]{2,1,0:T(4,128)(2,1)} reshape(bf16[64,4,2,4,256]{4,3,2,1,0:T(4,128)(2,1)} %copy.15) | data formatting | bytes 2097152 | tf_op jit(solution)/shard_map/reshape | solution.py:277
  121.4 1.0 shard_map.81
  (1 shorter events, 0.0 us)
Async XLA Ops:
  1.4 10.7 %copy-start.2 = (bf16[4,128,128]{2,1,0:T(8,128)(2,1)S(1)}, bf16[4,128,128]{2,1,0:T(8,128)(2,1)}, u32[]{:S(2)}) copy-start(bf16[4,128,128]{2,1,0:T(8,128)(2,1)} %inputs_ref.1) | copy-start | bytes 393220
  3.2 20.8 %collective-permute-start = (bf16[72,4,1024]{2,1,0:T(4,128)(2,1)S(1)}, bf16[72,4,1024]{2,1,0:T(4,128)(2,1)S(1)}, u32[]{:S(2)}, u32[]{:S(2)}) collective-permute-start(bf16[72,4,1024]{2,1,0:T(4,128)(2,1)S(1)} %get-tuple-element.24), channel_id=1, source_target_pairs={{0,16},{16,0},{1,17},{17,1},{2,18},{18,2},{3,19},{19,3},{4,20},{20... | collective-permute-start | bytes 1769480 | tf_op jit(solution)/shard_map/ppermute | solution.py:193
  13.5 26.7 %all-to-all-start = ((bf16[16,128,128]{2,1,0:T(8,128)(2,1)}), bf16[16,128,128]{2,1,0:T(8,128)(2,1)S(1)}, u32[]{:S(2)}, u32[]{:S(2)}) async-start(bf16[16,128,128]{2,1,0:T(8,128)(2,1)} %shard_map.76), calls=%async_computation | async-start | bytes 1048576 | tf_op jit(solution)/shard_map/all_to_all | solution.py:221
  24.6 15.7 %copy-start = (bf16[2048,64]{0,1:T(8,128)(2,1)S(1)}, bf16[2048,64]{0,1:T(8,128)(2,1)}, u32[]{:S(2)}) copy-start(bf16[2048,64]{0,1:T(8,128)(2,1)} %param.8) | copy-start | bytes 786436
  24.6 15.7 %copy-start.1 = (s32[4,128,64]{1,2,0:T(8,128)S(1)}, s32[4,128,64]{1,2,0:T(8,128)}, u32[]{:S(2)}) copy-start(s32[4,128,64]{1,2,0:T(8,128)} %param.7) | copy-start | bytes 393220
  24.7 23.6 %collective-permute-start.3 = (bf16[4,2,72,256]{3,2,1,0:T(8,128)(2,1)S(1)}, bf16[4,2,72,256]{3,2,1,0:T(8,128)(2,1)S(1)}, u32[]{:S(2)}, u32[]{:S(2)}) collective-permute-start(bf16[4,2,72,256]{3,2,1,0:T(8,128)(2,1)S(1)} %get-tuple-element.19), channel_id=1, source_target_pairs={{0,384},{128,0},{256,128},{384,256},{1,385},{129,1},{257,129},{385... | collective-permute-start | bytes 884744 | tf_op jit(solution)/shard_map/ppermute | solution.py:193
  29.2 19.0 %collective-permute-start.2 = (bf16[4,2,72,256]{3,2,1,0:T(8,128)(2,1)S(1)}, bf16[4,2,72,256]{3,2,1,0:T(8,128)(2,1)S(1)}, u32[]{:S(2)}, u32[]{:S(2)}) collective-permute-start(bf16[4,2,72,256]{3,2,1,0:T(8,128)(2,1)S(1)} %get-tuple-element.20), channel_id=1, source_target_pairs={{0,256},{128,384},{256,0},{384,128},{1,257},{129,385},{257,1},{385... | collective-permute-start | bytes 884744 | tf_op jit(solution)/shard_map/ppermute | solution.py:193
  31.7 16.6 %collective-permute-start.1 = (bf16[4,2,72,256]{3,2,1,0:T(8,128)(2,1)S(1)}, bf16[4,2,72,256]{3,2,1,0:T(8,128)(2,1)S(1)}, u32[]{:S(2)}, u32[]{:S(2)}) collective-permute-start(bf16[4,2,72,256]{3,2,1,0:T(8,128)(2,1)S(1)} %get-tuple-element.21), channel_id=1, source_target_pairs={{0,128},{128,256},{256,384},{384,0},{1,129},{129,257},{257,385},{3... | collective-permute-start | bytes 884744 | tf_op jit(solution)/shard_map/ppermute | solution.py:193
  41.9 11.6 %all-to-all-start.1 = ((bf16[8,64,128]{2,1,0:T(8,128)(2,1)}), bf16[8,64,128]{2,1,0:T(8,128)(2,1)S(1)}, u32[]{:S(2)}, u32[]{:S(2)}) async-start(bf16[8,64,128]{2,1,0:T(8,128)(2,1)} %get-tuple-element.11), calls=%async_computation.1 | async-start | bytes 262144 | tf_op jit(solution)/shard_map/all_to_all | solution.py:22

commit v4 on v3

v4 whole, which is shorter than its diff:
```python
import functools

import jax
import jax.numpy as jnp
from jax import lax
from jax.experimental import pallas as pl
from jax.experimental.pallas import tpu as pltpu
from jax.sharding import Mesh
from jax.sharding import PartitionSpec as P

AXES = ("x", "zp", "zn", "core", "zh", "y")
GROUP = ("x", "core")
CHIPS = ("zp", "zn", "zh", "y")
LAT = ("zh", "y")
NEAR_HALVES = ("zp", "zh", "y")
F32 = jnp.float32
BF16 = jnp.bfloat16
LANES = 128


def exchange(value, axes):
    return lax.all_to_all(value, axes, 0, 0, tiled=True)


def dot(a, b, dim_a, dim_b):
    return lax.dot_general(a, b, (((dim_a,), (dim_b,)), ((), ())), preferred_element_type=F32)


def call(body, out_shape, *args, scalars=0, scratch=()):
    specs = [pl.BlockSpec(memory_space=pltpu.SMEM)] * scalars
    specs += [pl.BlockSpec(memory_space=pltpu.VMEM)] * (len(args) - scalars)
    return pl.pallas_call(
        body,
        out_shape=out_shape,
        in_specs=specs,
        out_specs=jax.tree.map(lambda _: pl.BlockSpec(memory_space=pltpu.VMEM), out_shape),
        scratch_shapes=list(scratch),
        compiler_params=pltpu.CompilerParams(vmem_limit_bytes=40 * 1024 * 1024),
    )(*args)


def shape(dims, dtype=BF16):
    return jax.ShapeDtypeStruct(dims, dtype)


def own_slice(place, inputs_ref, out_ref):
    own = inputs_ref[place[0]]
    for j in range(out_ref.shape[0]):
        out_ref[j] = own


def encode(
    n_near, place, features_ref, target_ref, enc_ref, chosen_ref, codes_ref, active_ref
):
    parts, tokens, depth = features_ref.shape
    lat_dev = enc_ref.shape[0]
    total = jnp.zeros((lat_dev, tokens), F32)
    for j in range(parts):
        total = total + dot(enc_ref[:, j * depth : (j + 1) * depth], features_ref[j], 1, 1)
    ids = place[1] + lax.broadcasted_iota(jnp.int32, (lat_dev, tokens), 0)
    chosen = chosen_ref[place[0]]
    active = jnp.zeros((lat_dev, tokens), F32)
    for k in range(chosen.shape[0]):
        active = jnp.where(chosen[k : k + 1] == ids, 1.0, active)
    codes = (total * active).astype(BF16)
    active_ref[...] = active
    n_group = codes_ref.shape[0]
    cols = target_ref.shape[1] // n_group
    for g in range(n_group):
        codes_ref[g, :lat_dev] = codes
        first = (g % n_near * (n_group // n_near) + g // n_near) * cols
        target = target_ref[:, first : first + cols].astype(F32)
        pair = [target[:, i : i + LANES] for i in range(0, cols, LANES)]
        rows = jnp.concatenate(pair + [jnp.zeros((8 - len(pair), LANES), F32)], axis=0)
        codes_ref[g, lat_dev:] = rows.astype(BF16)


def row_blocks(tokens, n_chips, n_near, n_lat):
    for p in range(n_chips // n_lat):
        for n in range(n_near):
            yield (p * n_near + n) * n_lat, p * n_lat, n


def arrange(place, after, p0, p1, p2, p3, weights_ref):
    del after
    layers = weights_ref.shape[0]
    for d, piece in enumerate((p0, p1, p2, p3)):
        weights_ref[lax.rem(place[0] + layers - d, layers)] = piece[...]


def decode(n_lat, codes_ref, weights_ref, out_ref, *rows):
    n_group, _, tokens = codes_ref.shape
    n_chips, n_rows, cols = out_ref.shape
    layers, _, _, lat_dev, _ = weights_ref.shape
    n_near = n_group // layers
    flipped = []
    for s in range(layers):
        mine = codes_ref[s * n_near : (s + 1) * n_near, :lat_dev].reshape(-1, tokens)
        flipped.append(mine.T)
    for t in range(layers):
        total = jnp.zeros((tokens, cols), F32)
        for s in range(t + 1):
            near = weights_ref[s, t].reshape(n_near * lat_dev, cols)
            total = total + dot(flipped[s], near, 1, 0)
        for first, chip, n in row_blocks(tokens, n_chips, n_near, n_lat):
            start = chip * n_rows + t * n_near + n
            for i, row in enumerate(rows):
                piece = total[first : first + n_lat, i * LANES : (i + 1) * LANES]
                row[pl.ds(start, n_lat, stride=n_rows), :] = piece
    for i, row in enumerate(rows):
        piece = row[...].reshape(n_chips, n_rows, LANES).astype(BF16)
        out_ref[:, :, i * LANES : (i + 1) * LANES] = piece


def sum_rows(partial_ref, codes_ref, err_ref, pair_ref):
    n_chips, n_rows, cols = partial_ref.shape
    total = partial_ref[0].astype(F32)
    for c in range(1, n_chips):
        total = total + partial_ref[c].astype(F32)
    first = codes_ref.shape[1] - 8
    target = []
    for g in range(n_rows):
        rows = codes_ref[g, first:].astype(F32)
        target.append(jnp.concatenate([rows[i : i + 1] for i in range(cols // LANES)], axis=1))
    target = jnp.concatenate(target, axis=0)
    errors = total - target
    err_b = errors.astype(BF16)
    high = err_b.astype(F32)
    pair_ref[0] = high
    pair_ref[1] = errors - high
    for c in range(n_chips):
        err_ref[c] = err_b


def backward(n_lat, err_ref, codes_ref, weights_ref, pair_ref, out_ref, *scratch):
    n_group, _, tokens = codes_ref.shape
    layers, _, _, lat_dev, _ = weights_ref.shape
    n_chips, n_rows, cols = err_ref.shape
    n_near = n_group // layers
    near_lat = n_near * lat_dev
    parts = cols // LANES
    rows, mixed = scratch[:parts], scratch[parts:]
    for i, row in enumerate(rows):
        piece = err_ref[:, :, i * LANES : (i + 1) * LANES].astype(F32)
        row[...] = piece.reshape(n_chips * n_rows, LANES)
    err = []
    for t in range(layers):
        pieces = []
        for first, chip, n in row_blocks(tokens, n_chips, n_near, n_lat):
            start = chip * n_rows + t * n_near + n
            piece = [row[pl.ds(start, n_lat, stride=n_rows), :] for row in rows]
            pieces.append(jnp.concatenate(piece, axis=1))
        err.append(jnp.concatenate(pieces, axis=0).astype(BF16))
    dec_rows = layers * lat_dev
    grad_rows = lat_dev * LANES // cols
    for s in range(layers):
        mine = slice(s * n_near, (s + 1) * n_near)
        codes = codes_ref[mine, :lat_dev].reshape(near_lat, tokens)
        total = jnp.zeros((near_lat, tokens), F32)
        for t in range(layers):
            if t < s:
                row = jnp.zeros((near_lat, cols), F32)
            else:
                row = dot(codes, err[t], 1, 0)
                near = weights_ref[s, t]
                total = total + dot(near.reshape(near_lat, cols), err[t], 1, 1)
            for i, part in enumerate(mixed):
                piece = row[:, i * LANES : (i + 1) * LANES]
                part[pl.ds(t, near_lat, stride=layers), :] = piece
        for i, part in enumerate(mixed):
            piece = part[...].reshape(n_near, dec_rows, LANES).astype(BF16)
            out_ref[mine, i, 0:dec_rows] = piece
        total = total.reshape(n_near, parts, grad_rows, tokens).astype(BF16)
        out_ref[mine, :, dec_rows : dec_rows + grad_rows] = total
    for g in range(n_group):
        for i in range(parts):
            lanes = slice(i * LANES, (i + 1) * LANES)
            high = jnp.broadcast_to(pair_ref[0, g : g + 1, lanes], (8, LANES))
            low = jnp.broadcast_to(pair_ref[1, g : g + 1, lanes], (8, LANES))
            first = lax.broadcasted_iota(jnp.int32, (8, LANES), 0) == 0
            out_ref[g, i, dec_rows + grad_rows :] = jnp.where(first, high, low).astype(BF16)


def finish(
    layers, arrived_ref, tiles_ref, features_ref, active_ref, enc_ref, errors_ref, dec_ref, sem
):
    n_group, parts, n_rows, _ = arrived_ref.shape
    lat_dev, tokens = active_ref.shape
    grad_rows = lat_dev // parts
    dec_rows = n_rows - grad_rows - 8
    n_near = n_group // layers

    def column(g, i):
        return ((g % n_near * layers + g // n_near) * parts + i) * LANES

    copies = []
    for g in range(n_group):
        for i in range(parts):
            copy = pltpu.make_async_copy(
                tiles_ref.at[g, i, 0:lat_dev],
                dec_ref.at[:, :, pl.ds(column(g, i), LANES)],
                sem.at[g * parts + i],
            )
            copy.start()
            copies.append(copy)
    halves = []
    for i in range(parts):
        total = arrived_ref[0, i, dec_rows : dec_rows + grad_rows].astype(F32)
        for g in range(1, n_group):
            total = total + arrived_ref[g, i, dec_rows : dec_rows + grad_rows].astype(F32)
        halves.append(total)
    pre_grad = (jnp.concatenate(halves, axis=0) * active_ref[...]).astype(BF16)
    blocks, _, depth = features_ref.shape
    for j in range(blocks):
        enc_ref[:, j * depth : (j + 1) * depth] = dot(pre_grad, features_ref[j], 1, 0).astype(BF16)
    for g in range(n_group):
        for i in range(parts):
            pair = arrived_ref[g, i, dec_rows + grad_rows :].astype(F32)
            errors_ref[:, column(g, i) : column(g, i) + LANES] = pair[0:1] + pair[1:2]
    for copy in copies:
        copy.wait()


def shift(value, axis, by):
    count = lax.axis_size(axis)
    return lax.ppermute(value, axis, [(i, (i + by) % count) for i in range(count)])


def per_device(inputs, targets, top_index, enc_weight, dec_weight):
    layers, tokens, depth = inputs.shape
    lat_dev = enc_weight.shape[1]
    width = dec_weight.shape[2]
    n_group, n_chips, n_lat = lax.axis_size(GROUP), lax.axis_size(CHIPS), lax.axis_size(LAT)
    n_near = n_group // layers
    cols = width // n_group
    half = width // n_near
    dec_rows = layers * lat_dev
    grad_rows = lat_dev * LANES // cols
    parts = cols // LANES
    x, core = lax.axis_index("x"), lax.axis_index("core")
    lat_first = lax.axis_index(("zp", "zn", "core", "zh", "y")) * lat_dev
    place = jnp.stack([x, lat_first]).astype(jnp.int32)

    n_y = lax.axis_size("y")
    pairs = [[zp * 2 + 0, (1 - zp) * 2 + 1] for zp in range(2)]
    groups = [[i * n_y + y for i in pair for y in range(n_y)] for pair in pairs]
    own = call(own_slice, shape((n_lat, tokens, depth)), place, inputs, scalars=1)
    features = lax.all_to_all(own, NEAR_HALVES, 0, 0, tiled=True, axis_index_groups=groups)

    came = shift(dec_weight, "core", 1)
    kept, came = lax.optimization_barrier((dec_weight, came))
    kept = lax.dynamic_slice_in_dim(kept, core * half, half, 2)
    came = lax.dynamic_slice_in_dim(came, core * half, half, 2)
    mine = jnp.where(core == 0, jnp.stack([kept, came]), jnp.stack([came, kept]))
    mine = mine.reshape(n_near, lat_dev, layers, layers, cols).transpose(3, 2, 0, 1, 4)
    pieces = [lax.dynamic_index_in_dim(mine, x, 0, keepdims=False)]
    for d in range(1, layers):
        piece = lax.dynamic_index_in_dim(mine, (x + d) % layers, 0, keepdims=False)
        pieces.append(shift(piece, "x", d))

    codes, active = call(
        functools.partial(encode, n_near),
        (shape((n_group, lat_dev + 8, tokens)), shape((lat_dev, tokens), F32)),
        place,
        features,
        targets,
        enc_weight.T,
        top_index.transpose(0, 2, 1),
        scalars=1,
    )
    codes = exchange(codes, GROUP)
    weights = call(
        arrange,
        shape((layers, layers, n_near, lat_dev, cols)),
        place,
        active,
        *pieces,
        scalars=1,
    )

    partial = call(
        functools.partial(decode, n_lat),
        shape((n_chips, n_group, cols)),
        codes,
        weights,
        scratch=[pltpu.VMEM((n_chips * n_group, LANES), F32)] * (cols // LANES),
    )
    partial = exchange(partial, CHIPS)
    err_b, pair = call(
        sum_rows,
        (shape((n_chips, n_group, cols)), shape((2, n_group, cols), F32)),
        partial,
        codes,
    )
    err_b = exchange(err_b, CHIPS)
    outgoing = call(
        functools.partial(backward, n_lat),
        shape((n_group, parts, dec_rows + grad_rows + 8, LANES)),
        err_b,
        codes,
        weights,
        pair,
        scratch=[pltpu.VMEM((n_chips * n_group, LANES), F32)] * (cols // LANES)
        + [pltpu.VMEM((n_near * dec_rows, LANES), F32)] * (cols // LANES),
    )
    arrived = exchange(outgoing, GROUP)
    anywhere = pl.BlockSpec(memory_space=pl.ANY)
    vmem = pl.BlockSpec(memory_space=pltpu.VMEM)
    grad_enc, errors, grad_dec = pl.pallas_call(
        functools.partial(finish, layers),
        out_shape=(
            shape((lat_dev, width)),
            shape((1, width), F32),
            shape((lat_dev, layers, width)),
        ),
        in_specs=[vmem, anywhere, vmem, vmem],
        out_specs=(vmem, vmem, anywhere),
        scratch_shapes=[pltpu.SemaphoreType.DMA((n_group * parts,))],
    )(arrived, arrived.reshape(n_group, parts, -1, layers, LANES), features, active)
    return errors, grad_enc.T, grad_dec


def solution(mesh):
    fine = Mesh(mesh.devices.reshape(4, 2, 2, 2, 2, 8), AXES)
    in_specs = (
        P(None, None, LAT),
        P(AXES, None),
        P(),
        P(None, AXES),
        P(AXES, None, None),
    )
    out_specs = (P(AXES, None), P(None, AXES), P(AXES, None, None))
    return jax.shard_map(
        per_device, mesh=fine, in_specs=in_specs, out_specs=out_specs, check_vma=False
    )
```

time: 123 us -> 149 us (1.21)
  Pallas kernels: 5.9 us -> 40.1 us
  local copies, waits for them, and re-layouts: 7.92 us -> 3.26 us
  other arithmetic: 2.69 us -> 0.17 us
  waiting for transfers between devices: 11.3 us -> 9.39 us
    pallas_call x0 -> x1, Pallas kernels: none -> 35.2 us  [per_device(): pl.pallas_call(functools.partial(finish, layers), out_shape=(shape((lat_d...]
    reshape x2 -> x0, local copies, waits for them, and re-layouts: 3.59 us -> none  [the longest x1 2.25 us: per_device(): grad_dec = grad_dec.transpose(2, 3, 1, 0, 4).reshape(lat_dev, layers, width)]
    transpose x1 -> x0, local copies, waits for them, and re-layouts: 2.33 us -> none  [per_device(): grad_dec = grad_dec.transpose(2, 3, 1, 0, 4).reshape(lat_dev, layers, width)]
    concatenate x1 -> x0, other arithmetic: 1.77 us -> none  [per_device(): both = jnp.concatenate([dec_weight, target], axis=0)]
    dynamic_slice x0 -> x1, local copies, waits for them, and re-layouts: none -> 1.51 us  [per_device(): came = lax.dynamic_slice_in_dim(came, core * half, half, 2)]
  transfers between devices with their start and end apart: 6 -> 6, of which waited for: 2 -> 2; matrix products, arithmetic and copies ran while one was open for 1% -> 2% of each run, Pallas kernels for 3% -> 3%
where the time goes in v4:
time: 149 us; the launch traced here: 148 us
  blocking collectives  59.8 us (40%)
  Pallas kernels  40.1 us (27%)
  starting transfers between devices  34.6 us (23%)
  waiting for transfers between devices  9.39 us (6%)
  local copies, waits for them, and re-layouts  3.26 us (2%)
    all_to_all x3, blocking collectives, exchange(): return lax.all_to_all(value, axes, 0, 0, tiled=True)  59.8 us
    pallas_call x1, Pallas kernels, per_device(): pl.pallas_call(functools.partial(finish, layers), out_shape=(shape((lat_d...  35.2 us
    ppermute x4, starting transfers between devices, shift(): lax.ppermute(value, axis, [(i, (i + by) % count) for i in range(count)])  18.3 us
    all_to_all x1, starting transfers between devices, per_device(): lax.all_to_all(own, NEAR_HALVES, 0, 0, tiled=True, axis_index_groups=groups)  10 us
    all_to_all x1, starting transfers between devices, exchange(): return lax.all_to_all(value, axes, 0, 0, tiled=True)  6.32 us
    pallas_call x6, Pallas kernels, call(): pl.pallas_call(body, out_shape=out_shape, in_specs=specs, out_specs=jax.t...  4.89 us
    all_to_all x1, waiting for transfers between devices, exchange(): return lax.all_to_all(value, axes, 0, 0, tiled=True)  4.76 us
    all_to_all x1, waiting for transfers between devices, per_device(): lax.all_to_all(own, NEAR_HALVES, 0, 0, tiled=True, axis_index_groups=groups)  4.62 us
  transfers between devices with their start and end apart: 6, of which 2 were waited for; matrix products, arithmetic and copies ran while one was open for 2% of the time, Pallas kernels for 3%

profile of v4, /device:TPU:1, one launch (start us, length us, event | category | flops | bytes accessed | tf_op | source)
XLA Modules:
  0.0 148.2 jit_solution(8166235625099265935)
XLA Ops:
  0.6 8.8 %collective-permute-start = (bf16[64,4,2048]{2,1,0:T(4,128)(2,1)}, bf16[64,4,2048]{2,1,0:T(4,128)(2,1)}, u32[]{:S(2)}, u32[]{:S(2)}) collective-permute-start(bf16[64,4,2048]{2,1,0:T(4,128)(2,1)} %param.9), channel_id=1, source_target_pairs={{0,16},{16,0},{1,17},{17,1},{2,18},{18,2},{3,19},{19,3},{4,20},{20... | collective-permute-start | bytes 3145736 | tf_op jit(solution)/shard_map/ppermute | solution.py:226
  9.4 0.1 pad_add_fusion.place
  9.5 0.0 copy-start.4
  9.5 0.9 copy-done.4
  10.4 0.0 copy-start.6
  10.4 1.4 shard_map.76
  11.9 10.0 %all-to-all-start = ((bf16[16,128,128]{2,1,0:T(8,128)(2,1)}), bf16[16,128,128]{2,1,0:T(8,128)(2,1)S(1)}, u32[]{:S(2)}, u32[]{:S(2)}) async-start(bf16[16,128,128]{2,1,0:T(8,128)(2,1)} %shard_map.76), calls=%async_computation | async-start | bytes 1048576 | tf_op jit(solution)/shard_map/all_to_all | solution.py:248
  21.9 0.0 collective-permute-done
  22.0 0.0 copy-done.6
  22.0 1.5 %constant_dynamic-slice_fusion = (bf16[64,4,1024]{2,1,0:T(4,128)(2,1)S(1)}, bf16[64,4,1024]{2,1,0:T(4,128)(2,1)S(1)}) fusion(bf16[64,4,2048]{2,1,0:T(4,128)(2,1)} %collective-permute-done, s32[]{:T(128)S(6)} %select_n.42, bf16[64,4,2048]{2,1,0:T(4,128)(2,1)S(1)} %copy-done.6), kind=kLoop, calls=%fused_computation.5 | loop fusion | bytes 2097156 | tf_op jit(solution)/shard_map/dynamic_slice | solution.py:253
  23.5 0.2 reshape.20
  23.7 0.2 copy.11
  23.8 0.2 reshape.19
  24.1 0.2 copy.10
  24.2 0.1 maximum_select_fusion
  24.3 0.0 copy-start.1
  24.3 0.0 copy-start.3
  24.3 0.0 copy-start.5
  24.4 0.1 dynamic-slice_bitcast_fusion
  24.5 4.5 %collective-permute-start.3 = (bf16[4,2,64,256]{3,2,1,0:T(8,128)(2,1)S(1)}, bf16[4,2,64,256]{3,2,1,0:T(8,128)(2,1)S(1)}, u32[]{:S(2)}, u32[]{:S(2)}) collective-permute-start(bf16[4,2,64,256]{3,2,1,0:T(8,128)(2,1)S(1)} %get-tuple-element.21), channel_id=1, source_target_pairs={{0,384},{128,0},{256,128},{384,256},{1,385},{129,1},{257,129},{385... | collective-permute-start | bytes 786440 | tf_op jit(solution)/shard_map/ppermute | solution.py:226
  29.0 2.4 %collective-permute-start.2 = (bf16[4,2,64,256]{3,2,1,0:T(8,128)(2,1)S(1)}, bf16[4,2,64,256]{3,2,1,0:T(8,128)(2,1)S(1)}, u32[]{:S(2)}, u32[]{:S(2)}) collective-permute-start(bf16[4,2,64,256]{3,2,1,0:T(8,128)(2,1)S(1)} %get-tuple-element.22), channel_id=1, source_target_pairs={{0,256},{128,384},{256,0},{384,128},{1,257},{129,385},{257,1},{385... | collective-permute-start | bytes 786440 | tf_op jit(solution)/shard_map/ppermute | solution.py:226
  31.4 2.5 %collective-permute-start.1 = (bf16[4,2,64,256]{3,2,1,0:T(8,128)(2,1)S(1)}, bf16[4,2,64,256]{3,2,1,0:T(8,128)(2,1)S(1)}, u32[]{:S(2)}, u32[]{:S(2)}) collective-permute-start(bf16[4,2,64,256]{3,2,1,0:T(8,128)(2,1)S(1)} %get-tuple-element.23), channel_id=1, source_target_pairs={{0,128},{128,256},{256,384},{384,0},{1,129},{129,257},{257,385},{3... | collective-permute-start | bytes 786440 | tf_op jit(solution)/shard_map/ppermute | solution.py:226
  34.0 4.6 %all-to-all-done.features_ref = bf16[16,128,128]{2,1,0:T(8,128)(2,1)S(1)} async-done(((bf16[16,128,128]{2,1,0:T(8,128)(2,1)}), bf16[16,128,128]{2,1,0:T(8,128)(2,1)S(1)}, u32[]{:S(2)}, u32[]{:S(2)}) %all-to-all-start) | async-done | bytes 524320 | tf_op jit(solution)/shard_map/all_to_all | solution.py:248
  38.6 0.0 copy-start
  38.6 0.0 copy-done.1
  38.6 0.0 copy-done.3
  38.6 0.0 copy-done.5
  38.6 1.7 %shard_map.77 = (bf16[8,72,128]{2,1,0:T(8,128)(2,1)}, f32[64,128]{1,0:T(8,128)S(1)}) custom-call(s32[2]{0:T(128)S(1)} %pad_add_fusion.place, bf16[16,128,128]{2,1,0:T(8,128)(2,1)S(1)} %all-to-all-done.features_ref, bf16[1,2048]{1,0:T(2,128)(2,1)S(1)} %copy-done.5, bf16[64,2048]{1,0:T(8,128)(2,1)S(1)} %bitcast.22, s32[4,64,128]{2,1,0:T(8,128)S(1)} %bitcast.23), custom_call_target="tpu_custom_call" | custom-call | tf_op jit(solution)/shard_map/pallas_call | solution.py:32
  40.3 0.0 copy-start.2
  40.3 6.3 %all-to-all-start.1 = ((bf16[8,72,128]{2,1,0:T(8,128)(2,1)}), bf16[8,72,128]{2,1,0:T(8,128)(2,1)S(1)}, u32[]{:S(2)}, u32[]{:S(2)}) async-start(bf16[8,72,128]{2,1,0:T(8,128)(2,1)} %get-tuple-element.12), calls=%async_computation.1 | async-start | bytes 294912 | tf_op jit(solution)/shard_map/all_to_all | solution.py:22
  46.6 0.0 collective-permute-done.3.p3
  46.6 0.0 collective-permute-done.2.p2
  46.6 0.0 collective-permute-done.1.p1
  46.6 0.6 shard_map.78.weights_ref
  47.3 0.0 copy-done
  47.3 0.0 copy-done.2
  47.3 4.8 %all-to-all-done.1.codes_ref = bf16[8,72,128]{2,1,0:T(8,128)(2,1)S(1)} async-done(((bf16[8,72,128]{2,1,0:T(8,128)(2,1)}), bf16[8,72,128]{2,1,0:T(8,128)(2,1)S(1)}, u32[]{:S(2)}, u32[]{:S(2)}) %all-to-all-start.1) | async-done | bytes 147488 | tf_op jit(solution)/shard_map/all_to_all | solution.py:22
  52.0 0.4 shard_map.79
  52.5 18.2 %all_to_all.25.partial_ref = bf16[64,8,256]{2,1,0:T(8,128)(2,1)S(1)} all-to-all(bf16[64,8,256]{2,1,0:T(8,128)(2,1)S(1)} %shard_map.79), channel_id=1, replica_groups=mesh['x'=4,'zp'=2,'zn'=2,'core'=2,'zh'=2,'y'=8] {'zp','zn','zh','y'}, dimensions={0} | all-to-all | bytes 524288 | tf_op jit(solution)/shard_map/all_to_all | solution.py:22
  70.6 0.1 shard_map.80
  70.7 18.3 %all_to_all.26.err_ref = bf16[64,8,256]{2,1,0:T(8,128)(2,1)S(1)} all-to-all(bf16[64,8,256]{2,1,0:T(8,128)(2,1)S(1)} %get-tuple-element.16), channel_id=1, replica_groups=mesh['x'=4,'zp'=2,'zn'=2,'core'=2,'zh'=2,'y'=8] {'zp','zn','zh','y'}, dimensions={0} | all-to-all | bytes 524288 | tf_op jit(solution)/shard_map/all_to_all | solution.py:22
  89.0 0.6 shard_map.81
  89.6 23.4 %all_to_all.27.arrived_ref = bf16[8,2,296,128]{3,2,1,0:T(8,128)(2,1)} all-to-all(bf16[8,2,296,128]{3,2,1,0:T(8,128)(2,1)S(1)} %shard_map.81), channel_id=1, replica_groups=mesh['x'=4,'zp'=2,'zn'=2,'core'=2,'zh'=2,'y'=8] {'x','core'}, dimensions={0} | all-to-all | bytes 2424832 | tf_op jit(solution)/shard_map/all_to_all | solution.py:22
  113.0 35.2 %shard_map.82 = (bf16[64,2048]{1,0:T(8,128)(2,1)}, f32[1,2048]{1,0:T(1,128)}, bf16[64,4,2048]{2,1,0:T(4,128)(2,1)}) custom-call(bf16[8,2,296,128]{3,2,1,0:T(8,128)(2,1)} %all_to_all.27.arrived_ref, bf16[8,2,74,4,128]{4,3,2,1,0:T(4,128)(2,1)} %bitcast.24, bf16[16,128,128]{2,1,0:T(8,128)(2,1)} %copy-done, f32[64,128]{1,0:T(8,128)} %copy-done.2), custom_call_target="tpu_custom_call" | custom-call | tf_op jit(solution)/shard_map/pallas_call | solution.py:309
Async XLA Ops:
  0.6 21.3 %collective-permute-start = (bf16[64,4,2048]{2,1,0:T(4,128)(2,1)}, bf16[64,4,2048]{2,1,0:T(4,128)(2,1)}, u32[]{:S(2)}, u32[]{:S(2)}) collective-permute-start(bf16[64,4,2048]{2,1,0:T(4,128)(2,1)} %param.9), channel_id=1, source_target_pairs={{0,16},{16,0},{1,17},{17,1},{2,18},{18,2},{3,19},{19,3},{4,20},{20... | collective-permute-start | bytes 3145736 | tf_op jit(solution)/shard_map/ppermute | solution.py:226
  9.5 0.9 copy-start.4
  10.4 11.5 %copy-start.6 = (bf16[64,4,2048]{2,1,0:T(4,128)(2,1)S(1)}, bf16[64,4,2048]{2,1,0:T(4,128)(2,1)}, u32[]{:S(2)}) copy-start(bf16[64,4,2048]{2,1,0:T(4,128)(2,1)} %param.9) | copy-start | bytes 3145732
  11.9 26.7 %all-to-all-start = ((bf16[16,128,128]{2,1,0:T(8,128)(2,1)}), bf16[16,128,128]{2,1,0:T(8,128)(2,1)S(1)}, u32[]{:S(2)}, u32[]{:S(2)}) async-start(bf16[16,128,128]{2,1,0:T(8,128)(2,1)} %shard_map.76), calls=%async_computation | async-start | bytes 1048576 | tf_op jit(solution)/shard_map/all_to_all | solution.py:248
  24.3 14.3 %copy-start.1 = (bf16[2048,64]{0,1:T(8,128)(2,1)S(1)}, bf16[2048,64]{0,1:T(8,128)(2,1)}, u32[]{:S(2)}) copy-start(bf16[2048,64]{0,1:T(8,128)(2,1)} %param.8) | copy-start | bytes 786436
  24.3 14.2 %copy-start.3 = (s32[4,128,64]{1,2,0:T(8,128)S(1)}, s32[4,128,64]{1,2,0:T(8,128)}, u32[]{:S(2)}) copy-start(s32[4,128,64]{1,2,0:T(8,128)} %param.7) | copy-start | bytes 393220
  24.3 14.2 %copy-start.5 = (bf16[1,2048]{1,0:T(2,128)(2,1)S(1)}, bf16[1,2048]{1,0:T(2,128)(2,1)}, u32[]{:S(2)}) copy-start(bf16[1,2048]{1,0:T(2,128)(2,1)} %target_ref.1) | copy-start | bytes 12292
  24.5 22.1 %collective-permute-start.3 = (bf16[4,2,64,256]{3,2,1,0:T(8,128)(2,1)S(1)}, bf16[4,2,64,256]{3,2,1,0:T(8,128)(2,1)S(1)}, u32[]{:S(2)}, u32[]{:S(2)}) collective-permute-start(bf16[4,2,64,256]{3,2,1,0:T(8,128)(2,1)S(1)} %get-tuple-element.21), channel_id=1, source_target_pairs={{0,384},{128,0},{256,128},{384,256},{1,385},{129,1},{257,129},{385... | collective-permute-start | bytes 786440 | tf_op jit(solution)/shard_map/ppermute | solution.py:226
  29.0 17.6 %collective-permute-start.2 = (bf16[4,2,64,256]{3,2,1,0:T(8,128)(2,1)S(1)}, bf16[4,2,64,256]{3,2,1,0:T(8,128)(2,1)S(1)}, u32[]{:S(2)}, u32[]{:S(2)}) collective-permute-start(bf16[4,2,64,256]{3,2,1,0:T(8,128)(2,1)S(1)} %get-tuple-element.22), channel_id=1, source_target_pairs={{0,256},{128,384},{256,0},{384,128},{1,257},{129,385},{257,1},{385... | collective-permute-start | bytes 786440 | tf_op jit(solution)/shard_map/ppermute | solution.py:226
  31.4 15.2 %collective-permute-start.1 = (bf16[4,2,64,256]{3,2,1,0:T(8,128)(2,1)S(1)}, bf16[4,2,64,256]{3,2,1,0:T(8,128)(2,1)S(1)}, u32[]{:S(2)}, u32[]{:S(2)}) collective-permute-start(bf16[4,2,64,256]{3,2,1,0:T(8,128)(2,1)S(1)} %get-tuple-element.23), channel_id=1, source_target_pairs={{0,128},{128,256},{256,384},{384,0},{1,129},{129,257},{257,385},{3... | collective-permute-start | bytes 786440 | tf_op jit(solution)/shard_map/ppermute | solution.py:226
  38.6 8.7 %copy-start = (bf16[16,128,128]{2,1,0:T(8,128)(2,1)}, bf16[16,128,128]{2,1,0:T(8,128)(2,1)S(1)}, u32[]{:S(2)}) copy-start(bf16[16,128,128]{2,1,0:T(8,128)(2,1)S(1)} %all-to-all-done.features_ref) | copy-start | bytes 1572868
  40.3 7.0 %copy-start.2 = (f32[64,128]{1,0:T(8,128)}, f32[64,128]{1,0:T(8,128)S(1)}, u32[]{:S(2)}) copy-start(f32[64,128]{1,0:T(8,128)S(1)} %get-tuple-element.13.after.active_ref) | copy-start | bytes 98308
  40.3 11.7 %all-to-all-start.1 = ((bf16[8,72,128]{2,1,0:T(8,128)(2,1)}), bf16[8,72,128]{2,1,0:T(8,128)(2,1)S(1)}, u32[]{:S(2)}, u32[]{:S(2)}) async-start(bf16[8,72,128]{2,1,0:T(8,128)(2,1)} %get-tuple-element.12), calls=%async_computation.1 | async-start | bytes 294912 | tf_op jit(solution)/shard_map/all_to_all | solution.py:22

commit v5 on v4

--- a/solution.py
+++ b/solution.py
@@ -43,27 +43,32 @@
     return jax.ShapeDtypeStruct(dims, dtype)
 
 
-def own_slice(place, inputs_ref, out_ref):
-    own = inputs_ref[place[0]]
+def own_slice(place, inputs_ref, out_ref, own_ref, sem):
+    copy = pltpu.make_async_copy(inputs_ref.at[place[0]], own_ref, sem)
+    copy.start()
+    copy.wait()
+    own = own_ref[...]
     for j in range(out_ref.shape[0]):
         out_ref[j] = own
 
 
-def encode(
-    n_near, place, features_ref, target_ref, enc_ref, chosen_ref, codes_ref, active_ref
-):
+def find_active(place, chosen_ref, active_ref):
+    ids = place[1] + lax.broadcasted_iota(jnp.int32, active_ref.shape, 0)
+    chosen = chosen_ref[place[0]]
+    active = jnp.zeros(active_ref.shape, F32)
+    for k in range(chosen.shape[0]):
+        active = jnp.where(chosen[k : k + 1] == ids, 1.0, active)
+    active_ref[...] = active
+
+
+def encode(n_near, features_ref, target_ref, enc_ref, active_ref, codes_ref):
     parts, tokens, depth = features_ref.shape
     lat_dev = enc_ref.shape[0]
     total = jnp.zeros((lat_dev, tokens), F32)
-    for j in range(parts):
-        total = total + dot(enc_ref[:, j * depth : (j + 1) * depth], features_ref[j], 1, 1)
-    ids = place[1] + lax.broadcasted_iota(jnp.int32, (lat_dev, tokens), 0)
-    chosen = chosen_ref[place[0]]
-    active = jnp.zeros((lat_dev, tokens), F32)
-    for k in range(chosen.shape[0]):
-        active = jnp.where(chosen[k : k + 1] == ids, 1.0, active)
-    codes = (total * active).astype(BF16)
-    active_ref[...] = active
+    for j in range(0, parts, 2):
+        pair = jnp.concatenate([features_ref[j], features_ref[j + 1]], axis=1)
+        total = total + dot(enc_ref[:, j * depth : (j + 2) * depth], pair, 1, 1)
+    codes = (total * active_ref[...]).astype(BF16)
     n_group = codes_ref.shape[0]
     cols = target_ref.shape[1] // n_group
     for g in range(n_group):
@@ -182,7 +187,7 @@
 
 
 def finish(
-    layers, arrived_ref, tiles_ref, features_ref, active_ref, enc_ref, errors_ref, dec_ref, sem
+    layers, arrived_ref, tiles_ref, features_ref, active_ref, enc_ref, errors_ref, dec_ref
 ):
     n_group, parts, n_rows, _ = arrived_ref.shape
     lat_dev, tokens = active_ref.shape
@@ -193,16 +198,10 @@
     def column(g, i):
         return ((g % n_near * layers + g // n_near) * parts + i) * LANES
 
-    copies = []
     for g in range(n_group):
         for i in range(parts):
-            copy = pltpu.make_async_copy(
-                tiles_ref.at[g, i, 0:lat_dev],
-                dec_ref.at[:, :, pl.ds(column(g, i), LANES)],
-                sem.at[g * parts + i],
-            )
-            copy.start()
-            copies.append(copy)
+            first = column(g, i)
+            dec_ref[:, :, first : first + LANES] = tiles_ref[g, i, 0:lat_dev]
     halves = []
     for i in range(parts):
         total = arrived_ref[0, i, dec_rows : dec_rows + grad_rows].astype(F32)
@@ -217,8 +216,6 @@
         for i in range(parts):
             pair = arrived_ref[g, i, dec_rows + grad_rows :].astype(F32)
             errors_ref[:, column(g, i) : column(g, i) + LANES] = pair[0:1] + pair[1:2]
-    for copy in copies:
-        copy.wait()
 
 
 def shift(value, axis, by):
@@ -244,7 +241,14 @@
     n_y = lax.axis_size("y")
     pairs = [[zp * 2 + 0, (1 - zp) * 2 + 1] for zp in range(2)]
     groups = [[i * n_y + y for i in pair for y in range(n_y)] for pair in pairs]
-    own = call(own_slice, shape((n_lat, tokens, depth)), place, inputs, scalars=1)
+    anywhere = pl.BlockSpec(memory_space=pl.ANY)
+    own = pl.pallas_call(
+        own_slice,
+        out_shape=shape((n_lat, tokens, depth)),
+        in_specs=[pl.BlockSpec(memory_space=pltpu.SMEM), anywhere],
+        out_specs=pl.BlockSpec(memory_space=pltpu.VMEM),
+        scratch_shapes=[pltpu.VMEM((tokens, depth), BF16), pltpu.SemaphoreType.DMA],
+    )(place, inputs)
     features = lax.all_to_all(own, NEAR_HALVES, 0, 0, tiled=True, axis_index_groups=groups)
 
     came = shift(dec_weight, "core", 1)
@@ -253,27 +257,32 @@
     came = lax.dynamic_slice_in_dim(came, core * half, half, 2)
     mine = jnp.where(core == 0, jnp.stack([kept, came]), jnp.stack([came, kept]))
     mine = mine.reshape(n_near, lat_dev, layers, layers, cols).transpose(3, 2, 0, 1, 4)
-    pieces = [lax.dynamic_index_in_dim(mine, x, 0, keepdims=False)]
-    for d in range(1, layers):
-        piece = lax.dynamic_index_in_dim(mine, (x + d) % layers, 0, keepdims=False)
-        pieces.append(shift(piece, "x", d))
-
-    codes, active = call(
+    active = call(
+        find_active,
+        shape((lat_dev, tokens), F32),
+        place,
+        top_index.transpose(0, 2, 1),
+        scalars=1,
+    )
+    codes = call(
         functools.partial(encode, n_near),
-        (shape((n_group, lat_dev + 8, tokens)), shape((lat_dev, tokens), F32)),
-        place,
+        shape((n_group, lat_dev + 8, tokens)),
         features,
         targets,
         enc_weight.T,
-        top_index.transpose(0, 2, 1),
-        scalars=1,
-    )
-    codes = exchange(codes, GROUP)
+        active,
+    )
+    pieces = []
+    for d in range(layers):
+        pieces.append(lax.dynamic_index_in_dim(mine, (x + d) % layers, 0, keepdims=False))
+
+    pieces = [pieces[0]] + [shift(pieces[d], "x", d) for d in range(1, layers)]
+    arrived_codes = exchange(codes, GROUP)
     weights = call(
         arrange,
         shape((layers, layers, n_near, lat_dev, cols)),
         place,
-        active,
+        codes,
         *pieces,
         scalars=1,
     )
@@ -281,7 +290,7 @@
     partial = call(
         functools.partial(decode, n_lat),
         shape((n_chips, n_group, cols)),
-        codes,
+        arrived_codes,
         weights,
         scratch=[pltpu.VMEM((n_chips * n_group, LANES), F32)] * (cols // LANES),
     )
@@ -290,33 +299,28 @@
         sum_rows,
         (shape((n_chips, n_group, cols)), shape((2, n_group, cols), F32)),
         partial,
-        codes,
+        arrived_codes,
     )
     err_b = exchange(err_b, CHIPS)
     outgoing = call(
         functools.partial(backward, n_lat),
         shape((n_group, parts, dec_rows + grad_rows + 8, LANES)),
         err_b,
-        codes,
+        arrived_codes,
         weights,
         pair,
         scratch=[pltpu.VMEM((n_chips * n_group, LANES), F32)] * (cols // LANES)
         + [pltpu.VMEM((n_near * dec_rows, LANES), F32)] * (cols // LANES),
     )
     arrived = exchange(outgoing, GROUP)
-    anywhere = pl.BlockSpec(memory_space=pl.ANY)
-    vmem = pl.BlockSpec(memory_space=pltpu.VMEM)
-    grad_enc, errors, grad_dec = pl.pallas_call(
+    grad_enc, errors, grad_dec = call(
         functools.partial(finish, layers),
-        out_shape=(
-            shape((lat_dev, width)),
-            shape((1, width), F32),
-            shape((lat_dev, layers, width)),
-        ),
-        in_specs=[vmem, anywhere, vmem, vmem],
-        out_specs=(vmem, vmem, anywhere),
-        scratch_shapes=[pltpu.SemaphoreType.DMA((n_group * parts,))],
-    )(arrived, arrived.reshape(n_group, parts, -1, layers, LANES), features, active)
+        (shape((lat_dev, width)), shape((1, width), F32), shape((lat_dev, layers, width))),
+        arrived,
+        arrived.reshape(n_group, parts, -1, layers, LANES),
+        features,
+        active,
+    )
     return errors, grad_enc.T, grad_dec
 
 

time: 149 us -> 115 us (0.77)
  Pallas kernels: 40.1 us -> 7.85 us
    pallas_call x1, Pallas kernels: 35.2 us -> 2.32 us  [per_device(): pl.pallas_call(own_slice, out_shape=shape((n_lat, tokens, depth)), in_spe...]
    pallas_call x6 -> x7, Pallas kernels: 4.89 us -> 5.53 us  [call(): pl.pallas_call(body, out_shape=out_shape, in_specs=specs, out_specs=jax.t...]
  transfers between devices with their start and end apart: 6 -> 6, of which waited for: 2 -> 3; matrix products, arithmetic and copies ran while one was open for 2% -> 3% of each run, Pallas kernels for 3% -> 4%
where the time goes in v5:
time: 115 us; the launch traced here: 114 us
  blocking collectives  59.5 us (52%)
  starting transfers between devices  34.6 us (30%)
  waiting for transfers between devices  8.43 us (7%)
  Pallas kernels  7.85 us (7%)
  local copies, waits for them, and re-layouts  2.35 us (2%)
    all_to_all x3, blocking collectives, exchange(): return lax.all_to_all(value, axes, 0, 0, tiled=True)  59.5 us
    ppermute x4, starting transfers between devices, shift(): lax.ppermute(value, axis, [(i, (i + by) % count) for i in range(count)])  18.2 us
    all_to_all x1, starting transfers between devices, per_device(): lax.all_to_all(own, NEAR_HALVES, 0, 0, tiled=True, axis_index_groups=groups)  10 us
    all_to_all x1, starting transfers between devices, exchange(): return lax.all_to_all(value, axes, 0, 0, tiled=True)  6.32 us
    pallas_call x7, Pallas kernels, call(): pl.pallas_call(body, out_shape=out_shape, in_specs=specs, out_specs=jax.t...  5.53 us
    all_to_all x1, waiting for transfers between devices, exchange(): return lax.all_to_all(value, axes, 0, 0, tiled=True)  4.17 us
    all_to_all x1, waiting for transfers between devices, per_device(): lax.all_to_all(own, NEAR_HALVES, 0, 0, tiled=True, axis_index_groups=groups)  4.01 us
    pallas_call x1, Pallas kernels, per_device(): pl.pallas_call(own_slice, out_shape=shape((n_lat, tokens, depth)), in_spe...  2.32 us
  transfers between devices with their start and end apart: 6, of which 3 were waited for; matrix products, arithmetic and copies ran while one was open for 3% of the time, Pallas kernels for 4%

profile of v5, /device:TPU:1, one launch (start us, length us, event | category | flops | bytes accessed | tf_op | source)
XLA Modules:
  0.0 114.4 jit_solution(12028120883312874594)
XLA Ops:
  0.6 0.0 copy-start.4
  0.6 8.9 %collective-permute-start = (bf16[64,4,2048]{2,1,0:T(4,128)(2,1)}, bf16[64,4,2048]{2,1,0:T(4,128)(2,1)}, u32[]{:S(2)}, u32[]{:S(2)}) collective-permute-start(bf16[64,4,2048]{2,1,0:T(4,128)(2,1)} %param.9), channel_id=1, source_target_pairs={{0,16},{16,0},{1,17},{17,1},{2,18},{18,2},{3,19},{19,3},{4,20},{20... | collective-permute-start | bytes 3145736 | tf_op jit(solution)/shard_map/ppermute | solution.py:223
  9.6 0.6 pad_add_fusion.place
  10.2 2.3 %shard_map.76 = bf16[16,128,128]{2,1,0:T(8,128)(2,1)} custom-call(s32[2]{0:T(128)} %pad_add_fusion.place, bf16[4,128,128]{2,1,0:T(8,128)(2,1)} %inputs_ref.1), custom_call_target="tpu_custom_call" | custom-call | tf_op jit(solution)/shard_map/pallas_call | solution.py:245
  12.5 10.0 %all-to-all-start = ((bf16[16,128,128]{2,1,0:T(8,128)(2,1)}), bf16[16,128,128]{2,1,0:T(8,128)(2,1)S(1)}, u32[]{:S(2)}, u32[]{:S(2)}) async-start(bf16[16,128,128]{2,1,0:T(8,128)(2,1)} %shard_map.76), calls=%async_computation | async-start | bytes 1048576 | tf_op jit(solution)/shard_map/all_to_all | solution.py:252
  22.6 0.0 collective-permute-done
  22.6 0.0 copy-done.4
  22.6 1.5 %constant_dynamic-slice_fusion = (bf16[64,4,1024]{2,1,0:T(4,128)(2,1)S(1)}, bf16[64,4,1024]{2,1,0:T(4,128)(2,1)S(1)}) fusion(bf16[64,4,2048]{2,1,0:T(4,128)(2,1)} %collective-permute-done, s32[]{:T(128)S(6)} %select_n.46, bf16[64,4,2048]{2,1,0:T(4,128)(2,1)S(1)} %copy-done.4), kind=kLoop, calls=%fused_computation.5 | loop fusion | bytes 2097156 | tf_op jit(solution)/shard_map/dynamic_slice | solution.py:257
  24.1 0.2 reshape.20
  24.4 0.2 copy.11
  24.5 0.2 reshape.19
  24.7 0.2 copy.10
  24.9 0.1 maximum_select_fusion
  25.0 0.0 copy-start.1
  25.0 0.0 copy-start.3
  25.0 0.0 copy-start
  25.0 0.0 copy-start.2
  25.0 0.1 dynamic-slice_bitcast_fusion
  25.2 4.4 %collective-permute-start.3 = (bf16[4,2,64,256]{3,2,1,0:T(8,128)(2,1)S(1)}, bf16[4,2,64,256]{3,2,1,0:T(8,128)(2,1)S(1)}, u32[]{:S(2)}, u32[]{:S(2)}) collective-permute-start(bf16[4,2,64,256]{3,2,1,0:T(8,128)(2,1)S(1)} %get-tuple-element.17), channel_id=1, source_target_pairs={{0,384},{128,0},{256,128},{384,256},{1,385},{129,1},{257,129},{385... | collective-permute-start | bytes 786440 | tf_op jit(solution)/shard_map/ppermute | solution.py:223
  29.5 2.4 %collective-permute-start.2 = (bf16[4,2,64,256]{3,2,1,0:T(8,128)(2,1)S(1)}, bf16[4,2,64,256]{3,2,1,0:T(8,128)(2,1)S(1)}, u32[]{:S(2)}, u32[]{:S(2)}) collective-permute-start(bf16[4,2,64,256]{3,2,1,0:T(8,128)(2,1)S(1)} %get-tuple-element.18), channel_id=1, source_target_pairs={{0,256},{128,384},{256,0},{384,128},{1,257},{129,385},{257,1},{385... | collective-permute-start | bytes 786440 | tf_op jit(solution)/shard_map/ppermute | solution.py:223
  32.0 2.5 %collective-permute-start.1 = (bf16[4,2,64,256]{3,2,1,0:T(8,128)(2,1)S(1)}, bf16[4,2,64,256]{3,2,1,0:T(8,128)(2,1)S(1)}, u32[]{:S(2)}, u32[]{:S(2)}) collective-permute-start(bf16[4,2,64,256]{3,2,1,0:T(8,128)(2,1)S(1)} %get-tuple-element.19), channel_id=1, source_target_pairs={{0,128},{128,256},{256,384},{384,0},{1,129},{129,257},{257,385},{3... | collective-permute-start | bytes 786440 | tf_op jit(solution)/shard_map/ppermute | solution.py:223
  34.5 0.0 copy-done.1
  34.5 0.0 copy-done.3
  34.5 0.7 shard_map.77.active_ref
  35.2 4.0 %all-to-all-done.features_ref = bf16[16,128,128]{2,1,0:T(8,128)(2,1)S(1)} async-done(((bf16[16,128,128]{2,1,0:T(8,128)(2,1)}), bf16[16,128,128]{2,1,0:T(8,128)(2,1)S(1)}, u32[]{:S(2)}, u32[]{:S(2)}) %all-to-all-start) | async-done | bytes 524320 | tf_op jit(solution)/shard_map/all_to_all | solution.py:252
  39.2 0.0 copy-done
  39.2 0.0 copy-done.2
  39.2 1.0 shard_map.78.after
  40.2 6.3 %all-to-all-start.1 = ((bf16[8,72,128]{2,1,0:T(8,128)(2,1)}), bf16[8,72,128]{2,1,0:T(8,128)(2,1)S(1)}, u32[]{:S(2)}, u32[]{:S(2)}) async-start(bf16[8,72,128]{2,1,0:T(8,128)(2,1)} %shard_map.78.after), calls=%async_computation.1 | async-start | bytes 294912 | tf_op jit(solution)/shard_map/all_to_all | solution.py:22
  46.5 0.0 collective-permute-done.3.p3
  46.5 0.0 collective-permute-done.2.p2
  46.5 0.2 collective-permute-done.1.p1
  46.8 1.0 shard_map.79.weights_ref
  47.8 4.2 %all-to-all-done.1.codes_ref = bf16[8,72,128]{2,1,0:T(8,128)(2,1)S(1)} async-done(((bf16[8,72,128]{2,1,0:T(8,128)(2,1)}), bf16[8,72,128]{2,1,0:T(8,128)(2,1)S(1)}, u32[]{:S(2)}, u32[]{:S(2)}) %all-to-all-start.1) | async-done | bytes 147488 | tf_op jit(solution)/shard_map/all_to_all | solution.py:22
  52.0 0.4 shard_map.80
  52.4 18.5 %all_to_all.25.partial_ref = bf16[64,8,256]{2,1,0:T(8,128)(2,1)S(1)} all-to-all(bf16[64,8,256]{2,1,0:T(8,128)(2,1)S(1)} %shard_map.80), channel_id=1, replica_groups=mesh['x'=4,'zp'=2,'zn'=2,'core'=2,'zh'=2,'y'=8] {'zp','zn','zh','y'}, dimensions={0} | all-to-all | bytes 524288 | tf_op jit(solution)/shard_map/all_to_all | solution.py:22
  70.9 0.1 shard_map.81
  71.0 18.3 %all_to_all.26.err_ref = bf16[64,8,256]{2,1,0:T(8,128)(2,1)S(1)} all-to-all(bf16[64,8,256]{2,1,0:T(8,128)(2,1)S(1)} %get-tuple-element.12), channel_id=1, replica_groups=mesh['x'=4,'zp'=2,'zn'=2,'core'=2,'zh'=2,'y'=8] {'zp','zn','zh','y'}, dimensions={0} | all-to-all | bytes 524288 | tf_op jit(solution)/shard_map/all_to_all | solution.py:22
  89.3 0.6 shard_map.82
  90.0 22.7 %all_to_all.27.arrived_ref = bf16[8,2,296,128]{3,2,1,0:T(8,128)(2,1)S(1)} all-to-all(bf16[8,2,296,128]{3,2,1,0:T(8,128)(2,1)S(1)} %shard_map.82), channel_id=1, replica_groups=mesh['x'=4,'zp'=2,'zn'=2,'core'=2,'zh'=2,'y'=8] {'x','core'}, dimensions={0} | all-to-all | bytes 2424832 | tf_op jit(solution)/shard_map/all_to_all | solution.py:22
  112.6 1.7 %shard_map.83 = (bf16[64,2048]{1,0:T(8,128)(2,1)}, f32[1,2048]{1,0:T(1,128)}, bf16[64,4,2048]{2,1,0:T(4,128)(2,1)}) custom-call(bf16[8,2,296,128]{3,2,1,0:T(8,128)(2,1)S(1)} %all_to_all.27.arrived_ref, bf16[8,2,74,4,128]{4,3,2,1,0:T(4,128)(2,1)S(1)} %bitcast.22, bf16[16,128,128]{2,1,0:T(8,128)(2,1)S(1)} %all-to-all-done.features_ref, ...), custom_call_target="tpu_custom_call" | custom-call | tf_op jit(solution)/shard_map/pallas_call | solution.py:32
Async XLA Ops:
  0.6 22.0 %copy-start.4 = (bf16[64,4,2048]{2,1,0:T(4,128)(2,1)S(1)}, bf16[64,4,2048]{2,1,0:T(4,128)(2,1)}, u32[]{:S(2)}) copy-start(bf16[64,4,2048]{2,1,0:T(4,128)(2,1)} %param.9) | copy-start | bytes 3145732
  0.6 22.0 %collective-permute-start = (bf16[64,4,2048]{2,1,0:T(4,128)(2,1)}, bf16[64,4,2048]{2,1,0:T(4,128)(2,1)}, u32[]{:S(2)}, u32[]{:S(2)}) collective-permute-start(bf16[64,4,2048]{2,1,0:T(4,128)(2,1)} %param.9), channel_id=1, source_target_pairs={{0,16},{16,0},{1,17},{17,1},{2,18},{18,2},{3,19},{19,3},{4,20},{20... | collective-permute-start | bytes 3145736 | tf_op jit(solution)/shard_map/ppermute | solution.py:223
  12.5 26.7 %all-to-all-start = ((bf16[16,128,128]{2,1,0:T(8,128)(2,1)}), bf16[16,128,128]{2,1,0:T(8,128)(2,1)S(1)}, u32[]{:S(2)}, u32[]{:S(2)}) async-start(bf16[16,128,128]{2,1,0:T(8,128)(2,1)} %shard_map.76), calls=%async_computation | async-start | bytes 1048576 | tf_op jit(solution)/shard_map/all_to_all | solution.py:252
  25.0 9.5 %copy-start.1 = (s32[4,128,64]{1,2,0:T(8,128)S(1)}, s32[4,128,64]{1,2,0:T(8,128)}, u32[]{:S(2)}) copy-start(s32[4,128,64]{1,2,0:T(8,128)} %param.7) | copy-start | bytes 393220
  25.0 9.5 %copy-start.3 = (s32[2]{0:T(128)S(1)}, s32[2]{0:T(128)}, u32[]{:S(2)}) copy-start(s32[2]{0:T(128)} %pad_add_fusion.place) | copy-start | bytes 28
  25.0 14.2 %copy-start = (bf16[2048,64]{0,1:T(8,128)(2,1)S(1)}, bf16[2048,64]{0,1:T(8,128)(2,1)}, u32[]{:S(2)}) copy-start(bf16[2048,64]{0,1:T(8,128)(2,1)} %param.8) | copy-start | bytes 786436
  25.0 14.2 %copy-start.2 = (bf16[1,2048]{1,0:T(2,128)(2,1)S(1)}, bf16[1,2048]{1,0:T(2,128)(2,1)}, u32[]{:S(2)}) copy-start(bf16[1,2048]{1,0:T(2,128)(2,1)} %target_ref.1) | copy-start | bytes 12292
  25.2 21.4 %collective-permute-start.3 = (bf16[4,2,64,256]{3,2,1,0:T(8,128)(2,1)S(1)}, bf16[4,2,64,256]{3,2,1,0:T(8,128)(2,1)S(1)}, u32[]{:S(2)}, u32[]{:S(2)}) collective-permute-start(bf16[4,2,64,256]{3,2,1,0:T(8,128)(2,1)S(1)} %get-tuple-element.17), channel_id=1, source_target_pairs={{0,384},{128,0},{256,128},{384,256},{1,385},{129,1},{257,129},{385... | collective-permute-start | bytes 786440 | tf_op jit(solution)/shard_map/ppermute | solution.py:223
  29.5 17.0 %collective-permute-start.2 = (bf16[4,2,64,256]{3,2,1,0:T(8,128)(2,1)S(1)}, bf16[4,2,64,256]{3,2,1,0:T(8,128)(2,1)S(1)}, u32[]{:S(2)}, u32[]{:S(2)}) collective-permute-start(bf16[4,2,64,256]{3,2,1,0:T(8,128)(2,1)S(1)} %get-tuple-element.18), channel_id=1, source_target_pairs={{0,256},{128,384},{256,0},{384,128},{1,257},{129,385},{257,1},{385... | collective-permute-start | bytes 786440 | tf_op jit(solution)/shard_map/ppermute | solution.py:223
  32.0 14.8 %collective-permute-start.1 = (bf16[4,2,64,256]{3,2,1,0:T(8,128)(2,1)S(1)}, bf16[4,2,64,256]{3,2,1,0:T(8,128)(2,1)S(1)}, u32[]{:S(2)}, u32[]{:S(2)}) collective-permute-start(bf16[4,2,64,256]{3,2,1,0:T(8,128)(2,1)S(1)} %get-tuple-element.19), channel_id=1, source_target_pairs={{0,128},{128,256},{256,384},{384,0},{1,129},{129,257},{257,385},{3... | collective-permute-start | bytes 786440 | tf_op jit(solution)/shard_map/ppermute | solution.py:223
  40.2 11.7 %all-to-all-start.1 = ((bf16[8,72,128]{2,1,0:T(8,128)(2,1)}), bf16[8,72,128]{2,1,0:T(8,128)(2,1)S(1)}, u32[]{:S(2)}, u32[]{:S(2)}) async-start(bf16[8,72,128]{2,1,0:T(8,128)(2,1)} %shard_map.78.after), calls=%async_computation.1 | async-start | bytes 294912 | tf_op jit(solution)/shard_map/all_to_all | solution.py:22

commit v6 on v5

--- a/solution.py
+++ b/solution.py
@@ -41,15 +41,6 @@
 
 def shape(dims, dtype=BF16):
     return jax.ShapeDtypeStruct(dims, dtype)
-
-
-def own_slice(place, inputs_ref, out_ref, own_ref, sem):
-    copy = pltpu.make_async_copy(inputs_ref.at[place[0]], own_ref, sem)
-    copy.start()
-    copy.wait()
-    own = own_ref[...]
-    for j in range(out_ref.shape[0]):
-        out_ref[j] = own
 
 
 def find_active(place, chosen_ref, active_ref):
@@ -86,10 +77,10 @@
             yield (p * n_near + n) * n_lat, p * n_lat, n
 
 
-def arrange(place, after, p0, p1, p2, p3, weights_ref):
+def arrange(order, place, after, p0, p1, p2, p3, weights_ref):
     del after
     layers = weights_ref.shape[0]
-    for d, piece in enumerate((p0, p1, p2, p3)):
+    for d, piece in zip(order, (p0, p1, p2, p3)):
         weights_ref[lax.rem(place[0] + layers - d, layers)] = piece[...]
 
 
@@ -241,14 +232,8 @@
     n_y = lax.axis_size("y")
     pairs = [[zp * 2 + 0, (1 - zp) * 2 + 1] for zp in range(2)]
     groups = [[i * n_y + y for i in pair for y in range(n_y)] for pair in pairs]
-    anywhere = pl.BlockSpec(memory_space=pl.ANY)
-    own = pl.pallas_call(
-        own_slice,
-        out_shape=shape((n_lat, tokens, depth)),
-        in_specs=[pl.BlockSpec(memory_space=pltpu.SMEM), anywhere],
-        out_specs=pl.BlockSpec(memory_space=pltpu.VMEM),
-        scratch_shapes=[pltpu.VMEM((tokens, depth), BF16), pltpu.SemaphoreType.DMA],
-    )(place, inputs)
+    own = lax.dynamic_slice_in_dim(inputs, x, 1, 0)
+    own = jnp.broadcast_to(own, (n_lat, tokens, depth))
     features = lax.all_to_all(own, NEAR_HALVES, 0, 0, tiled=True, axis_index_groups=groups)
 
     came = shift(dec_weight, "core", 1)
@@ -276,14 +261,16 @@
     for d in range(layers):
         pieces.append(lax.dynamic_index_in_dim(mine, (x + d) % layers, 0, keepdims=False))
 
-    pieces = [pieces[0]] + [shift(pieces[d], "x", d) for d in range(1, layers)]
+    order = sorted(range(layers), key=lambda d: min(d, layers - d))
+    for d in order[1:]:
+        pieces[d] = shift(pieces[d], "x", d)
     arrived_codes = exchange(codes, GROUP)
     weights = call(
-        arrange,
+        functools.partial(arrange, order),
         shape((layers, layers, n_near, lat_dev, cols)),
         place,
         codes,
-        *pieces,
+        *[pieces[d] for d in order],
         scalars=1,
     )
 

time: 115 us -> 113 us (0.983)
  Pallas kernels: 7.85 us -> 5.53 us
    pallas_call x1 -> x0, Pallas kernels: 2.32 us -> none  [per_device(): pl.pallas_call(own_slice, out_shape=shape((n_lat, tokens, depth)), in_spe...]
  transfers between devices with their start and end apart: 6 -> 6, of which waited for: 3 -> 2; matrix products, arithmetic and copies ran while one was open for 3% -> 3% of each run, Pallas kernels for 4% -> 2%
where the time goes in v6:
time: 113 us; the launch traced here: 112 us
  blocking collectives  59.1 us (52%)
  starting transfers between devices  35.3 us (31%)
  waiting for transfers between devices  7.61 us (7%)
  Pallas kernels  5.53 us (5%)
  local copies, waits for them, and re-layouts  3.27 us (3%)
    all_to_all x3, blocking collectives, exchange(): return lax.all_to_all(value, axes, 0, 0, tiled=True)  59.1 us
    ppermute x4, starting transfers between devices, shift(): lax.ppermute(value, axis, [(i, (i + by) % count) for i in range(count)])  19 us
    all_to_all x1, starting transfers between devices, per_device(): lax.all_to_all(own, NEAR_HALVES, 0, 0, tiled=True, axis_index_groups=groups)  10 us
    all_to_all x1, starting transfers between devices, exchange(): return lax.all_to_all(value, axes, 0, 0, tiled=True)  6.32 us
    pallas_call x7, Pallas kernels, call(): pl.pallas_call(body, out_shape=out_shape, in_specs=specs, out_specs=jax.t...  5.53 us
    all_to_all x1, waiting for transfers between devices, exchange(): return lax.all_to_all(value, axes, 0, 0, tiled=True)  4.39 us
    all_to_all x1, waiting for transfers between devices, per_device(): lax.all_to_all(own, NEAR_HALVES, 0, 0, tiled=True, axis_index_groups=groups)  3.21 us
  transfers between devices with their start and end apart: 6, of which 2 were waited for; matrix products, arithmetic and copies ran while one was open for 3% of the time, Pallas kernels for 2%

profile of v6, /device:TPU:1, one launch (start us, length us, event | category | flops | bytes accessed | tf_op | source)
XLA Modules:
  0.0 112.0 jit_solution(11562408570258269452)
XLA Ops:
  0.6 0.0 copy-start
  0.6 0.0 copy-start.4
  0.7 8.9 %collective-permute-start = (bf16[64,4,2048]{2,1,0:T(4,128)(2,1)}, bf16[64,4,2048]{2,1,0:T(4,128)(2,1)}, u32[]{:S(2)}, u32[]{:S(2)}) collective-permute-start(bf16[64,4,2048]{2,1,0:T(4,128)(2,1)} %param.9), channel_id=1, source_target_pairs={{0,16},{16,0},{1,17},{17,1},{2,18},{18,2},{3,19},{19,3},{4,20},{20... | collective-permute-start | bytes 3145736 | tf_op jit(solution)/shard_map/ppermute | solution.py:214
  9.6 0.0 copy-done
  9.6 0.9 broadcast_in_dim.8
  10.5 10.0 %all-to-all-start = ((bf16[16,128,128]{2,1,0:T(8,128)(2,1)}), bf16[16,128,128]{2,1,0:T(8,128)(2,1)S(1)}, u32[]{:S(2)}, u32[]{:S(2)}) async-start(bf16[16,128,128]{2,1,0:T(8,128)(2,1)} %broadcast_in_dim.8), calls=%async_computation | async-start | bytes 1048576 | tf_op jit(solution)/shard_map/all_to_all | solution.py:237
  20.6 0.0 collective-permute-done
  20.6 0.0 copy-done.4
  20.6 1.5 %constant_dynamic-slice_fusion = (bf16[64,4,1024]{2,1,0:T(4,128)(2,1)S(1)}, bf16[64,4,1024]{2,1,0:T(4,128)(2,1)S(1)}) fusion(bf16[64,4,2048]{2,1,0:T(4,128)(2,1)} %collective-permute-done, s32[]{:T(128)S(6)} %select_n.50, bf16[64,4,2048]{2,1,0:T(4,128)(2,1)S(1)} %copy-done.4), kind=kLoop, calls=%fused_computation.6 | loop fusion | bytes 2097156 | tf_op jit(solution)/shard_map/dynamic_slice | solution.py:242
  22.1 0.2 reshape.20
  22.3 0.2 copy.11
  22.5 0.2 reshape.19
  22.7 0.2 copy.10
  22.9 0.1 maximum_select_fusion
  23.0 0.0 copy-start.2
  23.0 0.0 copy-start.1
  23.0 0.0 copy-start.3
  23.0 0.1 dynamic-slice_bitcast_fusion
  23.1 4.8 %collective-permute-start.3 = (bf16[4,2,64,256]{3,2,1,0:T(8,128)(2,1)S(1)}, bf16[4,2,64,256]{3,2,1,0:T(8,128)(2,1)S(1)}, u32[]{:S(2)}, u32[]{:S(2)}) collective-permute-start(bf16[4,2,64,256]{3,2,1,0:T(8,128)(2,1)S(1)} %get-tuple-element.17), channel_id=1, source_target_pairs={{0,256},{128,384},{256,0},{384,128},{1,257},{129,385},{257,1},{385... | collective-permute-start | bytes 786440 | tf_op jit(solution)/shard_map/ppermute | solution.py:214
  27.9 2.8 %collective-permute-start.2 = (bf16[4,2,64,256]{3,2,1,0:T(8,128)(2,1)S(1)}, bf16[4,2,64,256]{3,2,1,0:T(8,128)(2,1)S(1)}, u32[]{:S(2)}, u32[]{:S(2)}) collective-permute-start(bf16[4,2,64,256]{3,2,1,0:T(8,128)(2,1)S(1)} %get-tuple-element.18), channel_id=1, source_target_pairs={{0,384},{128,0},{256,128},{384,256},{1,385},{129,1},{257,129},{385... | collective-permute-start | bytes 786440 | tf_op jit(solution)/shard_map/ppermute | solution.py:214
  30.7 2.5 %collective-permute-start.1 = (bf16[4,2,64,256]{3,2,1,0:T(8,128)(2,1)S(1)}, bf16[4,2,64,256]{3,2,1,0:T(8,128)(2,1)S(1)}, u32[]{:S(2)}, u32[]{:S(2)}) collective-permute-start(bf16[4,2,64,256]{3,2,1,0:T(8,128)(2,1)S(1)} %get-tuple-element.19), channel_id=1, source_target_pairs={{0,128},{128,256},{256,384},{384,0},{1,129},{129,257},{257,385},{3... | collective-permute-start | bytes 786440 | tf_op jit(solution)/shard_map/ppermute | solution.py:214
  33.2 0.1 pad_add_fusion.place
  33.3 0.0 copy-done.2
  33.3 0.7 shard_map.76.active_ref
  34.0 3.2 %all-to-all-done.features_ref = bf16[16,128,128]{2,1,0:T(8,128)(2,1)S(1)} async-done(((bf16[16,128,128]{2,1,0:T(8,128)(2,1)}), bf16[16,128,128]{2,1,0:T(8,128)(2,1)S(1)}, u32[]{:S(2)}, u32[]{:S(2)}) %all-to-all-start) | async-done | bytes 524320 | tf_op jit(solution)/shard_map/all_to_all | solution.py:237
  37.2 0.0 copy-done.1
  37.2 0.0 copy-done.3
  37.2 1.0 shard_map.77.after
  38.2 6.3 %all-to-all-start.1 = ((bf16[8,72,128]{2,1,0:T(8,128)(2,1)}), bf16[8,72,128]{2,1,0:T(8,128)(2,1)S(1)}, u32[]{:S(2)}, u32[]{:S(2)}) async-start(bf16[8,72,128]{2,1,0:T(8,128)(2,1)} %shard_map.77.after), calls=%async_computation.1 | async-start | bytes 294912 | tf_op jit(solution)/shard_map/all_to_all | solution.py:22
  44.5 0.0 collective-permute-done.3.p3
  44.5 0.0 collective-permute-done.2.p2
  44.5 0.0 collective-permute-done.1.p1
  44.5 1.0 shard_map.78.weights_ref
  45.5 4.4 %all-to-all-done.1.codes_ref = bf16[8,72,128]{2,1,0:T(8,128)(2,1)S(1)} async-done(((bf16[8,72,128]{2,1,0:T(8,128)(2,1)}), bf16[8,72,128]{2,1,0:T(8,128)(2,1)S(1)}, u32[]{:S(2)}, u32[]{:S(2)}) %all-to-all-start.1) | async-done | bytes 147488 | tf_op jit(solution)/shard_map/all_to_all | solution.py:22
  49.9 0.4 shard_map.79
  50.3 18.2 %all_to_all.25.partial_ref = bf16[64,8,256]{2,1,0:T(8,128)(2,1)S(1)} all-to-all(bf16[64,8,256]{2,1,0:T(8,128)(2,1)S(1)} %shard_map.79), channel_id=1, replica_groups=mesh['x'=4,'zp'=2,'zn'=2,'core'=2,'zh'=2,'y'=8] {'zp','zn','zh','y'}, dimensions={0} | all-to-all | bytes 524288 | tf_op jit(solution)/shard_map/all_to_all | solution.py:22
  68.5 0.1 shard_map.80
  68.6 18.3 %all_to_all.26.err_ref = bf16[64,8,256]{2,1,0:T(8,128)(2,1)S(1)} all-to-all(bf16[64,8,256]{2,1,0:T(8,128)(2,1)S(1)} %get-tuple-element.12), channel_id=1, replica_groups=mesh['x'=4,'zp'=2,'zn'=2,'core'=2,'zh'=2,'y'=8] {'zp','zn','zh','y'}, dimensions={0} | all-to-all | bytes 524288 | tf_op jit(solution)/shard_map/all_to_all | solution.py:22
  86.9 0.6 shard_map.81
  87.5 22.7 %all_to_all.27.arrived_ref = bf16[8,2,296,128]{3,2,1,0:T(8,128)(2,1)S(1)} all-to-all(bf16[8,2,296,128]{3,2,1,0:T(8,128)(2,1)S(1)} %shard_map.81), channel_id=1, replica_groups=mesh['x'=4,'zp'=2,'zn'=2,'core'=2,'zh'=2,'y'=8] {'x','core'}, dimensions={0} | all-to-all | bytes 2424832 | tf_op jit(solution)/shard_map/all_to_all | solution.py:22
  110.2 1.7 %shard_map.82 = (bf16[64,2048]{1,0:T(8,128)(2,1)}, f32[1,2048]{1,0:T(1,128)}, bf16[64,4,2048]{2,1,0:T(4,128)(2,1)}) custom-call(bf16[8,2,296,128]{3,2,1,0:T(8,128)(2,1)S(1)} %all_to_all.27.arrived_ref, bf16[8,2,74,4,128]{4,3,2,1,0:T(4,128)(2,1)S(1)} %bitcast.24, bf16[16,128,128]{2,1,0:T(8,128)(2,1)S(1)} %all-to-all-done.features_ref, ...), custom_call_target="tpu_custom_call" | custom-call | tf_op jit(solution)/shard_map/pallas_call | solution.py:32
  (1 shorter events, 0.0 us)
Async XLA Ops:
  0.6 9.0 %copy-start = (bf16[4,128,128]{2,1,0:T(8,128)(2,1)S(1)}, bf16[4,128,128]{2,1,0:T(8,128)(2,1)}, u32[]{:S(2)}) copy-start(bf16[4,128,128]{2,1,0:T(8,128)(2,1)} %param.5) | copy-start | bytes 393220
  0.6 20.0 %copy-start.4 = (bf16[64,4,2048]{2,1,0:T(4,128)(2,1)S(1)}, bf16[64,4,2048]{2,1,0:T(4,128)(2,1)}, u32[]{:S(2)}) copy-start(bf16[64,4,2048]{2,1,0:T(4,128)(2,1)} %param.9) | copy-start | bytes 3145732
  0.7 20.0 %collective-permute-start = (bf16[64,4,2048]{2,1,0:T(4,128)(2,1)}, bf16[64,4,2048]{2,1,0:T(4,128)(2,1)}, u32[]{:S(2)}, u32[]{:S(2)}) collective-permute-start(bf16[64,4,2048]{2,1,0:T(4,128)(2,1)} %param.9), channel_id=1, source_target_pairs={{0,16},{16,0},{1,17},{17,1},{2,18},{18,2},{3,19},{19,3},{4,20},{20... | collective-permute-start | bytes 3145736 | tf_op jit(solution)/shard_map/ppermute | solution.py:214
  10.5 26.7 %all-to-all-start = ((bf16[16,128,128]{2,1,0:T(8,128)(2,1)}), bf16[16,128,128]{2,1,0:T(8,128)(2,1)S(1)}, u32[]{:S(2)}, u32[]{:S(2)}) async-start(bf16[16,128,128]{2,1,0:T(8,128)(2,1)} %broadcast_in_dim.8), calls=%async_computation | async-start | bytes 1048576 | tf_op jit(solution)/shard_map/all_to_all | solution.py:237
  23.0 10.3 %copy-start.2 = (s32[4,128,64]{1,2,0:T(8,128)S(1)}, s32[4,128,64]{1,2,0:T(8,128)}, u32[]{:S(2)}) copy-start(s32[4,128,64]{1,2,0:T(8,128)} %param.7) | copy-start | bytes 393220
  23.0 14.2 %copy-start.1 = (bf16[2048,64]{0,1:T(8,128)(2,1)S(1)}, bf16[2048,64]{0,1:T(8,128)(2,1)}, u32[]{:S(2)}) copy-start(bf16[2048,64]{0,1:T(8,128)(2,1)} %param.8) | copy-start | bytes 786436
  23.0 14.2 %copy-start.3 = (bf16[1,2048]{1,0:T(2,128)(2,1)S(1)}, bf16[1,2048]{1,0:T(2,128)(2,1)}, u32[]{:S(2)}) copy-start(bf16[1,2048]{1,0:T(2,128)(2,1)} %target_ref.1) | copy-start | bytes 12292
  23.1 21.4 %collective-permute-start.3 = (bf16[4,2,64,256]{3,2,1,0:T(8,128)(2,1)S(1)}, bf16[4,2,64,256]{3,2,1,0:T(8,128)(2,1)S(1)}, u32[]{:S(2)}, u32[]{:S(2)}) collective-permute-start(bf16[4,2,64,256]{3,2,1,0:T(8,128)(2,1)S(1)} %get-tuple-element.17), channel_id=1, source_target_pairs={{0,256},{128,384},{256,0},{384,128},{1,257},{129,385},{257,1},{385... | collective-permute-start | bytes 786440 | tf_op jit(solution)/shard_map/ppermute | solution.py:214
  27.9 16.6 %collective-permute-start.2 = (bf16[4,2,64,256]{3,2,1,0:T(8,128)(2,1)S(1)}, bf16[4,2,64,256]{3,2,1,0:T(8,128)(2,1)S(1)}, u32[]{:S(2)}, u32[]{:S(2)}) collective-permute-start(bf16[4,2,64,256]{3,2,1,0:T(8,128)(2,1)S(1)} %get-tuple-element.18), channel_id=1, source_target_pairs={{0,384},{128,0},{256,128},{384,256},{1,385},{129,1},{257,129},{385... | collective-permute-start | bytes 786440 | tf_op jit(solution)/shard_map/ppermute | solution.py:214
  30.7 13.8 %collective-permute-start.1 = (bf16[4,2,64,256]{3,2,1,0:T(8,128)(2,1)S(1)}, bf16[4,2,64,256]{3,2,1,0:T(8,128)(2,1)S(1)}, u32[]{:S(2)}, u32[]{:S(2)}) collective-permute-start(bf16[4,2,64,256]{3,2,1,0:T(8,128)(2,1)S(1)} %get-tuple-element.19), channel_id=1, source_target_pairs={{0,128},{128,256},{256,384},{384,0},{1,129},{129,257},{257,385},{3... | collective-permute-start | bytes 786440 | tf_op jit(solution)/shard_map/ppermute | solution.py:214
  38.2 11.7 %all-to-all-start.1 = ((bf16[8,72,128]{2,1,0:T(8,128)(2,1)}), bf16[8,72,128]{2,1,0:T(8,128)(2,1)S(1)}, u32[]{:S(2)}, u32[]{:S(2)}) async-start(bf16[8,72,128]{2,1,0:T(8,128)(2,1)} %shard_map.77.after), calls=%async_computation.1 | async-start | bytes 294912 | tf_op jit(solution)/shard_map/all_to_all | solution.py:22

commit v7 on v6

--- a/solution.py
+++ b/solution.py
@@ -148,7 +148,6 @@
             pieces.append(jnp.concatenate(piece, axis=1))
         err.append(jnp.concatenate(pieces, axis=0).astype(BF16))
     dec_rows = layers * lat_dev
-    grad_rows = lat_dev * LANES // cols
     for s in range(layers):
         mine = slice(s * n_near, (s + 1) * n_near)
         codes = codes_ref[mine, :lat_dev].reshape(near_lat, tokens)
@@ -165,25 +164,27 @@
                 part[pl.ds(t, near_lat, stride=layers), :] = piece
         for i, part in enumerate(mixed):
             piece = part[...].reshape(n_near, dec_rows, LANES).astype(BF16)
-            out_ref[mine, i, 0:dec_rows] = piece
-        total = total.reshape(n_near, parts, grad_rows, tokens).astype(BF16)
-        out_ref[mine, :, dec_rows : dec_rows + grad_rows] = total
+            out_ref[mine, i * dec_rows : (i + 1) * dec_rows] = piece
+        total = total.reshape(n_near, lat_dev, tokens).astype(BF16)
+        out_ref[mine, parts * dec_rows : parts * dec_rows + lat_dev] = total
     for g in range(n_group):
-        for i in range(parts):
-            lanes = slice(i * LANES, (i + 1) * LANES)
-            high = jnp.broadcast_to(pair_ref[0, g : g + 1, lanes], (8, LANES))
-            low = jnp.broadcast_to(pair_ref[1, g : g + 1, lanes], (8, LANES))
-            first = lax.broadcasted_iota(jnp.int32, (8, LANES), 0) == 0
-            out_ref[g, i, dec_rows + grad_rows :] = jnp.where(first, high, low).astype(BF16)
+        pair = [
+            pair_ref[k, g : g + 1, i * LANES : (i + 1) * LANES]
+            for k in range(2)
+            for i in range(parts)
+        ]
+        tile = jnp.concatenate(pair + [jnp.zeros((8 - len(pair), LANES), F32)], axis=0)
+        out_ref[g, parts * dec_rows + lat_dev :] = tile.astype(BF16)
 
 
 def finish(
     layers, arrived_ref, tiles_ref, features_ref, active_ref, enc_ref, errors_ref, dec_ref
 ):
-    n_group, parts, n_rows, _ = arrived_ref.shape
-    lat_dev, tokens = active_ref.shape
-    grad_rows = lat_dev // parts
-    dec_rows = n_rows - grad_rows - 8
+    n_group = arrived_ref.shape[0]
+    lat_dev = active_ref.shape[0]
+    parts = errors_ref.shape[1] // (n_group * LANES)
+    first_grad = parts * layers * lat_dev
+    grads = slice(first_grad, first_grad + lat_dev)
     n_near = n_group // layers
 
     def column(g, i):
@@ -192,21 +193,20 @@
     for g in range(n_group):
         for i in range(parts):
             first = column(g, i)
-            dec_ref[:, :, first : first + LANES] = tiles_ref[g, i, 0:lat_dev]
-    halves = []
-    for i in range(parts):
-        total = arrived_ref[0, i, dec_rows : dec_rows + grad_rows].astype(F32)
-        for g in range(1, n_group):
-            total = total + arrived_ref[g, i, dec_rows : dec_rows + grad_rows].astype(F32)
-        halves.append(total)
-    pre_grad = (jnp.concatenate(halves, axis=0) * active_ref[...]).astype(BF16)
+            dec_ref[:, :, first : first + LANES] = tiles_ref[g, i * lat_dev : (i + 1) * lat_dev]
+    total = arrived_ref[0, grads].astype(F32)
+    for g in range(1, n_group):
+        total = total + arrived_ref[g, grads].astype(F32)
+    pre_grad = (total * active_ref[...]).astype(BF16)
     blocks, _, depth = features_ref.shape
-    for j in range(blocks):
-        enc_ref[:, j * depth : (j + 1) * depth] = dot(pre_grad, features_ref[j], 1, 0).astype(BF16)
+    for j in range(0, blocks, 2):
+        pair = jnp.concatenate([features_ref[j], features_ref[j + 1]], axis=1)
+        enc_ref[:, j * depth : (j + 2) * depth] = dot(pre_grad, pair, 1, 0).astype(BF16)
     for g in range(n_group):
+        pair = arrived_ref[g, first_grad + lat_dev :].astype(F32)
         for i in range(parts):
-            pair = arrived_ref[g, i, dec_rows + grad_rows :].astype(F32)
-            errors_ref[:, column(g, i) : column(g, i) + LANES] = pair[0:1] + pair[1:2]
+            row = pair[i : i + 1] + pair[parts + i : parts + i + 1]
+            errors_ref[:, column(g, i) : column(g, i) + LANES] = row
 
 
 def shift(value, axis, by):
@@ -223,7 +223,6 @@
     cols = width // n_group
     half = width // n_near
     dec_rows = layers * lat_dev
-    grad_rows = lat_dev * LANES // cols
     parts = cols // LANES
     x, core = lax.axis_index("x"), lax.axis_index("core")
     lat_first = lax.axis_index(("zp", "zn", "core", "zh", "y")) * lat_dev
@@ -291,7 +290,7 @@
     err_b = exchange(err_b, CHIPS)
     outgoing = call(
         functools.partial(backward, n_lat),
-        shape((n_group, parts, dec_rows + grad_rows + 8, LANES)),
+        shape((n_group, parts * dec_rows + lat_dev + 8, LANES)),
         err_b,
         arrived_codes,
         weights,
@@ -304,7 +303,7 @@
         functools.partial(finish, layers),
         (shape((lat_dev, width)), shape((1, width), F32), shape((lat_dev, layers, width))),
         arrived,
-        arrived.reshape(n_group, parts, -1, layers, LANES),
+        arrived.reshape(n_group, -1, layers, LANES),
         features,
         active,
     )

time: 113 us -> 112 us (level)
  no operation moved by 1% of the time
where the time goes in v7:
time: 112 us
  blocking collectives  59 us (53%)
  starting transfers between devices  35.3 us (32%)
  waiting for transfers between devices  7.61 us (7%)
  Pallas kernels  5.44 us (5%)
  local copies, waits for them, and re-layouts  3.27 us (3%)
    all_to_all x3, blocking collectives, exchange(): return lax.all_to_all(value, axes, 0, 0, tiled=True)  59 us
    ppermute x4, starting transfers between devices, shift(): lax.ppermute(value, axis, [(i, (i + by) % count) for i in range(count)])  19 us
    all_to_all x1, starting transfers between devices, per_device(): lax.all_to_all(own, NEAR_HALVES, 0, 0, tiled=True, axis_index_groups=groups)  10 us
    all_to_all x1, starting transfers between devices, exchange(): return lax.all_to_all(value, axes, 0, 0, tiled=True)  6.32 us
    pallas_call x7, Pallas kernels, call(): pl.pallas_call(body, out_shape=out_shape, in_specs=specs, out_specs=jax.t...  5.44 us
    all_to_all x1, waiting for transfers between devices, exchange(): return lax.all_to_all(value, axes, 0, 0, tiled=True)  4.39 us
    all_to_all x1, waiting for transfers between devices, per_device(): lax.all_to_all(own, NEAR_HALVES, 0, 0, tiled=True, axis_index_groups=groups)  3.21 us
  transfers between devices with their start and end apart: 6, of which 2 were waited for; matrix products, arithmetic and copies ran while one was open for 3% of the time, Pallas kernels for 2%

profile of v7, /device:TPU:1, one launch (start us, length us, event | category | flops | bytes accessed | tf_op | source)
XLA Modules:
  0.0 111.7 jit_solution(6061918084631336993)
XLA Ops:
  0.6 0.0 copy-start
  0.6 0.0 copy-start.4
  0.7 8.9 %collective-permute-start = (bf16[64,4,2048]{2,1,0:T(4,128)(2,1)}, bf16[64,4,2048]{2,1,0:T(4,128)(2,1)}, u32[]{:S(2)}, u32[]{:S(2)}) collective-permute-start(bf16[64,4,2048]{2,1,0:T(4,128)(2,1)} %param.9), channel_id=1, source_target_pairs={{0,16},{16,0},{1,17},{17,1},{2,18},{18,2},{3,19},{19,3},{4,20},{20... | collective-permute-start | bytes 3145736 | tf_op jit(solution)/shard_map/ppermute | solution.py:214
  9.6 0.0 copy-done
  9.6 0.9 broadcast_in_dim.8
  10.5 10.0 %all-to-all-start = ((bf16[16,128,128]{2,1,0:T(8,128)(2,1)}), bf16[16,128,128]{2,1,0:T(8,128)(2,1)S(1)}, u32[]{:S(2)}, u32[]{:S(2)}) async-start(bf16[16,128,128]{2,1,0:T(8,128)(2,1)} %broadcast_in_dim.8), calls=%async_computation | async-start | bytes 1048576 | tf_op jit(solution)/shard_map/all_to_all | solution.py:236
  20.6 0.0 collective-permute-done
  20.6 0.0 copy-done.4
  20.6 1.5 %constant_dynamic-slice_fusion = (bf16[64,4,1024]{2,1,0:T(4,128)(2,1)S(1)}, bf16[64,4,1024]{2,1,0:T(4,128)(2,1)S(1)}) fusion(bf16[64,4,2048]{2,1,0:T(4,128)(2,1)} %collective-permute-done, s32[]{:T(128)S(6)} %select_n.50, bf16[64,4,2048]{2,1,0:T(4,128)(2,1)S(1)} %copy-done.4), kind=kLoop, calls=%fused_computation.6 | loop fusion | bytes 2097156 | tf_op jit(solution)/shard_map/dynamic_slice | solution.py:241
  22.1 0.2 reshape.20
  22.3 0.2 copy.11
  22.5 0.2 reshape.19
  22.7 0.2 copy.10
  22.9 0.1 maximum_select_fusion
  23.0 0.0 copy-start.2
  23.0 0.0 copy-start.1
  23.0 0.0 copy-start.3
  23.0 0.1 dynamic-slice_bitcast_fusion
  23.1 4.8 %collective-permute-start.3 = (bf16[4,2,64,256]{3,2,1,0:T(8,128)(2,1)S(1)}, bf16[4,2,64,256]{3,2,1,0:T(8,128)(2,1)S(1)}, u32[]{:S(2)}, u32[]{:S(2)}) collective-permute-start(bf16[4,2,64,256]{3,2,1,0:T(8,128)(2,1)S(1)} %get-tuple-element.17), channel_id=1, source_target_pairs={{0,256},{128,384},{256,0},{384,128},{1,257},{129,385},{257,1},{385... | collective-permute-start | bytes 786440 | tf_op jit(solution)/shard_map/ppermute | solution.py:214
  27.9 2.8 %collective-permute-start.2 = (bf16[4,2,64,256]{3,2,1,0:T(8,128)(2,1)S(1)}, bf16[4,2,64,256]{3,2,1,0:T(8,128)(2,1)S(1)}, u32[]{:S(2)}, u32[]{:S(2)}) collective-permute-start(bf16[4,2,64,256]{3,2,1,0:T(8,128)(2,1)S(1)} %get-tuple-element.18), channel_id=1, source_target_pairs={{0,384},{128,0},{256,128},{384,256},{1,385},{129,1},{257,129},{385... | collective-permute-start | bytes 786440 | tf_op jit(solution)/shard_map/ppermute | solution.py:214
  30.7 2.5 %collective-permute-start.1 = (bf16[4,2,64,256]{3,2,1,0:T(8,128)(2,1)S(1)}, bf16[4,2,64,256]{3,2,1,0:T(8,128)(2,1)S(1)}, u32[]{:S(2)}, u32[]{:S(2)}) collective-permute-start(bf16[4,2,64,256]{3,2,1,0:T(8,128)(2,1)S(1)} %get-tuple-element.19), channel_id=1, source_target_pairs={{0,128},{128,256},{256,384},{384,0},{1,129},{129,257},{257,385},{3... | collective-permute-start | bytes 786440 | tf_op jit(solution)/shard_map/ppermute | solution.py:214
  33.2 0.1 pad_add_fusion.place
  33.3 0.0 copy-done.2
  33.3 0.7 shard_map.76.active_ref
  34.0 3.2 %all-to-all-done.features_ref = bf16[16,128,128]{2,1,0:T(8,128)(2,1)S(1)} async-done(((bf16[16,128,128]{2,1,0:T(8,128)(2,1)}), bf16[16,128,128]{2,1,0:T(8,128)(2,1)S(1)}, u32[]{:S(2)}, u32[]{:S(2)}) %all-to-all-start) | async-done | bytes 524320 | tf_op jit(solution)/shard_map/all_to_all | solution.py:236
  37.2 0.0 copy-done.1
  37.2 0.0 copy-done.3
  37.2 1.0 shard_map.77.after
  38.2 6.3 %all-to-all-start.1 = ((bf16[8,72,128]{2,1,0:T(8,128)(2,1)}), bf16[8,72,128]{2,1,0:T(8,128)(2,1)S(1)}, u32[]{:S(2)}, u32[]{:S(2)}) async-start(bf16[8,72,128]{2,1,0:T(8,128)(2,1)} %shard_map.77.after), calls=%async_computation.1 | async-start | bytes 294912 | tf_op jit(solution)/shard_map/all_to_all | solution.py:22
  44.5 0.0 collective-permute-done.3.p3
  44.5 0.0 collective-permute-done.2.p2
  44.5 0.0 collective-permute-done.1.p1
  44.5 1.0 shard_map.78.weights_ref
  45.5 4.4 %all-to-all-done.1.codes_ref = bf16[8,72,128]{2,1,0:T(8,128)(2,1)S(1)} async-done(((bf16[8,72,128]{2,1,0:T(8,128)(2,1)}), bf16[8,72,128]{2,1,0:T(8,128)(2,1)S(1)}, u32[]{:S(2)}, u32[]{:S(2)}) %all-to-all-start.1) | async-done | bytes 147488 | tf_op jit(solution)/shard_map/all_to_all | solution.py:22
  49.9 0.4 shard_map.79
  50.3 18.2 %all_to_all.25.partial_ref = bf16[64,8,256]{2,1,0:T(8,128)(2,1)S(1)} all-to-all(bf16[64,8,256]{2,1,0:T(8,128)(2,1)S(1)} %shard_map.79), channel_id=1, replica_groups=mesh['x'=4,'zp'=2,'zn'=2,'core'=2,'zh'=2,'y'=8] {'zp','zn','zh','y'}, dimensions={0} | all-to-all | bytes 524288 | tf_op jit(solution)/shard_map/all_to_all | solution.py:22
  68.5 0.1 shard_map.80
  68.6 18.3 %all_to_all.26.err_ref = bf16[64,8,256]{2,1,0:T(8,128)(2,1)S(1)} all-to-all(bf16[64,8,256]{2,1,0:T(8,128)(2,1)S(1)} %get-tuple-element.12), channel_id=1, replica_groups=mesh['x'=4,'zp'=2,'zn'=2,'core'=2,'zh'=2,'y'=8] {'zp','zn','zh','y'}, dimensions={0} | all-to-all | bytes 524288 | tf_op jit(solution)/shard_map/all_to_all | solution.py:22
  86.9 0.6 shard_map.81
  87.5 22.5 %all_to_all.27.arrived_ref = bf16[8,584,128]{2,1,0:T(8,128)(2,1)S(1)} all-to-all(bf16[8,584,128]{2,1,0:T(8,128)(2,1)S(1)} %shard_map.81), channel_id=1, replica_groups=mesh['x'=4,'zp'=2,'zn'=2,'core'=2,'zh'=2,'y'=8] {'x','core'}, dimensions={0} | all-to-all | bytes 2392064 | tf_op jit(solution)/shard_map/all_to_all | solution.py:22
  110.0 1.7 %shard_map.82 = (bf16[64,2048]{1,0:T(8,128)(2,1)}, f32[1,2048]{1,0:T(1,128)}, bf16[64,4,2048]{2,1,0:T(4,128)(2,1)}) custom-call(bf16[8,584,128]{2,1,0:T(8,128)(2,1)S(1)} %all_to_all.27.arrived_ref, bf16[8,146,4,128]{3,2,1,0:T(4,128)(2,1)S(1)} %bitcast.24, bf16[16,128,128]{2,1,0:T(8,128)(2,1)S(1)} %all-to-all-done.features_ref, ...), custom_call_target="tpu_custom_call" | custom-call | tf_op jit(solution)/shard_map/pallas_call | solution.py:32
  (1 shorter events, 0.0 us)
Async XLA Ops:
  0.6 9.0 %copy-start = (bf16[4,128,128]{2,1,0:T(8,128)(2,1)S(1)}, bf16[4,128,128]{2,1,0:T(8,128)(2,1)}, u32[]{:S(2)}) copy-start(bf16[4,128,128]{2,1,0:T(8,128)(2,1)} %param.5) | copy-start | bytes 393220
  0.6 20.0 %copy-start.4 = (bf16[64,4,2048]{2,1,0:T(4,128)(2,1)S(1)}, bf16[64,4,2048]{2,1,0:T(4,128)(2,1)}, u32[]{:S(2)}) copy-start(bf16[64,4,2048]{2,1,0:T(4,128)(2,1)} %param.9) | copy-start | bytes 3145732
  0.7 20.0 %collective-permute-start = (bf16[64,4,2048]{2,1,0:T(4,128)(2,1)}, bf16[64,4,2048]{2,1,0:T(4,128)(2,1)}, u32[]{:S(2)}, u32[]{:S(2)}) collective-permute-start(bf16[64,4,2048]{2,1,0:T(4,128)(2,1)} %param.9), channel_id=1, source_target_pairs={{0,16},{16,0},{1,17},{17,1},{2,18},{18,2},{3,19},{19,3},{4,20},{20... | collective-permute-start | bytes 3145736 | tf_op jit(solution)/shard_map/ppermute | solution.py:214
  10.5 26.7 %all-to-all-start = ((bf16[16,128,128]{2,1,0:T(8,128)(2,1)}), bf16[16,128,128]{2,1,0:T(8,128)(2,1)S(1)}, u32[]{:S(2)}, u32[]{:S(2)}) async-start(bf16[16,128,128]{2,1,0:T(8,128)(2,1)} %broadcast_in_dim.8), calls=%async_computation | async-start | bytes 1048576 | tf_op jit(solution)/shard_map/all_to_all | solution.py:236
  23.0 10.3 %copy-start.2 = (s32[4,128,64]{1,2,0:T(8,128)S(1)}, s32[4,128,64]{1,2,0:T(8,128)}, u32[]{:S(2)}) copy-start(s32[4,128,64]{1,2,0:T(8,128)} %param.7) | copy-start | bytes 393220
  23.0 14.2 %copy-start.1 = (bf16[2048,64]{0,1:T(8,128)(2,1)S(1)}, bf16[2048,64]{0,1:T(8,128)(2,1)}, u32[]{:S(2)}) copy-start(bf16[2048,64]{0,1:T(8,128)(2,1)} %param.8) | copy-start | bytes 786436
  23.0 14.2 %copy-start.3 = (bf16[1,2048]{1,0:T(2,128)(2,1)S(1)}, bf16[1,2048]{1,0:T(2,128)(2,1)}, u32[]{:S(2)}) copy-start(bf16[1,2048]{1,0:T(2,128)(2,1)} %target_ref.1) | copy-start | bytes 12292
  23.1 21.4 %collective-permute-start.3 = (bf16[4,2,64,256]{3,2,1,0:T(8,128)(2,1)S(1)}, bf16[4,2,64,256]{3,2,1,0:T(8,128)(2,1)S(1)}, u32[]{:S(2)}, u32[]{:S(2)}) collective-permute-start(bf16[4,2,64,256]{3,2,1,0:T(8,128)(2,1)S(1)} %get-tuple-element.17), channel_id=1, source_target_pairs={{0,256},{128,384},{256,0},{384,128},{1,257},{129,385},{257,1},{385... | collective-permute-start | bytes 786440 | tf_op jit(solution)/shard_map/ppermute | solution.py:214
  27.9 16.6 %collective-permute-start.2 = (bf16[4,2,64,256]{3,2,1,0:T(8,128)(2,1)S(1)}, bf16[4,2,64,256]{3,2,1,0:T(8,128)(2,1)S(1)}, u32[]{:S(2)}, u32[]{:S(2)}) collective-permute-start(bf16[4,2,64,256]{3,2,1,0:T(8,128)(2,1)S(1)} %get-tuple-element.18), channel_id=1, source_target_pairs={{0,384},{128,0},{256,128},{384,256},{1,385},{129,1},{257,129},{385... | collective-permute-start | bytes 786440 | tf_op jit(solution)/shard_map/ppermute | solution.py:214
  30.7 13.8 %collective-permute-start.1 = (bf16[4,2,64,256]{3,2,1,0:T(8,128)(2,1)S(1)}, bf16[4,2,64,256]{3,2,1,0:T(8,128)(2,1)S(1)}, u32[]{:S(2)}, u32[]{:S(2)}) collective-permute-start(bf16[4,2,64,256]{3,2,1,0:T(8,128)(2,1)S(1)} %get-tuple-element.19), channel_id=1, source_target_pairs={{0,128},{128,256},{256,384},{384,0},{1,129},{129,257},{257,385},{3... | collective-permute-start | bytes 786440 | tf_op jit(solution)/shard_map/ppermute | solution.py:214
  38.2 11.7 %all-to-all-start.1 = ((bf16[8,72,128]{2,1,0:T(8,128)(2,1)}), bf16[8,72,128]{2,1,0:T(8,128)(2,1)S(1)}, u32[]{:S(2)}, u32[]{:S(2)}) async-start(bf16[8,72,128]{2,1,0:T(8,128)(2,1)} %shard_map.77.after), calls=%async_computation.1 | async-start | bytes 294912 | tf_op jit(solution)/shard_map/all_to_all | solution.py:22

commit v8 on v7

--- a/solution.py
+++ b/solution.py
@@ -56,9 +56,9 @@
     parts, tokens, depth = features_ref.shape
     lat_dev = enc_ref.shape[0]
     total = jnp.zeros((lat_dev, tokens), F32)
-    for j in range(0, parts, 2):
-        pair = jnp.concatenate([features_ref[j], features_ref[j + 1]], axis=1)
-        total = total + dot(enc_ref[:, j * depth : (j + 2) * depth], pair, 1, 1)
+    for j in range(0, parts, 4):
+        some = jnp.concatenate([features_ref[j + i] for i in range(4)], axis=1)
+        total = total + dot(enc_ref[:, j * depth : (j + 4) * depth], some, 1, 1)
     codes = (total * active_ref[...]).astype(BF16)
     n_group = codes_ref.shape[0]
     cols = target_ref.shape[1] // n_group
@@ -199,9 +199,9 @@
         total = total + arrived_ref[g, grads].astype(F32)
     pre_grad = (total * active_ref[...]).astype(BF16)
     blocks, _, depth = features_ref.shape
-    for j in range(0, blocks, 2):
-        pair = jnp.concatenate([features_ref[j], features_ref[j + 1]], axis=1)
-        enc_ref[:, j * depth : (j + 2) * depth] = dot(pre_grad, pair, 1, 0).astype(BF16)
+    for j in range(0, blocks, 4):
+        some = jnp.concatenate([features_ref[j + i] for i in range(4)], axis=1)
+        enc_ref[:, j * depth : (j + 4) * depth] = dot(pre_grad, some, 1, 0).astype(BF16)
     for g in range(n_group):
         pair = arrived_ref[g, first_grad + lat_dev :].astype(F32)
         for i in range(parts):

time: 112 us -> 112 us (level)
  no operation moved by 1% of the time
where the time goes in v8:
time: 112 us
  blocking collectives  59 us (53%)
  starting transfers between devices  35.3 us (32%)
  waiting for transfers between devices  7.61 us (7%)
  Pallas kernels  5.44 us (5%)
  local copies, waits for them, and re-layouts  3.27 us (3%)
    all_to_all x3, blocking collectives, exchange(): return lax.all_to_all(value, axes, 0, 0, tiled=True)  59 us
    ppermute x4, starting transfers between devices, shift(): lax.ppermute(value, axis, [(i, (i + by) % count) for i in range(count)])  19 us
    all_to_all x1, starting transfers between devices, per_device(): lax.all_to_all(own, NEAR_HALVES, 0, 0, tiled=True, axis_index_groups=groups)  10 us
    all_to_all x1, starting transfers between devices, exchange(): return lax.all_to_all(value, axes, 0, 0, tiled=True)  6.32 us
    pallas_call x7, Pallas kernels, call(): pl.pallas_call(body, out_shape=out_shape, in_specs=specs, out_specs=jax.t...  5.44 us
    all_to_all x1, waiting for transfers between devices, exchange(): return lax.all_to_all(value, axes, 0, 0, tiled=True)  4.39 us
    all_to_all x1, waiting for transfers between devices, per_device(): lax.all_to_all(own, NEAR_HALVES, 0, 0, tiled=True, axis_index_groups=groups)  3.21 us
  transfers between devices with their start and end apart: 6, of which 2 were waited for; matrix products, arithmetic and copies ran while one was open for 3% of the time, Pallas kernels for 2%

profile of v8, /device:TPU:1, one launch (start us, length us, event | category | flops | bytes accessed | tf_op | source)
XLA Modules:
  0.0 111.7 jit_solution(12123414080269570339)
XLA Ops:
  0.6 0.0 copy-start
  0.6 0.0 copy-start.4
  0.7 8.9 %collective-permute-start = (bf16[64,4,2048]{2,1,0:T(4,128)(2,1)}, bf16[64,4,2048]{2,1,0:T(4,128)(2,1)}, u32[]{:S(2)}, u32[]{:S(2)}) collective-permute-start(bf16[64,4,2048]{2,1,0:T(4,128)(2,1)} %param.9), channel_id=1, source_target_pairs={{0,16},{16,0},{1,17},{17,1},{2,18},{18,2},{3,19},{19,3},{4,20},{20... | collective-permute-start | bytes 3145736 | tf_op jit(solution)/shard_map/ppermute | solution.py:214
  9.6 0.0 copy-done
  9.6 0.9 broadcast_in_dim.8
  10.5 10.0 %all-to-all-start = ((bf16[16,128,128]{2,1,0:T(8,128)(2,1)}), bf16[16,128,128]{2,1,0:T(8,128)(2,1)S(1)}, u32[]{:S(2)}, u32[]{:S(2)}) async-start(bf16[16,128,128]{2,1,0:T(8,128)(2,1)} %broadcast_in_dim.8), calls=%async_computation | async-start | bytes 1048576 | tf_op jit(solution)/shard_map/all_to_all | solution.py:236
  20.6 0.0 collective-permute-done
  20.6 0.0 copy-done.4
  20.6 1.5 %constant_dynamic-slice_fusion = (bf16[64,4,1024]{2,1,0:T(4,128)(2,1)S(1)}, bf16[64,4,1024]{2,1,0:T(4,128)(2,1)S(1)}) fusion(bf16[64,4,2048]{2,1,0:T(4,128)(2,1)} %collective-permute-done, s32[]{:T(128)S(6)} %select_n.50, bf16[64,4,2048]{2,1,0:T(4,128)(2,1)S(1)} %copy-done.4), kind=kLoop, calls=%fused_computation.6 | loop fusion | bytes 2097156 | tf_op jit(solution)/shard_map/dynamic_slice | solution.py:241
  22.1 0.2 reshape.20
  22.3 0.2 copy.11
  22.5 0.2 reshape.19
  22.7 0.2 copy.10
  22.9 0.1 maximum_select_fusion
  23.0 0.0 copy-start.2
  23.0 0.0 copy-start.1
  23.0 0.0 copy-start.3
  23.0 0.1 dynamic-slice_bitcast_fusion
  23.1 4.8 %collective-permute-start.3 = (bf16[4,2,64,256]{3,2,1,0:T(8,128)(2,1)S(1)}, bf16[4,2,64,256]{3,2,1,0:T(8,128)(2,1)S(1)}, u32[]{:S(2)}, u32[]{:S(2)}) collective-permute-start(bf16[4,2,64,256]{3,2,1,0:T(8,128)(2,1)S(1)} %get-tuple-element.17), channel_id=1, source_target_pairs={{0,256},{128,384},{256,0},{384,128},{1,257},{129,385},{257,1},{385... | collective-permute-start | bytes 786440 | tf_op jit(solution)/shard_map/ppermute | solution.py:214
  27.9 2.8 %collective-permute-start.2 = (bf16[4,2,64,256]{3,2,1,0:T(8,128)(2,1)S(1)}, bf16[4,2,64,256]{3,2,1,0:T(8,128)(2,1)S(1)}, u32[]{:S(2)}, u32[]{:S(2)}) collective-permute-start(bf16[4,2,64,256]{3,2,1,0:T(8,128)(2,1)S(1)} %get-tuple-element.18), channel_id=1, source_target_pairs={{0,384},{128,0},{256,128},{384,256},{1,385},{129,1},{257,129},{385... | collective-permute-start | bytes 786440 | tf_op jit(solution)/shard_map/ppermute | solution.py:214
  30.7 2.5 %collective-permute-start.1 = (bf16[4,2,64,256]{3,2,1,0:T(8,128)(2,1)S(1)}, bf16[4,2,64,256]{3,2,1,0:T(8,128)(2,1)S(1)}, u32[]{:S(2)}, u32[]{:S(2)}) collective-permute-start(bf16[4,2,64,256]{3,2,1,0:T(8,128)(2,1)S(1)} %get-tuple-element.19), channel_id=1, source_target_pairs={{0,128},{128,256},{256,384},{384,0},{1,129},{129,257},{257,385},{3... | collective-permute-start | bytes 786440 | tf_op jit(solution)/shard_map/ppermute | solution.py:214
  33.2 0.1 pad_add_fusion.place
  33.3 0.0 copy-done.2
  33.3 0.7 shard_map.76.active_ref
  34.0 3.2 %all-to-all-done.features_ref = bf16[16,128,128]{2,1,0:T(8,128)(2,1)S(1)} async-done(((bf16[16,128,128]{2,1,0:T(8,128)(2,1)}), bf16[16,128,128]{2,1,0:T(8,128)(2,1)S(1)}, u32[]{:S(2)}, u32[]{:S(2)}) %all-to-all-start) | async-done | bytes 524320 | tf_op jit(solution)/shard_map/all_to_all | solution.py:236
  37.2 0.0 copy-done.1
  37.2 0.0 copy-done.3
  37.2 1.0 shard_map.77.after
  38.2 6.3 %all-to-all-start.1 = ((bf16[8,72,128]{2,1,0:T(8,128)(2,1)}), bf16[8,72,128]{2,1,0:T(8,128)(2,1)S(1)}, u32[]{:S(2)}, u32[]{:S(2)}) async-start(bf16[8,72,128]{2,1,0:T(8,128)(2,1)} %shard_map.77.after), calls=%async_computation.1 | async-start | bytes 294912 | tf_op jit(solution)/shard_map/all_to_all | solution.py:22
  44.5 0.0 collective-permute-done.3.p3
  44.5 0.0 collective-permute-done.2.p2
  44.5 0.0 collective-permute-done.1.p1
  44.5 1.0 shard_map.78.weights_ref
  45.5 4.4 %all-to-all-done.1.codes_ref = bf16[8,72,128]{2,1,0:T(8,128)(2,1)S(1)} async-done(((bf16[8,72,128]{2,1,0:T(8,128)(2,1)}), bf16[8,72,128]{2,1,0:T(8,128)(2,1)S(1)}, u32[]{:S(2)}, u32[]{:S(2)}) %all-to-all-start.1) | async-done | bytes 147488 | tf_op jit(solution)/shard_map/all_to_all | solution.py:22
  49.9 0.4 shard_map.79
  50.3 18.2 %all_to_all.25.partial_ref = bf16[64,8,256]{2,1,0:T(8,128)(2,1)S(1)} all-to-all(bf16[64,8,256]{2,1,0:T(8,128)(2,1)S(1)} %shard_map.79), channel_id=1, replica_groups=mesh['x'=4,'zp'=2,'zn'=2,'core'=2,'zh'=2,'y'=8] {'zp','zn','zh','y'}, dimensions={0} | all-to-all | bytes 524288 | tf_op jit(solution)/shard_map/all_to_all | solution.py:22
  68.5 0.1 shard_map.80
  68.6 18.3 %all_to_all.26.err_ref = bf16[64,8,256]{2,1,0:T(8,128)(2,1)S(1)} all-to-all(bf16[64,8,256]{2,1,0:T(8,128)(2,1)S(1)} %get-tuple-element.12), channel_id=1, replica_groups=mesh['x'=4,'zp'=2,'zn'=2,'core'=2,'zh'=2,'y'=8] {'zp','zn','zh','y'}, dimensions={0} | all-to-all | bytes 524288 | tf_op jit(solution)/shard_map/all_to_all | solution.py:22
  86.9 0.6 shard_map.81
  87.5 22.5 %all_to_all.27.arrived_ref = bf16[8,584,128]{2,1,0:T(8,128)(2,1)S(1)} all-to-all(bf16[8,584,128]{2,1,0:T(8,128)(2,1)S(1)} %shard_map.81), channel_id=1, replica_groups=mesh['x'=4,'zp'=2,'zn'=2,'core'=2,'zh'=2,'y'=8] {'x','core'}, dimensions={0} | all-to-all | bytes 2392064 | tf_op jit(solution)/shard_map/all_to_all | solution.py:22
  110.0 1.7 %shard_map.82 = (bf16[64,2048]{1,0:T(8,128)(2,1)}, f32[1,2048]{1,0:T(1,128)}, bf16[64,4,2048]{2,1,0:T(4,128)(2,1)}) custom-call(bf16[8,584,128]{2,1,0:T(8,128)(2,1)S(1)} %all_to_all.27.arrived_ref, bf16[8,146,4,128]{3,2,1,0:T(4,128)(2,1)S(1)} %bitcast.24, bf16[16,128,128]{2,1,0:T(8,128)(2,1)S(1)} %all-to-all-done.features_ref, ...), custom_call_target="tpu_custom_call" | custom-call | tf_op jit(solution)/shard_map/pallas_call | solution.py:32
  (1 shorter events, 0.0 us)
Async XLA Ops:
  0.6 9.0 %copy-start = (bf16[4,128,128]{2,1,0:T(8,128)(2,1)S(1)}, bf16[4,128,128]{2,1,0:T(8,128)(2,1)}, u32[]{:S(2)}) copy-start(bf16[4,128,128]{2,1,0:T(8,128)(2,1)} %param.5) | copy-start | bytes 393220
  0.6 20.0 %copy-start.4 = (bf16[64,4,2048]{2,1,0:T(4,128)(2,1)S(1)}, bf16[64,4,2048]{2,1,0:T(4,128)(2,1)}, u32[]{:S(2)}) copy-start(bf16[64,4,2048]{2,1,0:T(4,128)(2,1)} %param.9) | copy-start | bytes 3145732
  0.7 20.0 %collective-permute-start = (bf16[64,4,2048]{2,1,0:T(4,128)(2,1)}, bf16[64,4,2048]{2,1,0:T(4,128)(2,1)}, u32[]{:S(2)}, u32[]{:S(2)}) collective-permute-start(bf16[64,4,2048]{2,1,0:T(4,128)(2,1)} %param.9), channel_id=1, source_target_pairs={{0,16},{16,0},{1,17},{17,1},{2,18},{18,2},{3,19},{19,3},{4,20},{20... | collective-permute-start | bytes 3145736 | tf_op jit(solution)/shard_map/ppermute | solution.py:214
  10.5 26.7 %all-to-all-start = ((bf16[16,128,128]{2,1,0:T(8,128)(2,1)}), bf16[16,128,128]{2,1,0:T(8,128)(2,1)S(1)}, u32[]{:S(2)}, u32[]{:S(2)}) async-start(bf16[16,128,128]{2,1,0:T(8,128)(2,1)} %broadcast_in_dim.8), calls=%async_computation | async-start | bytes 1048576 | tf_op jit(solution)/shard_map/all_to_all | solution.py:236
  23.0 10.3 %copy-start.2 = (s32[4,128,64]{1,2,0:T(8,128)S(1)}, s32[4,128,64]{1,2,0:T(8,128)}, u32[]{:S(2)}) copy-start(s32[4,128,64]{1,2,0:T(8,128)} %param.7) | copy-start | bytes 393220
  23.0 14.2 %copy-start.1 = (bf16[2048,64]{0,1:T(8,128)(2,1)S(1)}, bf16[2048,64]{0,1:T(8,128)(2,1)}, u32[]{:S(2)}) copy-start(bf16[2048,64]{0,1:T(8,128)(2,1)} %param.8) | copy-start | bytes 786436
  23.0 14.2 %copy-start.3 = (bf16[1,2048]{1,0:T(2,128)(2,1)S(1)}, bf16[1,2048]{1,0:T(2,128)(2,1)}, u32[]{:S(2)}) copy-start(bf16[1,2048]{1,0:T(2,128)(2,1)} %target_ref.1) | copy-start | bytes 12292
  23.1 21.4 %collective-permute-start.3 = (bf16[4,2,64,256]{3,2,1,0:T(8,128)(2,1)S(1)}, bf16[4,2,64,256]{3,2,1,0:T(8,128)(2,1)S(1)}, u32[]{:S(2)}, u32[]{:S(2)}) collective-permute-start(bf16[4,2,64,256]{3,2,1,0:T(8,128)(2,1)S(1)} %get-tuple-element.17), channel_id=1, source_target_pairs={{0,256},{128,384},{256,0},{384,128},{1,257},{129,385},{257,1},{385... | collective-permute-start | bytes 786440 | tf_op jit(solution)/shard_map/ppermute | solution.py:214
  27.9 16.6 %collective-permute-start.2 = (bf16[4,2,64,256]{3,2,1,0:T(8,128)(2,1)S(1)}, bf16[4,2,64,256]{3,2,1,0:T(8,128)(2,1)S(1)}, u32[]{:S(2)}, u32[]{:S(2)}) collective-permute-start(bf16[4,2,64,256]{3,2,1,0:T(8,128)(2,1)S(1)} %get-tuple-element.18), channel_id=1, source_target_pairs={{0,384},{128,0},{256,128},{384,256},{1,385},{129,1},{257,129},{385... | collective-permute-start | bytes 786440 | tf_op jit(solution)/shard_map/ppermute | solution.py:214
  30.7 13.8 %collective-permute-start.1 = (bf16[4,2,64,256]{3,2,1,0:T(8,128)(2,1)S(1)}, bf16[4,2,64,256]{3,2,1,0:T(8,128)(2,1)S(1)}, u32[]{:S(2)}, u32[]{:S(2)}) collective-permute-start(bf16[4,2,64,256]{3,2,1,0:T(8,128)(2,1)S(1)} %get-tuple-element.19), channel_id=1, source_target_pairs={{0,128},{128,256},{256,384},{384,0},{1,129},{129,257},{257,385},{3... | collective-permute-start | bytes 786440 | tf_op jit(solution)/shard_map/ppermute | solution.py:214
  38.2 11.7 %all-to-all-start.1 = ((bf16[8,72,128]{2,1,0:T(8,128)(2,1)}), bf16[8,72,128]{2,1,0:T(8,128)(2,1)S(1)}, u32[]{:S(2)}, u32[]{:S(2)}) async-start(bf16[8,72,128]{2,1,0:T(8,128)(2,1)} %shard_map.77.after), calls=%async_computation.1 | async-start | bytes 294912 | tf_op jit(solution)/shard_map/all_to_all | solution.py:22

commit v9 on v7

--- a/solution.py
+++ b/solution.py
@@ -260,7 +260,7 @@
     for d in range(layers):
         pieces.append(lax.dynamic_index_in_dim(mine, (x + d) % layers, 0, keepdims=False))
 
-    order = sorted(range(layers), key=lambda d: min(d, layers - d))
+    order = [0] + list(range(layers - 1, 0, -1))
     for d in order[1:]:
         pieces[d] = shift(pieces[d], "x", d)
     arrived_codes = exchange(codes, GROUP)

time: 112 us -> 112 us (level)
  no operation moved by 1% of the time
where the time goes in v9:
time: 112 us
  blocking collectives  59 us (53%)
  starting transfers between devices  35.9 us (32%)
  waiting for transfers between devices  7.01 us (6%)
  Pallas kernels  5.44 us (5%)
  local copies, waits for them, and re-layouts  3.27 us (3%)
    all_to_all x3, blocking collectives, exchange(): return lax.all_to_all(value, axes, 0, 0, tiled=True)  59 us
    ppermute x4, starting transfers between devices, shift(): lax.ppermute(value, axis, [(i, (i + by) % count) for i in range(count)])  19.6 us
    all_to_all x1, starting transfers between devices, per_device(): lax.all_to_all(own, NEAR_HALVES, 0, 0, tiled=True, axis_index_groups=groups)  10 us
    all_to_all x1, starting transfers between devices, exchange(): return lax.all_to_all(value, axes, 0, 0, tiled=True)  6.32 us
    pallas_call x7, Pallas kernels, call(): pl.pallas_call(body, out_shape=out_shape, in_specs=specs, out_specs=jax.t...  5.44 us
    all_to_all x1, waiting for transfers between devices, exchange(): return lax.all_to_all(value, axes, 0, 0, tiled=True)  4.39 us
    all_to_all x1, waiting for transfers between devices, per_device(): lax.all_to_all(own, NEAR_HALVES, 0, 0, tiled=True, axis_index_groups=groups)  2.6 us
  transfers between devices with their start and end apart: 6, of which 2 were waited for; matrix products, arithmetic and copies ran while one was open for 3% of the time, Pallas kernels for 2%

profile of v9, /device:TPU:1, one launch (start us, length us, event | category | flops | bytes accessed | tf_op | source)
XLA Modules:
  0.0 111.7 jit_solution(7626744843233500230)
XLA Ops:
  0.6 0.0 copy-start
  0.6 0.0 copy-start.4
  0.7 8.9 %collective-permute-start = (bf16[64,4,2048]{2,1,0:T(4,128)(2,1)}, bf16[64,4,2048]{2,1,0:T(4,128)(2,1)}, u32[]{:S(2)}, u32[]{:S(2)}) collective-permute-start(bf16[64,4,2048]{2,1,0:T(4,128)(2,1)} %param.9), channel_id=1, source_target_pairs={{0,16},{16,0},{1,17},{17,1},{2,18},{18,2},{3,19},{19,3},{4,20},{20... | collective-permute-start | bytes 3145736 | tf_op jit(solution)/shard_map/ppermute | solution.py:214
  9.6 0.0 copy-done
  9.6 0.9 broadcast_in_dim.8
  10.5 10.0 %all-to-all-start = ((bf16[16,128,128]{2,1,0:T(8,128)(2,1)}), bf16[16,128,128]{2,1,0:T(8,128)(2,1)S(1)}, u32[]{:S(2)}, u32[]{:S(2)}) async-start(bf16[16,128,128]{2,1,0:T(8,128)(2,1)} %broadcast_in_dim.8), calls=%async_computation | async-start | bytes 1048576 | tf_op jit(solution)/shard_map/all_to_all | solution.py:236
  20.6 0.0 collective-permute-done
  20.6 0.0 copy-done.4
  20.6 1.5 %constant_dynamic-slice_fusion = (bf16[64,4,1024]{2,1,0:T(4,128)(2,1)S(1)}, bf16[64,4,1024]{2,1,0:T(4,128)(2,1)S(1)}) fusion(bf16[64,4,2048]{2,1,0:T(4,128)(2,1)} %collective-permute-done, s32[]{:T(128)S(6)} %select_n.50, bf16[64,4,2048]{2,1,0:T(4,128)(2,1)S(1)} %copy-done.4), kind=kLoop, calls=%fused_computation.6 | loop fusion | bytes 2097156 | tf_op jit(solution)/shard_map/dynamic_slice | solution.py:241
  22.1 0.2 reshape.20
  22.3 0.2 copy.11
  22.5 0.2 reshape.19
  22.7 0.2 copy.10
  22.9 0.1 maximum_select_fusion
  23.0 0.0 copy-start.2
  23.0 0.0 copy-start.1
  23.0 0.0 copy-start.3
  23.0 0.1 dynamic-slice_bitcast_fusion
  23.1 3.3 %collective-permute-start.3 = (bf16[4,2,64,256]{3,2,1,0:T(8,128)(2,1)S(1)}, bf16[4,2,64,256]{3,2,1,0:T(8,128)(2,1)S(1)}, u32[]{:S(2)}, u32[]{:S(2)}) collective-permute-start(bf16[4,2,64,256]{3,2,1,0:T(8,128)(2,1)S(1)} %get-tuple-element.17), channel_id=1, source_target_pairs={{0,128},{128,256},{256,384},{384,0},{1,129},{129,257},{257,385},{3... | collective-permute-start | bytes 786440 | tf_op jit(solution)/shard_map/ppermute | solution.py:214
  26.4 4.4 %collective-permute-start.2 = (bf16[4,2,64,256]{3,2,1,0:T(8,128)(2,1)S(1)}, bf16[4,2,64,256]{3,2,1,0:T(8,128)(2,1)S(1)}, u32[]{:S(2)}, u32[]{:S(2)}) collective-permute-start(bf16[4,2,64,256]{3,2,1,0:T(8,128)(2,1)S(1)} %get-tuple-element.18), channel_id=1, source_target_pairs={{0,256},{128,384},{256,0},{384,128},{1,257},{129,385},{257,1},{385... | collective-permute-start | bytes 786440 | tf_op jit(solution)/shard_map/ppermute | solution.py:214
  30.8 3.1 %collective-permute-start.1 = (bf16[4,2,64,256]{3,2,1,0:T(8,128)(2,1)S(1)}, bf16[4,2,64,256]{3,2,1,0:T(8,128)(2,1)S(1)}, u32[]{:S(2)}, u32[]{:S(2)}) collective-permute-start(bf16[4,2,64,256]{3,2,1,0:T(8,128)(2,1)S(1)} %get-tuple-element.19), channel_id=1, source_target_pairs={{0,384},{128,0},{256,128},{384,256},{1,385},{129,1},{257,129},{385... | collective-permute-start | bytes 786440 | tf_op jit(solution)/shard_map/ppermute | solution.py:214
  33.8 0.1 pad_add_fusion.place
  33.9 0.0 copy-done.2
  33.9 0.7 shard_map.76.active_ref
  34.6 2.6 %all-to-all-done.features_ref = bf16[16,128,128]{2,1,0:T(8,128)(2,1)S(1)} async-done(((bf16[16,128,128]{2,1,0:T(8,128)(2,1)}), bf16[16,128,128]{2,1,0:T(8,128)(2,1)S(1)}, u32[]{:S(2)}, u32[]{:S(2)}) %all-to-all-start) | async-done | bytes 524320 | tf_op jit(solution)/shard_map/all_to_all | solution.py:236
  37.2 0.0 copy-done.1
  37.2 0.0 copy-done.3
  37.2 1.0 shard_map.77.after
  38.2 6.3 %all-to-all-start.1 = ((bf16[8,72,128]{2,1,0:T(8,128)(2,1)}), bf16[8,72,128]{2,1,0:T(8,128)(2,1)S(1)}, u32[]{:S(2)}, u32[]{:S(2)}) async-start(bf16[8,72,128]{2,1,0:T(8,128)(2,1)} %shard_map.77.after), calls=%async_computation.1 | async-start | bytes 294912 | tf_op jit(solution)/shard_map/all_to_all | solution.py:22
  44.5 0.0 collective-permute-done.3.p3
  44.5 0.0 collective-permute-done.2.p2
  44.5 0.0 collective-permute-done.1.p1
  44.5 1.0 shard_map.78.weights_ref
  45.5 4.4 %all-to-all-done.1.codes_ref = bf16[8,72,128]{2,1,0:T(8,128)(2,1)S(1)} async-done(((bf16[8,72,128]{2,1,0:T(8,128)(2,1)}), bf16[8,72,128]{2,1,0:T(8,128)(2,1)S(1)}, u32[]{:S(2)}, u32[]{:S(2)}) %all-to-all-start.1) | async-done | bytes 147488 | tf_op jit(solution)/shard_map/all_to_all | solution.py:22
  49.9 0.4 shard_map.79
  50.3 18.2 %all_to_all.25.partial_ref = bf16[64,8,256]{2,1,0:T(8,128)(2,1)S(1)} all-to-all(bf16[64,8,256]{2,1,0:T(8,128)(2,1)S(1)} %shard_map.79), channel_id=1, replica_groups=mesh['x'=4,'zp'=2,'zn'=2,'core'=2,'zh'=2,'y'=8] {'zp','zn','zh','y'}, dimensions={0} | all-to-all | bytes 524288 | tf_op jit(solution)/shard_map/all_to_all | solution.py:22
  68.5 0.1 shard_map.80
  68.6 18.3 %all_to_all.26.err_ref = bf16[64,8,256]{2,1,0:T(8,128)(2,1)S(1)} all-to-all(bf16[64,8,256]{2,1,0:T(8,128)(2,1)S(1)} %get-tuple-element.12), channel_id=1, replica_groups=mesh['x'=4,'zp'=2,'zn'=2,'core'=2,'zh'=2,'y'=8] {'zp','zn','zh','y'}, dimensions={0} | all-to-all | bytes 524288 | tf_op jit(solution)/shard_map/all_to_all | solution.py:22
  86.9 0.6 shard_map.81
  87.5 22.5 %all_to_all.27.arrived_ref = bf16[8,584,128]{2,1,0:T(8,128)(2,1)S(1)} all-to-all(bf16[8,584,128]{2,1,0:T(8,128)(2,1)S(1)} %shard_map.81), channel_id=1, replica_groups=mesh['x'=4,'zp'=2,'zn'=2,'core'=2,'zh'=2,'y'=8] {'x','core'}, dimensions={0} | all-to-all | bytes 2392064 | tf_op jit(solution)/shard_map/all_to_all | solution.py:22
  110.0 1.7 %shard_map.82 = (bf16[64,2048]{1,0:T(8,128)(2,1)}, f32[1,2048]{1,0:T(1,128)}, bf16[64,4,2048]{2,1,0:T(4,128)(2,1)}) custom-call(bf16[8,584,128]{2,1,0:T(8,128)(2,1)S(1)} %all_to_all.27.arrived_ref, bf16[8,146,4,128]{3,2,1,0:T(4,128)(2,1)S(1)} %bitcast.24, bf16[16,128,128]{2,1,0:T(8,128)(2,1)S(1)} %all-to-all-done.features_ref, ...), custom_call_target="tpu_custom_call" | custom-call | tf_op jit(solution)/shard_map/pallas_call | solution.py:32
  (1 shorter events, 0.0 us)
Async XLA Ops:
  0.6 9.0 %copy-start = (bf16[4,128,128]{2,1,0:T(8,128)(2,1)S(1)}, bf16[4,128,128]{2,1,0:T(8,128)(2,1)}, u32[]{:S(2)}) copy-start(bf16[4,128,128]{2,1,0:T(8,128)(2,1)} %param.5) | copy-start | bytes 393220
  0.6 20.0 %copy-start.4 = (bf16[64,4,2048]{2,1,0:T(4,128)(2,1)S(1)}, bf16[64,4,2048]{2,1,0:T(4,128)(2,1)}, u32[]{:S(2)}) copy-start(bf16[64,4,2048]{2,1,0:T(4,128)(2,1)} %param.9) | copy-start | bytes 3145732
  0.7 20.0 %collective-permute-start = (bf16[64,4,2048]{2,1,0:T(4,128)(2,1)}, bf16[64,4,2048]{2,1,0:T(4,128)(2,1)}, u32[]{:S(2)}, u32[]{:S(2)}) collective-permute-start(bf16[64,4,2048]{2,1,0:T(4,128)(2,1)} %param.9), channel_id=1, source_target_pairs={{0,16},{16,0},{1,17},{17,1},{2,18},{18,2},{3,19},{19,3},{4,20},{20... | collective-permute-start | bytes 3145736 | tf_op jit(solution)/shard_map/ppermute | solution.py:214
  10.5 26.7 %all-to-all-start = ((bf16[16,128,128]{2,1,0:T(8,128)(2,1)}), bf16[16,128,128]{2,1,0:T(8,128)(2,1)S(1)}, u32[]{:S(2)}, u32[]{:S(2)}) async-start(bf16[16,128,128]{2,1,0:T(8,128)(2,1)} %broadcast_in_dim.8), calls=%async_computation | async-start | bytes 1048576 | tf_op jit(solution)/shard_map/all_to_all | solution.py:236
  23.0 10.9 %copy-start.2 = (s32[4,128,64]{1,2,0:T(8,128)S(1)}, s32[4,128,64]{1,2,0:T(8,128)}, u32[]{:S(2)}) copy-start(s32[4,128,64]{1,2,0:T(8,128)} %param.7) | copy-start | bytes 393220
  23.0 14.2 %copy-start.1 = (bf16[2048,64]{0,1:T(8,128)(2,1)S(1)}, bf16[2048,64]{0,1:T(8,128)(2,1)}, u32[]{:S(2)}) copy-start(bf16[2048,64]{0,1:T(8,128)(2,1)} %param.8) | copy-start | bytes 786436
  23.0 14.2 %copy-start.3 = (bf16[1,2048]{1,0:T(2,128)(2,1)S(1)}, bf16[1,2048]{1,0:T(2,128)(2,1)}, u32[]{:S(2)}) copy-start(bf16[1,2048]{1,0:T(2,128)(2,1)} %target_ref.1) | copy-start | bytes 12292
  23.1 21.4 %collective-permute-start.3 = (bf16[4,2,64,256]{3,2,1,0:T(8,128)(2,1)S(1)}, bf16[4,2,64,256]{3,2,1,0:T(8,128)(2,1)S(1)}, u32[]{:S(2)}, u32[]{:S(2)}) collective-permute-start(bf16[4,2,64,256]{3,2,1,0:T(8,128)(2,1)S(1)} %get-tuple-element.17), channel_id=1, source_target_pairs={{0,128},{128,256},{256,384},{384,0},{1,129},{129,257},{257,385},{3... | collective-permute-start | bytes 786440 | tf_op jit(solution)/shard_map/ppermute | solution.py:214
  26.4 18.1 %collective-permute-start.2 = (bf16[4,2,64,256]{3,2,1,0:T(8,128)(2,1)S(1)}, bf16[4,2,64,256]{3,2,1,0:T(8,128)(2,1)S(1)}, u32[]{:S(2)}, u32[]{:S(2)}) collective-permute-start(bf16[4,2,64,256]{3,2,1,0:T(8,128)(2,1)S(1)} %get-tuple-element.18), channel_id=1, source_target_pairs={{0,256},{128,384},{256,0},{384,128},{1,257},{129,385},{257,1},{385... | collective-permute-start | bytes 786440 | tf_op jit(solution)/shard_map/ppermute | solution.py:214
  30.8 13.8 %collective-permute-start.1 = (bf16[4,2,64,256]{3,2,1,0:T(8,128)(2,1)S(1)}, bf16[4,2,64,256]{3,2,1,0:T(8,128)(2,1)S(1)}, u32[]{:S(2)}, u32[]{:S(2)}) collective-permute-start(bf16[4,2,64,256]{3,2,1,0:T(8,128)(2,1)S(1)} %get-tuple-element.19), channel_id=1, source_target_pairs={{0,384},{128,0},{256,128},{384,256},{1,385},{129,1},{257,129},{385... | collective-permute-start | bytes 786440 | tf_op jit(solution)/shard_map/ppermute | solution.py:214
  38.2 11.7 %all-to-all-start.1 = ((bf16[8,72,128]{2,1,0:T(8,128)(2,1)}), bf16[8,72,128]{2,1,0:T(8,128)(2,1)S(1)}, u32[]{:S(2)}, u32[]{:S(2)}) async-start(bf16[8,72,128]{2,1,0:T(8,128)(2,1)} %shard_map.77.after), calls=%async_computation.1 | async-start | bytes 294912 | tf_op jit(solution)/shard_map/all_to_all | solution.py:22
